TPU v7x, 256 devices: a whole 4x4x8 slice. The times are simulated.
256 devices in a mesh: mem: 16 (over z, core), dom: 16 (over x, y).
Axes of the slice: x: 4, y: 4, z: 8, core: 2. Of those that a mesh axis runs over, the one named last changes fastest.
Arguments:
- prior_sample_set: float32 [256, 32, 64, 128], P('mem', None, 'dom'), may hold values from -6 to 6
- crossing_number_north: float32 [32], replicated, may hold values from -0.7 to 0.7
- crossing_number_east: float32 [32], replicated, may hold values from -0.7 to 0.7
- spreading_number: float32 [32], replicated, may hold values from 0.01 to 0.08
- obs_cell: int32 [16384], P('dom'), may hold values from 0 to 16383
- obs_value: float32 [16384], P('dom'), may hold values from -6 to 6
- obs_var: float32 [16384], P('dom'), may hold values from 0.25 to 4
- tile_list: int32 [16, 32, 256], P('dom', 'mem'), may hold values from 0 to 3071, as said below
- tile_count: int32 [16, 32], P('dom', 'mem'), may hold values from 1 to 256, as said below
Outputs:
- analysis: float32 [256, 32, 64, 128], P('mem', None, 'dom')
Inputs may be any that keep to these rules, and one draw needn't show every extreme that they name: `tile_list`: entries of one tile are distinct; entry p names observation p mod 1024 of the strip before the tile's own, its own, or the one after, periodically, as p // 1024 is 0, 1 or 2. Only the first tile_count entries are used. `tile_count`: some tile uses 256 observations in every draw. `obs_cell`: numbered by level, then row of the strip, then column.
All inputs are finite; a program needn't handle non-finite values.
Results may differ from a plain program's by a relative error of at most 0.0003.
Values sent between devices are 32-bit elements; how exact they have to be, the bound alone decides.
No kernel may reach another device: no remote copies, remote signals or barrier semaphores. Data moves between devices by JAX's collectives and lax.ppermute only.
A program may use at most 64 MiB of HBM per device.

v0:
```python
import jax
import jax.numpy as jnp
from jax import lax
from jax.experimental import pallas as pl
from jax.experimental.pallas import tpu as pltpu
from jax.sharding import PartitionSpec as P

LOC = 8
STEPS = 3
NS_ITERS = 5
INFLATION = 1.1

F32 = jnp.float32
BF16 = jnp.bfloat16
LEVELS = 32
ROWS = 4
COLS = 128
CELL_ROWS = LEVELS * ROWS
OBS_CHUNKS = 8
META = 3 * OBS_CHUNKS
PACK = CELL_ROWS + META
SLOT_ROWS = 4
COLS_HERE = 8
SEND = COLS_HERE + SLOT_ROWS
PER_MEM = 16
STRIPS = 16
HEIGHT = STRIPS * ROWS


def lane_gather(values, lanes):
    return jnp.take_along_axis(values, lanes, axis=1, mode="promise_in_bounds")


def forecast_kernel(where_ref, north_ref, east_ref, mix_ref, in_ref, out_ref, meta_ref, q_ref, t1_ref, t2_ref, hx_ref):
    def load(s, _):
        for r in range(ROWS):
            q_ref[pl.ds(s * CELL_ROWS + r * LEVELS, LEVELS), :] = in_ref[
                pl.ds(s * PACK + r, LEVELS, stride=ROWS), :
            ]
        return 0

    lax.fori_loop(0, STRIPS, load, 0)

    def level_group(g, _):
        sub = lax.broadcasted_iota(jnp.int32, (8, COLS), 0)

        def spread(ref):
            value = jnp.full((8, COLS), ref[g * 8], F32)
            for i in range(1, 8):
                value = jnp.where(sub == i, ref[g * 8 + i], value)
            return value

        north, east, mix = spread(north_ref), spread(east_ref), spread(mix_ref)
        up, down = mix - 0.5 * north, mix + 0.5 * north
        right, left = mix - 0.5 * east, mix + 0.5 * east
        mid = -4.0 * mix

        def stage(src, dst, scale):
            a, b, c, d, e = up * scale, down * scale, right * scale, left * scale, mid * scale

            def at(ref, x):
                return ref.at[pl.ds(pl.multiple_of(x * LEVELS + g * 8, 8), 8), :]

            def row(x, carry):
                prev, cur = carry
                nxt = at(src, lax.rem(x + 1, HEIGHT))[...]
                at(dst, x)[...] = (
                    at(q_ref, x)[...]
                    + (a * nxt + b * prev)
                    + (c * pltpu.roll(cur, COLS - 1, 1) + d * pltpu.roll(cur, 1, 1))
                    + e * cur
                )
                return cur, nxt

            lax.fori_loop(0, HEIGHT, row, (at(src, HEIGHT - 1)[...], at(src, 0)[...]), unroll=8)

        def step(_, c):
            stage(q_ref, t1_ref, 1.0 / 3.0)
            stage(t1_ref, t2_ref, 0.5)
            stage(t2_ref, q_ref, 1.0)
            return c

        lax.fori_loop(0, STEPS, step, 0)
        return 0

    lax.fori_loop(0, LEVELS // 8, level_group, 0)

    for g in range(2):
        lanes, rows = [], []
        for j in range(OBS_CHUNKS):
            cell = in_ref[pl.ds(g * 8 * PACK + CELL_ROWS + j, 8, stride=PACK), :].astype(jnp.int32)
            lanes.append(cell & (COLS - 1))
            line = cell >> 7
            rows.append((line & (ROWS - 1)) * LEVELS + (line >> 2))

        def pick(p, acc):
            src = q_ref[pl.ds(p + g * 8 * CELL_ROWS, 8, stride=CELL_ROWS), :]
            return tuple(
                jnp.where(rows[j] == p, lane_gather(src, lanes[j]), acc[j]) for j in range(OBS_CHUNKS)
            )

        acc = lax.fori_loop(
            0, CELL_ROWS, pick, tuple(jnp.zeros((8, COLS), F32) for _ in range(OBS_CHUNKS)), unroll=4
        )
        for j in range(OBS_CHUNKS):
            hx_ref[pl.ds(g * 64 + j, 8, stride=OBS_CHUNKS), :] = acc[j]

    def store(s, _):
        base = pl.multiple_of(s * CELL_ROWS, 8)
        to = pl.multiple_of(s * PACK, 8)
        out_ref[pl.ds(to, CELL_ROWS), :] = q_ref[pl.ds(base, CELL_ROWS), :].T
        for t in range(3):
            strip = lax.rem(s + STRIPS - 1 + t, STRIPS)
            out_ref[pl.ds(to + CELL_ROWS + 8 * t, 8), :] = hx_ref[pl.ds(pl.multiple_of(strip * 8, 8), 8), :]
        return 0

    lax.fori_loop(0, STRIPS, store, 0)

    meta_ref[...] = jnp.zeros_like(meta_ref)
    for t in range(3):
        strip = lax.rem(where_ref[0] + STRIPS - 1 + t, STRIPS)
        for which in range(3):
            meta_ref[pl.ds(t * 64 + which, 8, stride=8), :] = in_ref[
                pl.ds(pl.multiple_of(strip * PACK + CELL_ROWS + which * 8, 8), 8), :
            ]


def select_kernel(where_ref, list_ref, in_ref, out_ref, d_ref):
    for j in range(META):
        d_ref[pl.ds(j * PER_MEM, PER_MEM), :] = in_ref[pl.ds(CELL_ROWS + j, PER_MEM, stride=PACK), :]

    def peer(kb, _):
        to = pl.multiple_of(kb * SEND * PER_MEM, 8)
        for c in range(COLS_HERE):
            out_ref[pl.ds(to + c * PER_MEM, PER_MEM), :] = in_ref[
                pl.ds(kb * COLS_HERE + c, PER_MEM, stride=PACK), :
            ]
        first = lax.bitwise_xor(where_ref[1], kb) * SLOT_ROWS
        for q in range(SLOT_ROWS):
            slot = jnp.broadcast_to(list_ref[pl.ds(first + q, 1), :], (8, COLS))
            lanes = slot & (COLS - 1)
            chunk = slot >> 7
            low = jnp.zeros((8, COLS), F32)
            high = jnp.zeros((8, COLS), F32)
            for j in range(META):
                here = chunk == j
                low = jnp.where(here, lane_gather(d_ref[pl.ds(j * PER_MEM, 8), :], lanes), low)
                high = jnp.where(here, lane_gather(d_ref[pl.ds(j * PER_MEM + 8, 8), :], lanes), high)
            at = to + (COLS_HERE + q) * PER_MEM
            out_ref[pl.ds(at, 8), :] = low
            out_ref[pl.ds(at + 8, 8), :] = high
        return 0

    lax.fori_loop(0, PER_MEM, peer, 0)


def parts(x):
    high = x.astype(BF16)
    return high, (x - high.astype(F32)).astype(BF16)


def product(a, b, dims=(((1,), (0,)), ((), ()))):
    def dot(x, y):
        return lax.dot_general(x, y, dims, preferred_element_type=F32)

    return dot(a[0], b[0]) + (dot(a[0], b[1]) + dot(a[1], b[0]))


def update_kernel(where_ref, count_ref, list_ref, meta_ref, in_ref, out_ref, it_ref, root_ref):
    members = 256
    row_id = lax.broadcasted_iota(jnp.int32, (members, members), 0)
    col_id = lax.broadcasted_iota(jnp.int32, (members, members), 1)
    diagonal = row_id == col_id
    slot_id = lax.broadcasted_iota(jnp.int32, (1, COLS), 1)

    def plus_identity(x, scale):
        return jnp.where(diagonal, x + scale, x)

    norms, drives = [], []
    for t in range(2):
        values, rhos, anomalies = [], [], []
        for h in range(2):
            slot = list_ref[pl.ds(2 * t + h, 1), :]
            wide = jnp.broadcast_to(slot, (8, COLS))
            lanes = wide & (COLS - 1)
            chunk = wide >> 7
            found = jnp.zeros((8, COLS), F32)
            for j in range(META):
                found = jnp.where(chunk == j, lane_gather(meta_ref[pl.ds(j * 8, 8), :], lanes), found)
            line = found[0:1].astype(jnp.int32)
            strip = where_ref[0] + STRIPS - 1 + (slot >> 10)
            strip = strip & (STRIPS - 1)
            place_x = (strip * ROWS + ((line >> 7) & (ROWS - 1))).astype(F32)
            place_y = (line & (COLS - 1)).astype(F32)
            centre_x = (where_ref[0] * 4).astype(F32) + 1.5
            centre_y = ((where_ref[1] * 2 + t) * 4).astype(F32) + 1.5
            dx = place_x - centre_x + 0.5 * HEIGHT
            dx = jnp.where(dx >= HEIGHT, dx - HEIGHT, dx)
            dx = jnp.where(dx < 0, dx + HEIGHT, dx) - 0.5 * HEIGHT
            dy = place_y - centre_y + 0.5 * COLS
            dy = jnp.where(dy >= COLS, dy - COLS, dy)
            dy = jnp.where(dy < 0, dy + COLS, dy) - 0.5 * COLS
            live = slot_id + h * COLS < count_ref[0, t]
            spread = found[2:3] * (1.0 + (dx * dx + dy * dy) / float(LOC * LOC))
            rho = jnp.where(live, 1.0 / spread, 0.0)
            obs = in_ref[:, COLS_HERE + 2 * t + h].reshape(members, COLS)
            mean = jnp.sum(obs, axis=0, keepdims=True) * (1.0 / members)
            values.append(found[1:2] - mean)
            rhos.append(rho)
            anomalies.append(obs - mean)
        anomaly = jnp.concatenate(anomalies, axis=1)
        rho = jnp.concatenate(rhos, axis=1)
        innovation = jnp.concatenate(values, axis=1)
        drives.append(jnp.sum(anomaly * (rho * innovation), axis=1, keepdims=True))
        scaled = parts(anomaly * jnp.sqrt(rho))
        gram = product(scaled, scaled, (((1,), (1,)), ((), ())))
        gram = plus_identity(gram, (members - 1) / INFLATION)
        norm = jnp.sqrt(jnp.sum(jnp.sum(gram * gram, axis=1, keepdims=True), axis=0, keepdims=True))
        norms.append(norm)
        it = gram / norm
        factor = plus_identity(-0.5 * it, 1.5)
        root_ref[t] = factor
        it_ref[t] = product(parts(it), parts(factor))

    def iteration(_, c):
        for t in range(2):
            root, it = parts(root_ref[t]), parts(it_ref[t])
            factor = parts(plus_identity(-0.5 * product(root, it), 1.5))
            it_ref[t] = product(it, factor)
            root_ref[t] = product(factor, root)
        return c

    lax.fori_loop(0, NS_ITERS - 2, iteration, 0)

    for t in range(2):
        root, it = parts(root_ref[t]), parts(it_ref[t])
        factor = parts(plus_identity(-0.5 * product(root, it), 1.5))
        full = product(factor, root)
        inner = jnp.sum(full * drives[t], axis=0, keepdims=True)
        shift = jnp.sum(full * inner, axis=1, keepdims=True) / norms[t]
        scale = jnp.sqrt((members - 1) / norms[t])
        root = parts(full * scale)
        for c in range(4 * t, 4 * t + 4):
            x = in_ref[:, c].reshape(members, COLS)
            mean = jnp.sum(x, axis=0, keepdims=True) * (1.0 / members)
            x = x - mean
            moved = mean + jnp.sum(x * shift, axis=0, keepdims=True)
            out = product(root, parts(x)) + moved
            out_ref[:, c] = out.reshape(PER_MEM, PER_MEM, COLS)


def finish_kernel(in_ref, out_ref):
    def member(m, _):
        block = in_ref[pl.ds(m, COLS, stride=PER_MEM), :].T
        for r in range(ROWS):
            out_ref[pl.ds(m * CELL_ROWS + r, LEVELS, stride=ROWS), :] = block[r * LEVELS : (r + 1) * LEVELS]
        return 0

    lax.fori_loop(0, PER_MEM, member, 0)


SMEM = pl.BlockSpec(memory_space=pltpu.SMEM)
VMEM = pl.BlockSpec(memory_space=pltpu.VMEM)


def shards(prior, north, east, mix, obs_cell, obs_value, obs_var, tile_list, tile_count):
    dom, mem = lax.axis_index("dom"), lax.axis_index("mem")
    where = jnp.stack([dom, mem]).astype(jnp.int32)
    own = tile_list.reshape(SLOT_ROWS, COLS)
    lists = own
    for bit in range(4):
        other = lax.ppermute(lists, "mem", [(i, i ^ (1 << bit)) for i in range(PER_MEM)])
        lists = jnp.concatenate([lists, other], axis=0)

    meta = jnp.concatenate([obs_cell.astype(F32), obs_value, obs_var]).reshape(META, COLS)
    packed = jnp.concatenate(
        [prior.reshape(PER_MEM, CELL_ROWS, COLS), jnp.broadcast_to(meta[None], (PER_MEM, META, COLS))], axis=1
    )
    whole = lax.all_to_all(packed, "dom", split_axis=0, concat_axis=0, tiled=True)
    field, near = pl.pallas_call(
        forecast_kernel,
        name="forecast",
        out_shape=(
            jax.ShapeDtypeStruct((STRIPS * PACK, COLS), F32),
            jax.ShapeDtypeStruct((META * 8, COLS), F32),
        ),
        in_specs=[SMEM, SMEM, SMEM, SMEM, VMEM],
        out_specs=(VMEM, VMEM),
        scratch_shapes=[
            pltpu.VMEM((HEIGHT * LEVELS, COLS), F32),
            pltpu.VMEM((HEIGHT * LEVELS, COLS), F32),
            pltpu.VMEM((HEIGHT * LEVELS, COLS), F32),
            pltpu.VMEM((STRIPS * OBS_CHUNKS, COLS), F32),
        ],
    )(where, north, east, mix, whole.reshape(STRIPS * PACK, COLS))
    strip = lax.all_to_all(
        field.reshape(STRIPS, PACK, COLS), "dom", split_axis=0, concat_axis=0, tiled=True
    )
    sent = pl.pallas_call(
        select_kernel,
        name="select",
        out_shape=jax.ShapeDtypeStruct((PER_MEM * SEND * PER_MEM, COLS), F32),
        in_specs=[SMEM, VMEM, VMEM],
        out_specs=VMEM,
        scratch_shapes=[pltpu.VMEM((META * PER_MEM, COLS), F32)],
    )(where, lists, strip.reshape(PER_MEM * PACK, COLS))
    tiles = lax.all_to_all(
        sent.reshape(PER_MEM, SEND * PER_MEM, COLS), "mem", split_axis=0, concat_axis=0, tiled=True
    )
    updated = pl.pallas_call(
        update_kernel,
        name="update",
        out_shape=jax.ShapeDtypeStruct((PER_MEM, COLS_HERE, PER_MEM, COLS), F32),
        in_specs=[SMEM, SMEM, VMEM, VMEM, VMEM],
        out_specs=VMEM,
        scratch_shapes=[pltpu.VMEM((2, 256, 256), F32), pltpu.VMEM((2, 256, 256), F32)],
    )(where, tile_count, own, near, tiles.reshape(PER_MEM, SEND, PER_MEM, COLS))
    back = lax.all_to_all(
        updated.reshape(PER_MEM, COLS_HERE * PER_MEM, COLS), "mem", split_axis=0, concat_axis=0, tiled=True
    )
    result = pl.pallas_call(
        finish_kernel,
        name="finish",
        out_shape=jax.ShapeDtypeStruct((PER_MEM * CELL_ROWS, COLS), F32),
        in_specs=[VMEM],
        out_specs=VMEM,
    )(back.reshape(PER_MEM * COLS_HERE * PER_MEM, COLS))
    return result.reshape(PER_MEM, LEVELS, ROWS, COLS)


def solution(mesh):
    placed = (
        P("mem", None, "dom", None),
        P(),
        P(),
        P(),
        P("dom"),
        P("dom"),
        P("dom"),
        P("dom", "mem", None),
        P("dom", "mem"),
    )
    return jax.shard_map(
        shards, mesh=mesh, in_specs=placed, out_specs=P("mem", None, "dom", None), check_vma=False
    )
```

profile of v0, /device:TPU:1, one launch (start us, length us, event | category | flops | bytes accessed | tf_op | source)
XLA Modules:
  0.0 201.0 jit_solution(14868267391991432360)
XLA Ops:
  0.0 0.7 convert_bitcast_fusion
  0.7 0.7 pad_maximum_fusion.1
  1.4 2.4 %pad_maximum_fusion = f32[16,152,128]{2,1,0:T(8,128)} fusion(f32[16,24,128]{2,1,0:T(8,128)S(1)} %broadcast_in_dim.2, f32[16,128,128]{2,1,0:T(8,128)} %bitcast.22), kind=kLoop, calls=%fused_computation | loop fusion | flops 311296 | bytes 2490368 | tf_op jit(solution)/shard_map/concatenate | solution.py:276
  3.8 7.6 %all-to-all-start = ((f32[16,152,128]{2,1,0:T(8,128)}), f32[16,152,128]{2,1,0:T(8,128)S(1)}, u32[]{:S(2)}, u32[]{:S(2)}) async-start(f32[16,152,128]{2,1,0:T(8,128)} %pad_maximum_fusion), calls=%async_computation | async-start | bytes 2490368 | tf_op jit(solution)/shard_map/all_to_all | solution.py:279
  11.4 0.6 pad_add_fusion.3.where_ref
  11.9 17.0 %all-to-all-done = f32[16,152,128]{2,1,0:T(8,128)S(1)} async-done(((f32[16,152,128]{2,1,0:T(8,128)}), f32[16,152,128]{2,1,0:T(8,128)S(1)}, u32[]{:S(2)}, u32[]{:S(2)}) %all-to-all-start) | async-done | bytes 1245216 | tf_op jit(solution)/shard_map/all_to_all | solution.py:279
  29.0 0.0 copy-start.1
  29.0 1.0 copy-done.1
  30.0 42.5 %forecast.1 = (f32[2432,128]{1,0:T(8,128)}, f32[192,128]{1,0:T(8,128)}) custom-call(s32[2]{0:T(128)} %pad_add_fusion.3.where_ref, f32[32]{0:T(128)} %north_ref.1, f32[32]{0:T(128)} %east_ref.1, f32[32]{0:T(128)} %mix_ref.1, f32[2432,128]{1,0:T(8,128)} %bitcast.18), custom_call_target="tpu_custom_call" | custom-call | tf_op jit(solution)/shard_map/forecast/pallas_call | solution.py:280
  72.5 0.0 copy-start.3
  72.5 4.4 %all-to-all-start.1 = ((f32[16,152,128]{2,1,0:T(8,128)}), f32[16,152,128]{2,1,0:T(8,128)S(1)}, u32[]{:S(2)}, u32[]{:S(2)}) async-start(f32[16,152,128]{2,1,0:T(8,128)} %bitcast.21), calls=%async_computation.1 | async-start | bytes 2490368 | tf_op jit(solution)/shard_map/all_to_all | solution.py:296
  76.9 0.0 copy-done.3
  77.0 0.0 copy-start.2
  77.0 2.9 %collective-permute-start = (s32[4,128]{1,0:T(4,128)S(1)}, s32[4,128]{1,0:T(4,128)S(1)}, u32[]{:S(2)}, u32[]{:S(2)}) collective-permute-start(s32[4,128]{1,0:T(4,128)S(1)} %reshape.34.list_ref), channel_id=1, source_target_pairs={{0,16},{16,0},{32,48},{48,32},{64,80},{80,64},{96,112},{112,96},{1... | collective-permute-start | bytes 6152 | tf_op jit(solution)/shard_map/ppermute | solution.py:272
  79.8 0.8 collective-permute-done
  80.7 1.6 collective-permute-start.1
  82.3 1.3 collective-permute-done.1
  83.6 3.0 %collective-permute-start.2 = (s32[16,128]{1,0:T(8,128)S(1)}, s32[16,128]{1,0:T(8,128)S(1)}, u32[]{:S(2)}, u32[]{:S(2)}) collective-permute-start(s32[16,128]{1,0:T(8,128)S(1)} %pad_add_fusion.1), channel_id=1, source_target_pairs={{0,64},{16,80},{32,96},{48,112},{64,0},{80,16},{96,32},{112,48},{1... | collective-permute-start | bytes 24584 | tf_op jit(solution)/shard_map/ppermute | solution.py:272
  86.6 1.3 collective-permute-done.2
  87.9 6.1 %collective-permute-start.3 = (s32[32,128]{1,0:T(8,128)S(1)}, s32[32,128]{1,0:T(8,128)S(1)}, u32[]{:S(2)}, u32[]{:S(2)}) collective-permute-start(s32[32,128]{1,0:T(8,128)S(1)} %pad_add_fusion), channel_id=1, source_target_pairs={{0,128},{16,144},{32,160},{48,176},{64,192},{80,208},{96,224},{112... | collective-permute-start | bytes 49160 | tf_op jit(solution)/shard_map/ppermute | solution.py:272
  94.0 1.4 collective-permute-done.3
  95.5 2.4 %concatenate.36.list_ref = s32[64,128]{1,0:T(8,128)} concatenate(s32[4,128]{1,0:T(4,128)S(1)} %reshape.34.list_ref, s32[4,128]{1,0:T(4,128)S(1)} %collective-permute-done, s32[8,128]{1,0:T(8,128)S(1)} %collective-permute-done.1, s32[16,128]{1,0:T(8,128)S(1)} %collective-permute-done.2, s32[32,128]{1,0:T(8,128)S(1)} %collective-permute-done.3), dimensions={0} | concatenate | bytes 65536 | tf_op jit(solution)/shard_map/concatenate | solution.py:273
  97.9 0.0 all-to-all-done.1
  97.9 0.0 copy-start
  97.9 1.0 copy-done
  98.9 7.1 %select.1 = f32[3072,128]{1,0:T(8,128)} custom-call(s32[2]{0:T(128)} %pad_add_fusion.3.where_ref, s32[64,128]{1,0:T(8,128)} %concatenate.36.list_ref, f32[2432,128]{1,0:T(8,128)} %bitcast.17), custom_call_target="tpu_custom_call" | custom-call | tf_op jit(solution)/shard_map/select/pallas_call | solution.py:299
  106.0 0.0 copy-done.2
  106.0 49.6 %all_to_all.20 = f32[16,192,128]{2,1,0:T(8,128)} all-to-all(f32[16,192,128]{2,1,0:T(8,128)} %bitcast.16), channel_id=1, replica_groups=mesh['mem'=16,'dom'=16] {'mem'}, dimensions={0} | all-to-all | bytes 3145728 | tf_op jit(solution)/shard_map/all_to_all | solution.py:307
  155.7 9.9 %update.1 = f32[16,8,16,128]{3,2,1,0:T(8,128)} custom-call(s32[2]{0:T(128)} %pad_add_fusion.3.where_ref, s32[1,2]{1,0:T(1,128)} %count_ref.1, s32[4,128]{1,0:T(4,128)} %copy-done.2, f32[192,128]{1,0:T(8,128)} %get-tuple-element.7.meta_ref, f32[16,12,16,128]{3,2,1,0:T(8,128)} %bitcast.15), custom_call_target="tpu_custom_call" | custom-call | tf_op jit(solution)/shard_map/update/pallas_call | solution.py:310
  165.6 31.6 %all_to_all.21 = f32[16,128,128]{2,1,0:T(8,128)} all-to-all(f32[16,128,128]{2,1,0:T(8,128)} %bitcast.19), channel_id=1, replica_groups=mesh['mem'=16,'dom'=16] {'mem'}, dimensions={0} | all-to-all | bytes 2097152 | tf_op jit(solution)/shard_map/all_to_all | solution.py:318
  197.2 3.9 %finish.1 = f32[2048,128]{1,0:T(8,128)} custom-call(f32[2048,128]{1,0:T(8,128)} %bitcast.20), custom_call_target="tpu_custom_call" | custom-call | tf_op jit(solution)/shard_map/finish/pallas_call | solution.py:321
  (5 shorter events, 0.1 us)
Async XLA Ops:
  3.8 25.2 %all-to-all-start = ((f32[16,152,128]{2,1,0:T(8,128)}), f32[16,152,128]{2,1,0:T(8,128)S(1)}, u32[]{:S(2)}, u32[]{:S(2)}) async-start(f32[16,152,128]{2,1,0:T(8,128)} %pad_maximum_fusion), calls=%async_computation | async-start | bytes 2490368 | tf_op jit(solution)/shard_map/all_to_all | solution.py:279
  29.0 1.0 copy-start.1
  72.5 4.4 %copy-start.3 = (s32[1,2,256]{2,1,0:T(2,128)S(1)}, s32[1,2,256]{2,1,0:T(2,128)}, u32[]{:S(2)}) copy-start(s32[1,2,256]{2,1,0:T(2,128)} %param.16) | copy-start | bytes 6148
  72.5 25.4 %all-to-all-start.1 = ((f32[16,152,128]{2,1,0:T(8,128)}), f32[16,152,128]{2,1,0:T(8,128)S(1)}, u32[]{:S(2)}, u32[]{:S(2)}) async-start(f32[16,152,128]{2,1,0:T(8,128)} %bitcast.21), calls=%async_computation.1 | async-start | bytes 2490368 | tf_op jit(solution)/shard_map/all_to_all | solution.py:296
  77.0 29.1 %copy-start.2 = (s32[4,128]{1,0:T(4,128)}, s32[4,128]{1,0:T(4,128)S(1)}, u32[]{:S(2)}) copy-start(s32[4,128]{1,0:T(4,128)S(1)} %reshape.34.list_ref) | copy-start | bytes 6148
  77.0 3.7 %collective-permute-start = (s32[4,128]{1,0:T(4,128)S(1)}, s32[4,128]{1,0:T(4,128)S(1)}, u32[]{:S(2)}, u32[]{:S(2)}) collective-permute-start(s32[4,128]{1,0:T(4,128)S(1)} %reshape.34.list_ref), channel_id=1, source_target_pairs={{0,16},{16,0},{32,48},{48,32},{64,80},{80,64},{96,112},{112,96},{1... | collective-permute-start | bytes 6152 | tf_op jit(solution)/shard_map/ppermute | solution.py:272
  80.7 2.9 %collective-permute-start.1 = (s32[8,128]{1,0:T(8,128)S(1)}, s32[8,128]{1,0:T(8,128)S(1)}, u32[]{:S(2)}, u32[]{:S(2)}) collective-permute-start(s32[8,128]{1,0:T(8,128)S(1)} %pad_add_fusion.2), channel_id=1, source_target_pairs={{0,32},{16,48},{32,0},{48,16},{64,96},{80,112},{96,64},{112,80},{1... | collective-permute-start | bytes 12296 | tf_op jit(solution)/shard_map/ppermute | solution.py:272
  83.6 4.3 %collective-permute-start.2 = (s32[16,128]{1,0:T(8,128)S(1)}, s32[16,128]{1,0:T(8,128)S(1)}, u32[]{:S(2)}, u32[]{:S(2)}) collective-permute-start(s32[16,128]{1,0:T(8,128)S(1)} %pad_add_fusion.1), channel_id=1, source_target_pairs={{0,64},{16,80},{32,96},{48,112},{64,0},{80,16},{96,32},{112,48},{1... | collective-permute-start | bytes 24584 | tf_op jit(solution)/shard_map/ppermute | solution.py:272
  87.9 7.5 %collective-permute-start.3 = (s32[32,128]{1,0:T(8,128)S(1)}, s32[32,128]{1,0:T(8,128)S(1)}, u32[]{:S(2)}, u32[]{:S(2)}) collective-permute-start(s32[32,128]{1,0:T(8,128)S(1)} %pad_add_fusion), channel_id=1, source_target_pairs={{0,128},{16,144},{32,160},{48,176},{64,192},{80,208},{96,224},{112... | collective-permute-start | bytes 49160 | tf_op jit(solution)/shard_map/ppermute | solution.py:272
  97.9 1.0 copy-start
where the time goes:
time: 202 us; the launch traced here: 201 us
  blocking collectives  81.2 us (40%)
  Pallas kernels  63.4 us (31%)
  starting transfers between devices  25.6 us (13%)
  waiting for transfers between devices  21.9 us (11%)
  local copies, waits for them, and re-layouts  4.51 us (2%)
  other arithmetic  4.37 us (2%)
    all_to_all x1, blocking collectives, shards(): lax.all_to_all(sent.reshape(PER_MEM, SEND * PER_MEM, COLS), 'mem', split_...  49.6 us
    pallas_call x1, Pallas kernels, shards(): pl.pallas_call(forecast_kernel, name='forecast', out_shape=(jax.ShapeDtyp...  42.5 us
    all_to_all x1, blocking collectives, shards(): lax.all_to_all(updated.reshape(PER_MEM, COLS_HERE * PER_MEM, COLS), 'mem'...  31.6 us
    all_to_all x1, waiting for transfers between devices, shards(): lax.all_to_all(packed, 'dom', split_axis=0, concat_axis=0, tiled=True)  17 us
    ppermute x4, starting transfers between devices, shards(): lax.ppermute(lists, 'mem', [(i, i ^ 1 << bit) for i in range(PER_MEM)])  13.6 us
    pallas_call x1, Pallas kernels, shards(): pl.pallas_call(update_kernel, name='update', out_shape=jax.ShapeDtypeStru...  9.94 us
    all_to_all x1, starting transfers between devices, shards(): lax.all_to_all(packed, 'dom', split_axis=0, concat_axis=0, tiled=True)  7.57 us
    pallas_call x1, Pallas kernels, shards(): pl.pallas_call(select_kernel, name='select', out_shape=jax.ShapeDtypeStru...  7.11 us
  transfers between devices with their start and end apart: 6, of which 5 were waited for; matrix products, arithmetic and copies ran while one was open for 2% of the time, Pallas kernels for 0%

commit v1 on v0

--- a/solution.py
+++ b/solution.py
@@ -31,7 +31,7 @@
     return jnp.take_along_axis(values, lanes, axis=1, mode="promise_in_bounds")
 
 
-def forecast_kernel(where_ref, north_ref, east_ref, mix_ref, in_ref, out_ref, meta_ref, q_ref, t1_ref, t2_ref, hx_ref):
+def forecast_kernel(where_ref, north_ref, east_ref, mix_ref, in_ref, list_ref, out_ref, meta_ref, q_ref, t1_ref, t2_ref, hx_ref):
     def load(s, _):
         for r in range(ROWS):
             q_ref[pl.ds(s * CELL_ROWS + r * LEVELS, LEVELS), :] = in_ref[
@@ -61,18 +61,18 @@
             def at(ref, x):
                 return ref.at[pl.ds(pl.multiple_of(x * LEVELS + g * 8, 8), 8), :]
 
-            def row(x, carry):
-                prev, cur = carry
-                nxt = at(src, lax.rem(x + 1, HEIGHT))[...]
+            prev, cur = at(src, HEIGHT - 1)[...], at(src, 0)[...]
+            first = cur
+            for x in range(HEIGHT):
+                nxt = first if x == HEIGHT - 1 else at(src, x + 1)[...]
+                base = cur if src is q_ref else at(q_ref, x)[...]
                 at(dst, x)[...] = (
-                    at(q_ref, x)[...]
+                    base
                     + (a * nxt + b * prev)
                     + (c * pltpu.roll(cur, COLS - 1, 1) + d * pltpu.roll(cur, 1, 1))
                     + e * cur
                 )
-                return cur, nxt
-
-            lax.fori_loop(0, HEIGHT, row, (at(src, HEIGHT - 1)[...], at(src, 0)[...]), unroll=8)
+                prev, cur = cur, nxt
 
         def step(_, c):
             stage(q_ref, t1_ref, 1.0 / 3.0)
@@ -259,6 +259,7 @@
     lax.fori_loop(0, PER_MEM, member, 0)
 
 
+PARAMS = pltpu.CompilerParams(vmem_limit_bytes=20 * 1024 * 1024)
 SMEM = pl.BlockSpec(memory_space=pltpu.SMEM)
 VMEM = pl.BlockSpec(memory_space=pltpu.VMEM)
 
@@ -279,12 +280,13 @@
     whole = lax.all_to_all(packed, "dom", split_axis=0, concat_axis=0, tiled=True)
     field, near = pl.pallas_call(
         forecast_kernel,
+        compiler_params=PARAMS,
         name="forecast",
         out_shape=(
             jax.ShapeDtypeStruct((STRIPS * PACK, COLS), F32),
             jax.ShapeDtypeStruct((META * 8, COLS), F32),
         ),
-        in_specs=[SMEM, SMEM, SMEM, SMEM, VMEM],
+        in_specs=[SMEM, SMEM, SMEM, SMEM, VMEM, pl.BlockSpec(memory_space=pl.ANY)],
         out_specs=(VMEM, VMEM),
         scratch_shapes=[
             pltpu.VMEM((HEIGHT * LEVELS, COLS), F32),
@@ -292,12 +294,13 @@
             pltpu.VMEM((HEIGHT * LEVELS, COLS), F32),
             pltpu.VMEM((STRIPS * OBS_CHUNKS, COLS), F32),
         ],
-    )(where, north, east, mix, whole.reshape(STRIPS * PACK, COLS))
+    )(where, north, east, mix, whole.reshape(STRIPS * PACK, COLS), lists)
     strip = lax.all_to_all(
         field.reshape(STRIPS, PACK, COLS), "dom", split_axis=0, concat_axis=0, tiled=True
     )
     sent = pl.pallas_call(
         select_kernel,
+        compiler_params=PARAMS,
         name="select",
         out_shape=jax.ShapeDtypeStruct((PER_MEM * SEND * PER_MEM, COLS), F32),
         in_specs=[SMEM, VMEM, VMEM],
@@ -309,6 +312,7 @@
     )
     updated = pl.pallas_call(
         update_kernel,
+        compiler_params=PARAMS,
         name="update",
         out_shape=jax.ShapeDtypeStruct((PER_MEM, COLS_HERE, PER_MEM, COLS), F32),
         in_specs=[SMEM, SMEM, VMEM, VMEM, VMEM],
@@ -320,6 +324,7 @@
     )
     result = pl.pallas_call(
         finish_kernel,
+        compiler_params=PARAMS,
         name="finish",
         out_shape=jax.ShapeDtypeStruct((PER_MEM * CELL_ROWS, COLS), F32),
         in_specs=[VMEM],

time: 202 us -> 167 us (0.83)
  Pallas kernels: 63.4 us -> 34.3 us
  blocking collectives: 81.2 us -> 103 us
  waiting for transfers between devices: 21.9 us -> 5.7 us
  starting transfers between devices: 25.6 us -> 19.5 us
  local copies, waits for them, and re-layouts: 4.51 us -> 0.07 us
    pallas_call x4, Pallas kernels: 63.4 us -> 34.3 us  [the longest x1 18.4 us: shards(): pl.pallas_call(forecast_kernel, compiler_params=PARAMS, name='forecast',...]
    all_to_all x0 -> x1, blocking collectives: none -> 21.1 us  [shards(): lax.all_to_all(field.reshape(STRIPS, PACK, COLS), 'dom', split_axis=0, co...]
    all_to_all x1, waiting for transfers between devices: 17 us -> 0.92 us  [shards(): lax.all_to_all(packed, 'dom', split_axis=0, concat_axis=0, tiled=True)]
    all_to_all x1 -> x0, starting transfers between devices: 4.43 us -> none  [shards(): lax.all_to_all(field.reshape(STRIPS, PACK, COLS), 'dom', split_axis=0, co...]
    concatenate x1, local copies, waits for them, and re-layouts: 2.4 us -> 0.02 us  [shards(): lists = jnp.concatenate([lists, other], axis=0)]
    unnamed x8 -> x10, local copies, waits for them, and re-layouts: 2.08 us -> 0.02 us
  transfers between devices with their start and end apart: 6 -> 5, of which waited for: 5 -> 5; matrix products, arithmetic and copies ran while one was open for 2% -> 0% of each run, Pallas kernels for 0% -> 0%
where the time goes in v1:
time: 167 us
  blocking collectives  103 us (62%)
  Pallas kernels  34.3 us (21%)
  starting transfers between devices  19.5 us (12%)
  waiting for transfers between devices  5.7 us (3%)
  other arithmetic  3.86 us (2%)
    all_to_all x1, blocking collectives, shards(): lax.all_to_all(sent.reshape(PER_MEM, SEND * PER_MEM, COLS), 'mem', split_...  50.9 us
    all_to_all x1, blocking collectives, shards(): lax.all_to_all(updated.reshape(PER_MEM, COLS_HERE * PER_MEM, COLS), 'mem'...  31.2 us
    all_to_all x1, blocking collectives, shards(): lax.all_to_all(field.reshape(STRIPS, PACK, COLS), 'dom', split_axis=0, co...  21.1 us
    pallas_call x1, Pallas kernels, shards(): pl.pallas_call(forecast_kernel, compiler_params=PARAMS, name='forecast',...  18.4 us
    ppermute x4, starting transfers between devices, shards(): lax.ppermute(lists, 'mem', [(i, i ^ 1 << bit) for i in range(PER_MEM)])  11.8 us
    pallas_call x1, Pallas kernels, shards(): pl.pallas_call(update_kernel, compiler_params=PARAMS, name='update', out_...  8.04 us
    all_to_all x1, starting transfers between devices, shards(): lax.all_to_all(packed, 'dom', split_axis=0, concat_axis=0, tiled=True)  7.72 us
    pallas_call x1, Pallas kernels, shards(): pl.pallas_call(select_kernel, compiler_params=PARAMS, name='select', out_...  5.17 us
  transfers between devices with their start and end apart: 5, of which 5 were waited for; matrix products, arithmetic and copies ran while one was open for 0% of the time, Pallas kernels for 0%

profile of v1, /device:TPU:1, one launch (start us, length us, event | category | flops | bytes accessed | tf_op | source)
XLA Modules:
  0.0 166.7 jit_solution(4611335758801917134)
XLA Ops:
  0.0 0.7 convert_bitcast_fusion
  0.7 0.7 pad_maximum_fusion.1
  1.4 2.4 %pad_maximum_fusion = f32[16,152,128]{2,1,0:T(8,128)} fusion(f32[16,24,128]{2,1,0:T(8,128)S(1)} %broadcast_in_dim.2, f32[16,128,128]{2,1,0:T(8,128)} %bitcast.22), kind=kLoop, calls=%fused_computation | loop fusion | flops 311296 | bytes 2490368 | tf_op jit(solution)/shard_map/concatenate | solution.py:277
  3.8 0.0 copy-start.4
  3.8 0.0 copy-start
  3.8 0.0 copy-start.1
  3.8 0.0 copy-start.2
  3.8 7.7 %all-to-all-start = ((f32[16,152,128]{2,1,0:T(8,128)}), f32[16,152,128]{2,1,0:T(8,128)S(1)}, u32[]{:S(2)}, u32[]{:S(2)}) async-start(f32[16,152,128]{2,1,0:T(8,128)} %pad_maximum_fusion), calls=%async_computation | async-start | bytes 2490368 | tf_op jit(solution)/shard_map/all_to_all | solution.py:280
  11.5 0.0 copy-done.4
  11.5 1.0 collective-permute-start
  12.6 0.8 collective-permute-done
  13.4 1.6 collective-permute-start.1
  15.1 1.3 collective-permute-done.1
  16.3 3.0 %collective-permute-start.2 = (s32[16,128]{1,0:T(8,128)S(1)}, s32[16,128]{1,0:T(8,128)S(1)}, u32[]{:S(2)}, u32[]{:S(2)}) collective-permute-start(s32[16,128]{1,0:T(8,128)S(1)} %pad_add_fusion.1), channel_id=1, source_target_pairs={{0,64},{16,80},{32,96},{48,112},{64,0},{80,16},{96,32},{112,48},{1... | collective-permute-start | bytes 24584 | tf_op jit(solution)/shard_map/ppermute | solution.py:273
  19.3 1.3 collective-permute-done.2
  20.7 6.1 %collective-permute-start.3 = (s32[32,128]{1,0:T(8,128)S(1)}, s32[32,128]{1,0:T(8,128)S(1)}, u32[]{:S(2)}, u32[]{:S(2)}) collective-permute-start(s32[32,128]{1,0:T(8,128)S(1)} %pad_add_fusion), channel_id=1, source_target_pairs={{0,128},{16,144},{32,160},{48,176},{64,192},{80,208},{96,224},{112... | collective-permute-start | bytes 49160 | tf_op jit(solution)/shard_map/ppermute | solution.py:273
  26.8 0.1 pad_add_fusion.3.where_ref
  26.9 1.3 collective-permute-done.3
  28.2 0.9 all-to-all-done
  29.1 0.0 copy-done
  29.2 0.0 copy-done.1
  29.2 0.0 copy-done.2
  29.2 18.4 %forecast.1 = (f32[2432,128]{1,0:T(8,128)S(1)}, f32[192,128]{1,0:T(8,128)S(1)}) custom-call(s32[2]{0:T(128)S(1)} %pad_add_fusion.3.where_ref, f32[32]{0:T(128)S(1)} %copy-done, f32[32]{0:T(128)S(1)} %copy-done.1, f32[32]{0:T(128)S(1)} %copy-done.2, f32[2432,128]{1,0:T(8,128)S(1)} %bitcast.17, s32[64,128]{1,0:T(8,128)S(1)} %concatenate.36.list_ref), custom_call_target="tpu_custom_call" | custom-call | tf_op jit(solution)/shard_map/forecast/pallas_call | solution.py:281
  47.6 21.1 %all_to_all.20 = f32[16,152,128]{2,1,0:T(8,128)S(1)} all-to-all(f32[16,152,128]{2,1,0:T(8,128)S(1)} %bitcast.21), channel_id=1, replica_groups=mesh['mem'=16,'dom'=16] {'dom'}, dimensions={0} | all-to-all | bytes 2490368 | tf_op jit(solution)/shard_map/all_to_all | solution.py:298
  68.7 5.2 %select.1 = f32[3072,128]{1,0:T(8,128)S(1)} custom-call(s32[2]{0:T(128)S(1)} %pad_add_fusion.3.where_ref, s32[64,128]{1,0:T(8,128)S(1)} %concatenate.36.list_ref, f32[2432,128]{1,0:T(8,128)S(1)} %bitcast.18), custom_call_target="tpu_custom_call" | custom-call | tf_op jit(solution)/shard_map/select/pallas_call | solution.py:301
  73.9 0.0 copy-start.3
  73.9 50.9 %all_to_all.21 = f32[16,192,128]{2,1,0:T(8,128)S(1)} all-to-all(f32[16,192,128]{2,1,0:T(8,128)S(1)} %bitcast.16), channel_id=1, replica_groups=mesh['mem'=16,'dom'=16] {'mem'}, dimensions={0} | all-to-all | bytes 3145728 | tf_op jit(solution)/shard_map/all_to_all | solution.py:310
  124.8 0.0 copy-done.3
  124.8 8.0 %update.1 = f32[16,8,16,128]{3,2,1,0:T(8,128)S(1)} custom-call(s32[2]{0:T(128)S(1)} %pad_add_fusion.3.where_ref, s32[1,2]{1,0:T(1,128)S(1)} %copy-done.3, s32[4,128]{1,0:T(4,128)S(1)} %reshape.34.list_ref, f32[192,128]{1,0:T(8,128)S(1)} %get-tuple-element.7.meta_ref, f32[16,12,16,128]{3,2,1,0:T(8,128)S(1)} %bitcast.15), custom_call_target="tpu_custom_call" | custom-call | tf_op jit(solution)/shard_map/update/pallas_call | solution.py:313
  132.9 31.2 %all_to_all.22 = f32[16,128,128]{2,1,0:T(8,128)S(1)} all-to-all(f32[16,128,128]{2,1,0:T(8,128)S(1)} %bitcast.19), channel_id=1, replica_groups=mesh['mem'=16,'dom'=16] {'mem'}, dimensions={0} | all-to-all | bytes 2097152 | tf_op jit(solution)/shard_map/all_to_all | solution.py:322
  164.1 2.6 %finish.1 = f32[2048,128]{1,0:T(8,128)} custom-call(f32[2048,128]{1,0:T(8,128)S(1)} %bitcast.20), custom_call_target="tpu_custom_call" | custom-call | tf_op jit(solution)/shard_map/finish/pallas_call | solution.py:325
  (6 shorter events, 0.1 us)
Async XLA Ops:
  3.8 7.7 %copy-start.4 = (s32[1,2,256]{2,1,0:T(2,128)S(1)}, s32[1,2,256]{2,1,0:T(2,128)}, u32[]{:S(2)}) copy-start(s32[1,2,256]{2,1,0:T(2,128)} %param.16) | copy-start | bytes 6148
  3.8 25.4 %copy-start = (f32[32]{0:T(128)S(1)}, f32[32]{0:T(128)}, u32[]{:S(2)}) copy-start(f32[32]{0:T(128)} %north_ref.1) | copy-start | bytes 388
  3.8 25.4 %copy-start.1 = (f32[32]{0:T(128)S(1)}, f32[32]{0:T(128)}, u32[]{:S(2)}) copy-start(f32[32]{0:T(128)} %east_ref.1) | copy-start | bytes 388
  3.8 25.4 %copy-start.2 = (f32[32]{0:T(128)S(1)}, f32[32]{0:T(128)}, u32[]{:S(2)}) copy-start(f32[32]{0:T(128)} %mix_ref.1) | copy-start | bytes 388
  3.8 25.4 %all-to-all-start = ((f32[16,152,128]{2,1,0:T(8,128)}), f32[16,152,128]{2,1,0:T(8,128)S(1)}, u32[]{:S(2)}, u32[]{:S(2)}) async-start(f32[16,152,128]{2,1,0:T(8,128)} %pad_maximum_fusion), calls=%async_computation | async-start | bytes 2490368 | tf_op jit(solution)/shard_map/all_to_all | solution.py:280
  11.5 1.9 %collective-permute-start = (s32[4,128]{1,0:T(4,128)S(1)}, s32[4,128]{1,0:T(4,128)S(1)}, u32[]{:S(2)}, u32[]{:S(2)}) collective-permute-start(s32[4,128]{1,0:T(4,128)S(1)} %reshape.34.list_ref), channel_id=1, source_target_pairs={{0,16},{16,0},{32,48},{48,32},{64,80},{80,64},{96,112},{112,96},{1... | collective-permute-start | bytes 6152 | tf_op jit(solution)/shard_map/ppermute | solution.py:273
  13.4 2.9 %collective-permute-start.1 = (s32[8,128]{1,0:T(8,128)S(1)}, s32[8,128]{1,0:T(8,128)S(1)}, u32[]{:S(2)}, u32[]{:S(2)}) collective-permute-start(s32[8,128]{1,0:T(8,128)S(1)} %pad_add_fusion.2), channel_id=1, source_target_pairs={{0,32},{16,48},{32,0},{48,16},{64,96},{80,112},{96,64},{112,80},{1... | collective-permute-start | bytes 12296 | tf_op jit(solution)/shard_map/ppermute | solution.py:273
  16.3 4.3 %collective-permute-start.2 = (s32[16,128]{1,0:T(8,128)S(1)}, s32[16,128]{1,0:T(8,128)S(1)}, u32[]{:S(2)}, u32[]{:S(2)}) collective-permute-start(s32[16,128]{1,0:T(8,128)S(1)} %pad_add_fusion.1), channel_id=1, source_target_pairs={{0,64},{16,80},{32,96},{48,112},{64,0},{80,16},{96,32},{112,48},{1... | collective-permute-start | bytes 24584 | tf_op jit(solution)/shard_map/ppermute | solution.py:273
  20.7 7.5 %collective-permute-start.3 = (s32[32,128]{1,0:T(8,128)S(1)}, s32[32,128]{1,0:T(8,128)S(1)}, u32[]{:S(2)}, u32[]{:S(2)}) collective-permute-start(s32[32,128]{1,0:T(8,128)S(1)} %pad_add_fusion), channel_id=1, source_target_pairs={{0,128},{16,144},{32,160},{48,176},{64,192},{80,208},{96,224},{112... | collective-permute-start | bytes 49160 | tf_op jit(solution)/shard_map/ppermute | solution.py:273
  73.9 50.9 %copy-start.3 = (s32[1,2]{1,0:T(1,128)S(1)}, s32[1,2]{1,0:T(1,128)}, u32[]{:S(2)}) copy-start(s32[1,2]{1,0:T(1,128)} %count_ref.1) | copy-start | bytes 28

commit v2 on v1

--- a/solution.py
+++ b/solution.py
@@ -25,16 +25,48 @@
 PER_MEM = 16
 STRIPS = 16
 HEIGHT = STRIPS * ROWS
+PITCH = CELL_ROWS + 8
+
+
+LANES = lax.GatherDimensionNumbers(
+    offset_dims=(),
+    collapsed_slice_dims=(1,),
+    start_index_map=(1,),
+    operand_batching_dims=(0,),
+    start_indices_batching_dims=(0,),
+)
 
 
 def lane_gather(values, lanes):
-    return jnp.take_along_axis(values, lanes, axis=1, mode="promise_in_bounds")
-
-
-def forecast_kernel(where_ref, north_ref, east_ref, mix_ref, in_ref, list_ref, out_ref, meta_ref, q_ref, t1_ref, t2_ref, hx_ref):
+    return lax.gather(
+        values, lanes[..., None], LANES, (1, 1), mode=lax.GatherScatterMode.PROMISE_IN_BOUNDS
+    )
+
+
+def pack_kernel(prior_ref, cell_ref, value_ref, var_ref, out_ref, sems):
+    def copy(m):
+        return pltpu.make_async_copy(
+            prior_ref.at[pl.ds(m * CELL_ROWS, CELL_ROWS), :],
+            out_ref.at[pl.ds(m * PACK, CELL_ROWS), :],
+            sems.at[m],
+        )
+
+    for m in range(PER_MEM):
+        copy(m).start()
+    cell, value, var = cell_ref[...].astype(F32), value_ref[...], var_ref[...]
+    for m in range(PER_MEM):
+        at = m * PACK + CELL_ROWS
+        out_ref[at : at + 8, :] = cell
+        out_ref[at + 8 : at + 16, :] = value
+        out_ref[at + 16 : at + 24, :] = var
+    for m in range(PER_MEM):
+        copy(m).wait()
+
+
+def forecast_kernel(where_ref, north_ref, east_ref, mix_ref, in_ref, out_ref, hx_ref, meta_ref, q_ref, t1_ref, t2_ref):
     def load(s, _):
         for r in range(ROWS):
-            q_ref[pl.ds(s * CELL_ROWS + r * LEVELS, LEVELS), :] = in_ref[
+            q_ref[pl.ds(pl.multiple_of(s * PITCH + r * LEVELS, 8), LEVELS), :] = in_ref[
                 pl.ds(s * PACK + r, LEVELS, stride=ROWS), :
             ]
         return 0
@@ -59,7 +91,8 @@
             a, b, c, d, e = up * scale, down * scale, right * scale, left * scale, mid * scale
 
             def at(ref, x):
-                return ref.at[pl.ds(pl.multiple_of(x * LEVELS + g * 8, 8), 8), :]
+                at_row = x // ROWS * PITCH + x % ROWS * LEVELS
+                return ref.at[pl.ds(pl.multiple_of(at_row + g * 8, 8), 8), :]
 
             prev, cur = at(src, HEIGHT - 1)[...], at(src, 0)[...]
             first = cur
@@ -94,24 +127,21 @@
             rows.append((line & (ROWS - 1)) * LEVELS + (line >> 2))
 
         def pick(p, acc):
-            src = q_ref[pl.ds(p + g * 8 * CELL_ROWS, 8, stride=CELL_ROWS), :]
+            src = q_ref[pl.ds(p + g * 8 * PITCH, 8, stride=PITCH), :]
             return tuple(
                 jnp.where(rows[j] == p, lane_gather(src, lanes[j]), acc[j]) for j in range(OBS_CHUNKS)
             )
 
         acc = lax.fori_loop(
-            0, CELL_ROWS, pick, tuple(jnp.zeros((8, COLS), F32) for _ in range(OBS_CHUNKS)), unroll=4
+            0, CELL_ROWS, pick, tuple(jnp.zeros((8, COLS), F32) for _ in range(OBS_CHUNKS)), unroll=16
         )
         for j in range(OBS_CHUNKS):
             hx_ref[pl.ds(g * 64 + j, 8, stride=OBS_CHUNKS), :] = acc[j]
 
     def store(s, _):
-        base = pl.multiple_of(s * CELL_ROWS, 8)
-        to = pl.multiple_of(s * PACK, 8)
+        base = pl.multiple_of(s * PITCH, 8)
+        to = pl.multiple_of(s * CELL_ROWS, 8)
         out_ref[pl.ds(to, CELL_ROWS), :] = q_ref[pl.ds(base, CELL_ROWS), :].T
-        for t in range(3):
-            strip = lax.rem(s + STRIPS - 1 + t, STRIPS)
-            out_ref[pl.ds(to + CELL_ROWS + 8 * t, 8), :] = hx_ref[pl.ds(pl.multiple_of(strip * 8, 8), 8), :]
         return 0
 
     lax.fori_loop(0, STRIPS, store, 0)
@@ -125,33 +155,32 @@
             ]
 
 
-def select_kernel(where_ref, list_ref, in_ref, out_ref, d_ref):
-    for j in range(META):
-        d_ref[pl.ds(j * PER_MEM, PER_MEM), :] = in_ref[pl.ds(CELL_ROWS + j, PER_MEM, stride=PACK), :]
-
-    def peer(kb, _):
-        to = pl.multiple_of(kb * SEND * PER_MEM, 8)
-        for c in range(COLS_HERE):
-            out_ref[pl.ds(to + c * PER_MEM, PER_MEM), :] = in_ref[
-                pl.ds(kb * COLS_HERE + c, PER_MEM, stride=PACK), :
+def select_kernel(where_ref, list_ref, hx_ref, in_ref, out_ref):
+    def strip(a, _):
+        for kb in range(PER_MEM):
+            out_ref[pl.ds((kb * STRIPS + a) * SEND, COLS_HERE), :] = in_ref[
+                pl.ds(pl.multiple_of(a * CELL_ROWS + kb * COLS_HERE, 8), COLS_HERE), :
             ]
-        first = lax.bitwise_xor(where_ref[1], kb) * SLOT_ROWS
-        for q in range(SLOT_ROWS):
-            slot = jnp.broadcast_to(list_ref[pl.ds(first + q, 1), :], (8, COLS))
+        sources = []
+        for t in range(3):
+            near = lax.rem(a + STRIPS - 1 + t, STRIPS) * OBS_CHUNKS
+            for j in range(OBS_CHUNKS):
+                sources.append(jnp.broadcast_to(hx_ref[pl.ds(near + j, 1), :], (8, COLS)))
+        for g in range(PER_MEM // 2):
+            slot = list_ref[pl.ds(pl.multiple_of(a * PER_MEM * SLOT_ROWS + g * 8, 8), 8), :]
             lanes = slot & (COLS - 1)
             chunk = slot >> 7
-            low = jnp.zeros((8, COLS), F32)
-            high = jnp.zeros((8, COLS), F32)
-            for j in range(META):
-                here = chunk == j
-                low = jnp.where(here, lane_gather(d_ref[pl.ds(j * PER_MEM, 8), :], lanes), low)
-                high = jnp.where(here, lane_gather(d_ref[pl.ds(j * PER_MEM + 8, 8), :], lanes), high)
-            at = to + (COLS_HERE + q) * PER_MEM
-            out_ref[pl.ds(at, 8), :] = low
-            out_ref[pl.ds(at + 8, 8), :] = high
-        return 0
-
-    lax.fori_loop(0, PER_MEM, peer, 0)
+            found = lane_gather(sources[0], lanes)
+            for j in range(1, META):
+                found = jnp.where(chunk == j, lane_gather(sources[j], lanes), found)
+            for i in range(2):
+                kb = lax.bitwise_xor(where_ref[1], 2 * g + i)
+                out_ref[pl.ds((kb * STRIPS + a) * SEND + COLS_HERE, SLOT_ROWS), :] = found[
+                    i * SLOT_ROWS : (i + 1) * SLOT_ROWS
+                ]
+        return 0
+
+    lax.fori_loop(0, STRIPS, strip, 0)
 
 
 def parts(x):
@@ -203,7 +232,7 @@
             live = slot_id + h * COLS < count_ref[0, t]
             spread = found[2:3] * (1.0 + (dx * dx + dy * dy) / float(LOC * LOC))
             rho = jnp.where(live, 1.0 / spread, 0.0)
-            obs = in_ref[:, COLS_HERE + 2 * t + h].reshape(members, COLS)
+            obs = in_ref[pl.ds(COLS_HERE + 2 * t + h, members, stride=SEND), :]
             mean = jnp.sum(obs, axis=0, keepdims=True) * (1.0 / members)
             values.append(found[1:2] - mean)
             rhos.append(rho)
@@ -241,7 +270,7 @@
         scale = jnp.sqrt((members - 1) / norms[t])
         root = parts(full * scale)
         for c in range(4 * t, 4 * t + 4):
-            x = in_ref[:, c].reshape(members, COLS)
+            x = in_ref[pl.ds(c, members, stride=SEND), :]
             mean = jnp.sum(x, axis=0, keepdims=True) * (1.0 / members)
             x = x - mean
             moved = mean + jnp.sum(x * shift, axis=0, keepdims=True)
@@ -273,42 +302,52 @@
         other = lax.ppermute(lists, "mem", [(i, i ^ (1 << bit)) for i in range(PER_MEM)])
         lists = jnp.concatenate([lists, other], axis=0)
 
-    meta = jnp.concatenate([obs_cell.astype(F32), obs_value, obs_var]).reshape(META, COLS)
-    packed = jnp.concatenate(
-        [prior.reshape(PER_MEM, CELL_ROWS, COLS), jnp.broadcast_to(meta[None], (PER_MEM, META, COLS))], axis=1
-    )
-    whole = lax.all_to_all(packed, "dom", split_axis=0, concat_axis=0, tiled=True)
-    field, near = pl.pallas_call(
+    packed = pl.pallas_call(
+        pack_kernel,
+        compiler_params=PARAMS,
+        name="pack",
+        out_shape=jax.ShapeDtypeStruct((PER_MEM * PACK, COLS), F32),
+        in_specs=[pl.BlockSpec(memory_space=pl.ANY), VMEM, VMEM, VMEM],
+        out_specs=VMEM,
+        scratch_shapes=[pltpu.SemaphoreType.DMA((PER_MEM,))],
+    )(
+        prior.reshape(PER_MEM * CELL_ROWS, COLS),
+        obs_cell.reshape(OBS_CHUNKS, COLS),
+        obs_value.reshape(OBS_CHUNKS, COLS),
+        obs_var.reshape(OBS_CHUNKS, COLS),
+    )
+    whole = lax.all_to_all(
+        packed.reshape(PER_MEM, PACK, COLS), "dom", split_axis=0, concat_axis=0, tiled=True
+    )
+    every = lax.all_to_all(
+        jnp.broadcast_to(lists[None], (STRIPS, PER_MEM * SLOT_ROWS, COLS)),
+        "dom", split_axis=0, concat_axis=0, tiled=True,
+    )
+    field, hx, near = pl.pallas_call(
         forecast_kernel,
         compiler_params=PARAMS,
+        cost_estimate=pl.CostEstimate(flops=30_000_000, bytes_accessed=60_000_000, transcendentals=0),
         name="forecast",
         out_shape=(
-            jax.ShapeDtypeStruct((STRIPS * PACK, COLS), F32),
+            jax.ShapeDtypeStruct((STRIPS * CELL_ROWS, COLS), F32),
+            jax.ShapeDtypeStruct((STRIPS * OBS_CHUNKS, COLS), F32),
             jax.ShapeDtypeStruct((META * 8, COLS), F32),
         ),
-        in_specs=[SMEM, SMEM, SMEM, SMEM, VMEM, pl.BlockSpec(memory_space=pl.ANY)],
-        out_specs=(VMEM, VMEM),
-        scratch_shapes=[
-            pltpu.VMEM((HEIGHT * LEVELS, COLS), F32),
-            pltpu.VMEM((HEIGHT * LEVELS, COLS), F32),
-            pltpu.VMEM((HEIGHT * LEVELS, COLS), F32),
-            pltpu.VMEM((STRIPS * OBS_CHUNKS, COLS), F32),
-        ],
-    )(where, north, east, mix, whole.reshape(STRIPS * PACK, COLS), lists)
-    strip = lax.all_to_all(
-        field.reshape(STRIPS, PACK, COLS), "dom", split_axis=0, concat_axis=0, tiled=True
-    )
+        in_specs=[SMEM, SMEM, SMEM, SMEM, VMEM],
+        out_specs=(VMEM, VMEM, VMEM),
+        scratch_shapes=[pltpu.VMEM((STRIPS * PITCH, COLS), F32)] * 3,
+    )(where, north, east, mix, whole.reshape(STRIPS * PACK, COLS))
     sent = pl.pallas_call(
         select_kernel,
         compiler_params=PARAMS,
         name="select",
-        out_shape=jax.ShapeDtypeStruct((PER_MEM * SEND * PER_MEM, COLS), F32),
-        in_specs=[SMEM, VMEM, VMEM],
+        out_shape=jax.ShapeDtypeStruct((PER_MEM * STRIPS * SEND, COLS), F32),
+        in_specs=[SMEM, VMEM, VMEM, VMEM],
         out_specs=VMEM,
-        scratch_shapes=[pltpu.VMEM((META * PER_MEM, COLS), F32)],
-    )(where, lists, strip.reshape(PER_MEM * PACK, COLS))
+    )(where, every.reshape(STRIPS * PER_MEM * SLOT_ROWS, COLS), hx, field)
     tiles = lax.all_to_all(
-        sent.reshape(PER_MEM, SEND * PER_MEM, COLS), "mem", split_axis=0, concat_axis=0, tiled=True
+        sent.reshape(PER_MEM * STRIPS, SEND // 4, 4, COLS),
+        ("mem", "dom"), split_axis=0, concat_axis=0, tiled=True,
     )
     updated = pl.pallas_call(
         update_kernel,
@@ -318,7 +357,7 @@
         in_specs=[SMEM, SMEM, VMEM, VMEM, VMEM],
         out_specs=VMEM,
         scratch_shapes=[pltpu.VMEM((2, 256, 256), F32), pltpu.VMEM((2, 256, 256), F32)],
-    )(where, tile_count, own, near, tiles.reshape(PER_MEM, SEND, PER_MEM, COLS))
+    )(where, tile_count, own, near, tiles.reshape(PER_MEM * STRIPS * SEND, COLS))
     back = lax.all_to_all(
         updated.reshape(PER_MEM, COLS_HERE * PER_MEM, COLS), "mem", split_axis=0, concat_axis=0, tiled=True
     )

time: 167 us -> 159 us (0.952)
  blocking collectives: 103 us -> 90.2 us
  starting transfers between devices: 19.5 us -> 25.2 us
  local copies, waits for them, and re-layouts: 0.07 us -> 4.19 us
  other arithmetic: 3.86 us -> 0.1 us
    all_to_all x2 -> x1, blocking collectives: 72 us -> 57.2 us  [shards(): lax.all_to_all(sent.reshape(PER_MEM * STRIPS, SEND // 4, 4, COLS), ('mem'...]
    all_to_all x1 -> x2, starting transfers between devices: 7.72 us -> 13.4 us  [the longest x1 7.72 us: shards(): lax.all_to_all(packed.reshape(PER_MEM, PACK, COLS), 'dom', split_axis=0,...]
    concatenate x3 -> x0, other arithmetic: 3.76 us -> none  [the longest x1 2.37 us: shards(): jnp.concatenate([prior.reshape(PER_MEM, CELL_ROWS, COLS), jnp.broadcast_t...]
    unnamed x10 -> x18, local copies, waits for them, and re-layouts: 0.02 us -> 3.31 us
    all_to_all x1, blocking collectives: 31.2 us -> 33 us  [shards(): lax.all_to_all(updated.reshape(PER_MEM, COLS_HERE * PER_MEM, COLS), 'mem'...]
    pallas_call x1 -> x2, Pallas kernels: 18.4 us -> 17.5 us  [the longest x1 14.9 us: shards(): pl.pallas_call(forecast_kernel, compiler_params=PARAMS, cost_estimate=pl....]
  transfers between devices with their start and end apart: 5 -> 6, of which waited for: 5 -> 5; matrix products, arithmetic and copies ran while one was open for 0% -> 0% of each run, Pallas kernels for 0% -> 9%
where the time goes in v2:
time: 159 us
  blocking collectives  90.2 us (57%)
  Pallas kernels  33.4 us (21%)
  starting transfers between devices  25.2 us (16%)
  waiting for transfers between devices  5.78 us (4%)
  local copies, waits for them, and re-layouts  4.19 us (3%)
    all_to_all x1, blocking collectives, shards(): lax.all_to_all(sent.reshape(PER_MEM * STRIPS, SEND // 4, 4, COLS), ('mem'...  57.2 us
    all_to_all x1, blocking collectives, shards(): lax.all_to_all(updated.reshape(PER_MEM, COLS_HERE * PER_MEM, COLS), 'mem'...  33 us
    pallas_call x1, Pallas kernels, shards(): pl.pallas_call(forecast_kernel, compiler_params=PARAMS, cost_estimate=pl....  14.9 us
    ppermute x4, starting transfers between devices, shards(): lax.ppermute(lists, 'mem', [(i, i ^ 1 << bit) for i in range(PER_MEM)])  11.8 us
    pallas_call x1, Pallas kernels, shards(): pl.pallas_call(update_kernel, compiler_params=PARAMS, name='update', out_...  8.01 us
    all_to_all x1, starting transfers between devices, shards(): lax.all_to_all(packed.reshape(PER_MEM, PACK, COLS), 'dom', split_axis=0,...  7.72 us
    all_to_all x1, starting transfers between devices, shards(): lax.all_to_all(jnp.broadcast_to(lists[None], (STRIPS, PER_MEM * SLOT_ROWS...  5.73 us
    pallas_call x1, Pallas kernels, shards(): pl.pallas_call(select_kernel, compiler_params=PARAMS, name='select', out_...  5.28 us
  transfers between devices with their start and end apart: 6, of which 5 were waited for; matrix products, arithmetic and copies ran while one was open for 0% of the time, Pallas kernels for 9%

profile of v2, /device:TPU:1, one launch (start us, length us, event | category | flops | bytes accessed | tf_op | source)
XLA Modules:
  0.0 159.0 jit_solution(13863321946812668382)
XLA Ops:
  0.0 0.0 copy-start
  0.0 1.2 copy-done
  1.2 0.0 copy-start.1
  1.2 0.7 copy-done.1
  1.9 0.0 copy-start.2
  1.9 0.7 copy-done.2
  2.6 0.0 copy-start.3
  2.6 0.7 copy-done.3
  3.3 2.6 %pack.1 = f32[2432,128]{1,0:T(8,128)} custom-call(f32[2048,128]{1,0:T(8,128)S(1)} %bitcast.20, s32[8,128]{1,0:T(8,128)S(1)} %bitcast.21, f32[8,128]{1,0:T(8,128)S(1)} %bitcast.22, f32[8,128]{1,0:T(8,128)S(1)} %bitcast.23), custom_call_target="tpu_custom_call" | custom-call | tf_op jit(solution)/shard_map/pack/pallas_call | solution.py:305
  5.9 0.0 copy-start.8
  5.9 0.0 copy-start.4
  5.9 0.0 copy-start.5
  5.9 0.0 copy-start.6
  5.9 7.7 %all-to-all-start = ((f32[16,152,128]{2,1,0:T(8,128)}), f32[16,152,128]{2,1,0:T(8,128)S(1)}, u32[]{:S(2)}, u32[]{:S(2)}) async-start(f32[16,152,128]{2,1,0:T(8,128)} %bitcast.6), calls=%async_computation | async-start | bytes 2490368 | tf_op jit(solution)/shard_map/all_to_all | solution.py:319
  13.6 0.0 copy-done.8
  13.7 1.0 collective-permute-start
  14.7 0.8 collective-permute-done
  15.5 1.6 %collective-permute-start.1 = (s32[8,128]{1,0:T(8,128)S(1)}, s32[8,128]{1,0:T(8,128)S(1)}, u32[]{:S(2)}, u32[]{:S(2)}) collective-permute-start(s32[8,128]{1,0:T(8,128)S(1)} %pad_add_fusion.2), channel_id=1, source_target_pairs={{0,32},{16,48},{32,0},{48,16},{64,96},{80,112},{96,64},{112,80},{1... | collective-permute-start | bytes 12296 | tf_op jit(solution)/shard_map/ppermute | solution.py:302
  17.2 1.3 collective-permute-done.1
  18.5 3.0 %collective-permute-start.2 = (s32[16,128]{1,0:T(8,128)S(1)}, s32[16,128]{1,0:T(8,128)S(1)}, u32[]{:S(2)}, u32[]{:S(2)}) collective-permute-start(s32[16,128]{1,0:T(8,128)S(1)} %pad_add_fusion.1), channel_id=1, source_target_pairs={{0,64},{16,80},{32,96},{48,112},{64,0},{80,16},{96,32},{112,48},{1... | collective-permute-start | bytes 24584 | tf_op jit(solution)/shard_map/ppermute | solution.py:302
  21.5 1.3 collective-permute-done.2
  22.8 6.1 %collective-permute-start.3 = (s32[32,128]{1,0:T(8,128)S(1)}, s32[32,128]{1,0:T(8,128)S(1)}, u32[]{:S(2)}, u32[]{:S(2)}) collective-permute-start(s32[32,128]{1,0:T(8,128)S(1)} %pad_add_fusion), channel_id=1, source_target_pairs={{0,128},{16,144},{32,160},{48,176},{64,192},{80,208},{96,224},{112... | collective-permute-start | bytes 49160 | tf_op jit(solution)/shard_map/ppermute | solution.py:302
  28.9 1.4 collective-permute-done.3
  30.3 0.9 all-to-all-done
  31.3 0.8 broadcast_in_dim.2
  32.1 5.7 %all-to-all-start.1 = ((s32[16,64,128]{2,1,0:T(8,128)}), s32[16,64,128]{2,1,0:T(8,128)S(1)}, u32[]{:S(2)}, u32[]{:S(2)}) async-start(s32[16,64,128]{2,1,0:T(8,128)} %broadcast_in_dim.2), calls=%async_computation.1 | async-start | bytes 1048576 | tf_op jit(solution)/shard_map/all_to_all | solution.py:322
  37.8 0.1 pad_add_fusion.3.where_ref
  37.9 0.0 copy-done.4
  37.9 0.0 copy-done.5
  37.9 0.0 copy-done.6
  37.9 14.9 %forecast.1 = (f32[2048,128]{1,0:T(8,128)S(1)}, f32[128,128]{1,0:T(8,128)S(1)}, f32[192,128]{1,0:T(8,128)S(1)}) custom-call(s32[2]{0:T(128)S(1)} %pad_add_fusion.3.where_ref, f32[32]{0:T(128)S(1)} %copy-done.4, f32[32]{0:T(128)S(1)} %copy-done.5, f32[32]{0:T(128)S(1)} %copy-done.6, f32[2432,128]{1,0:T(8,128)S(1)} %bitcast.16), custom_call_target="tpu_custom_call" | custom-call | flops 30000000 | bytes 60000000 | tf_op jit(solution)/shard_map/forecast/pallas_call | solution.py:326
  52.9 0.0 all-to-all-done.1
  52.9 5.3 %select.1 = f32[3072,128]{1,0:T(8,128)S(1)} custom-call(s32[2]{0:T(128)S(1)} %pad_add_fusion.3.where_ref, s32[1024,128]{1,0:T(8,128)S(1)} %bitcast.19, f32[128,128]{1,0:T(8,128)S(1)} %get-tuple-element.9.hx_ref, f32[2048,128]{1,0:T(8,128)S(1)} %get-tuple-element.10.in_ref), custom_call_target="tpu_custom_call" | custom-call | tf_op jit(solution)/shard_map/select/pallas_call | solution.py:340
  58.2 0.0 copy-start.7
  58.2 57.2 %all_to_all.20 = f32[256,3,4,128]{3,2,1,0:T(4,128)S(1)} all-to-all(f32[256,3,4,128]{3,2,1,0:T(4,128)S(1)} %bitcast.15), channel_id=1, replica_groups=mesh['mem'=16,'dom'=16] {'mem','dom'}, dimensions={0} | all-to-all | bytes 3145728 | tf_op jit(solution)/shard_map/all_to_all | solution.py:348
  115.3 0.0 copy-done.7
  115.3 8.0 %update.1 = f32[16,8,16,128]{3,2,1,0:T(8,128)S(1)} custom-call(s32[2]{0:T(128)S(1)} %pad_add_fusion.3.where_ref, s32[1,2]{1,0:T(1,128)S(1)} %copy-done.7, s32[4,128]{1,0:T(4,128)S(1)} %reshape.40.list_ref, f32[192,128]{1,0:T(8,128)S(1)} %get-tuple-element.8.meta_ref, f32[3072,128]{1,0:T(8,128)S(1)} %bitcast.14), custom_call_target="tpu_custom_call" | custom-call | tf_op jit(solution)/shard_map/update/pallas_call | solution.py:352
  123.4 33.0 %all_to_all.21 = f32[16,128,128]{2,1,0:T(8,128)S(1)} all-to-all(f32[16,128,128]{2,1,0:T(8,128)S(1)} %bitcast.17), channel_id=1, replica_groups=mesh['mem'=16,'dom'=16] {'mem'}, dimensions={0} | all-to-all | bytes 2097152 | tf_op jit(solution)/shard_map/all_to_all | solution.py:361
  156.4 2.6 %finish.1 = f32[2048,128]{1,0:T(8,128)} custom-call(f32[2048,128]{1,0:T(8,128)S(1)} %bitcast.18), custom_call_target="tpu_custom_call" | custom-call | tf_op jit(solution)/shard_map/finish/pallas_call | solution.py:364
  (5 shorter events, 0.1 us)
Async XLA Ops:
  0.0 1.2 copy-start
  1.2 0.7 copy-start.1
  1.9 0.7 copy-start.2
  2.6 0.7 copy-start.3
  5.9 7.8 %copy-start.8 = (s32[1,2,256]{2,1,0:T(2,128)S(1)}, s32[1,2,256]{2,1,0:T(2,128)}, u32[]{:S(2)}) copy-start(s32[1,2,256]{2,1,0:T(2,128)} %param.16) | copy-start | bytes 6148
  5.9 32.1 %copy-start.4 = (f32[32]{0:T(128)S(1)}, f32[32]{0:T(128)}, u32[]{:S(2)}) copy-start(f32[32]{0:T(128)} %north_ref.1) | copy-start | bytes 388
  5.9 32.0 %copy-start.5 = (f32[32]{0:T(128)S(1)}, f32[32]{0:T(128)}, u32[]{:S(2)}) copy-start(f32[32]{0:T(128)} %east_ref.1) | copy-start | bytes 388
  5.9 32.0 %copy-start.6 = (f32[32]{0:T(128)S(1)}, f32[32]{0:T(128)}, u32[]{:S(2)}) copy-start(f32[32]{0:T(128)} %mix_ref.1) | copy-start | bytes 388
  5.9 25.4 %all-to-all-start = ((f32[16,152,128]{2,1,0:T(8,128)}), f32[16,152,128]{2,1,0:T(8,128)S(1)}, u32[]{:S(2)}, u32[]{:S(2)}) async-start(f32[16,152,128]{2,1,0:T(8,128)} %bitcast.6), calls=%async_computation | async-start | bytes 2490368 | tf_op jit(solution)/shard_map/all_to_all | solution.py:319
  13.7 1.9 %collective-permute-start = (s32[4,128]{1,0:T(4,128)S(1)}, s32[4,128]{1,0:T(4,128)S(1)}, u32[]{:S(2)}, u32[]{:S(2)}) collective-permute-start(s32[4,128]{1,0:T(4,128)S(1)} %reshape.40.list_ref), channel_id=1, source_target_pairs={{0,16},{16,0},{32,48},{48,32},{64,80},{80,64},{96,112},{112,96},{1... | collective-permute-start | bytes 6152 | tf_op jit(solution)/shard_map/ppermute | solution.py:302
  15.5 2.9 %collective-permute-start.1 = (s32[8,128]{1,0:T(8,128)S(1)}, s32[8,128]{1,0:T(8,128)S(1)}, u32[]{:S(2)}, u32[]{:S(2)}) collective-permute-start(s32[8,128]{1,0:T(8,128)S(1)} %pad_add_fusion.2), channel_id=1, source_target_pairs={{0,32},{16,48},{32,0},{48,16},{64,96},{80,112},{96,64},{112,80},{1... | collective-permute-start | bytes 12296 | tf_op jit(solution)/shard_map/ppermute | solution.py:302
  18.5 4.3 %collective-permute-start.2 = (s32[16,128]{1,0:T(8,128)S(1)}, s32[16,128]{1,0:T(8,128)S(1)}, u32[]{:S(2)}, u32[]{:S(2)}) collective-permute-start(s32[16,128]{1,0:T(8,128)S(1)} %pad_add_fusion.1), channel_id=1, source_target_pairs={{0,64},{16,80},{32,96},{48,112},{64,0},{80,16},{96,32},{112,48},{1... | collective-permute-start | bytes 24584 | tf_op jit(solution)/shard_map/ppermute | solution.py:302
  22.8 7.5 %collective-permute-start.3 = (s32[32,128]{1,0:T(8,128)S(1)}, s32[32,128]{1,0:T(8,128)S(1)}, u32[]{:S(2)}, u32[]{:S(2)}) collective-permute-start(s32[32,128]{1,0:T(8,128)S(1)} %pad_add_fusion), channel_id=1, source_target_pairs={{0,128},{16,144},{32,160},{48,176},{64,192},{80,208},{96,224},{112... | collective-permute-start | bytes 49160 | tf_op jit(solution)/shard_map/ppermute | solution.py:302
  32.1 20.8 %all-to-all-start.1 = ((s32[16,64,128]{2,1,0:T(8,128)}), s32[16,64,128]{2,1,0:T(8,128)S(1)}, u32[]{:S(2)}, u32[]{:S(2)}) async-start(s32[16,64,128]{2,1,0:T(8,128)} %broadcast_in_dim.2), calls=%async_computation.1 | async-start | bytes 1048576 | tf_op jit(solution)/shard_map/all_to_all | solution.py:322
  58.2 57.2 %copy-start.7 = (s32[1,2]{1,0:T(1,128)S(1)}, s32[1,2]{1,0:T(1,128)}, u32[]{:S(2)}) copy-start(s32[1,2]{1,0:T(1,128)} %count_ref.1) | copy-start | bytes 28

commit v3 on v2

--- a/solution.py
+++ b/solution.py
@@ -18,7 +18,6 @@
 CELL_ROWS = LEVELS * ROWS
 OBS_CHUNKS = 8
 META = 3 * OBS_CHUNKS
-PACK = CELL_ROWS + META
 SLOT_ROWS = 4
 COLS_HERE = 8
 SEND = COLS_HERE + SLOT_ROWS
@@ -26,6 +25,8 @@
 STRIPS = 16
 HEIGHT = STRIPS * ROWS
 PITCH = CELL_ROWS + 8
+LISTS = PER_MEM * SLOT_ROWS
+AUX = LISTS + META
 
 
 LANES = lax.GatherDimensionNumbers(
@@ -43,35 +44,25 @@
     )
 
 
-def pack_kernel(prior_ref, cell_ref, value_ref, var_ref, out_ref, sems):
-    def copy(m):
-        return pltpu.make_async_copy(
-            prior_ref.at[pl.ds(m * CELL_ROWS, CELL_ROWS), :],
-            out_ref.at[pl.ds(m * PACK, CELL_ROWS), :],
-            sems.at[m],
-        )
-
-    for m in range(PER_MEM):
-        copy(m).start()
-    cell, value, var = cell_ref[...].astype(F32), value_ref[...], var_ref[...]
-    for m in range(PER_MEM):
-        at = m * PACK + CELL_ROWS
-        out_ref[at : at + 8, :] = cell
-        out_ref[at + 8 : at + 16, :] = value
-        out_ref[at + 16 : at + 24, :] = var
-    for m in range(PER_MEM):
-        copy(m).wait()
-
-
-def forecast_kernel(where_ref, north_ref, east_ref, mix_ref, in_ref, out_ref, hx_ref, meta_ref, q_ref, t1_ref, t2_ref):
+def aux_kernel(own_ref, l1_ref, l2_ref, l3_ref, l4_ref, cell_ref, value_ref, var_ref, out_ref):
+    parts_in = [own_ref, l1_ref, l2_ref, l3_ref, l4_ref, cell_ref, value_ref, var_ref]
+    for s in range(STRIPS):
+        at = s * AUX
+        for ref in parts_in:
+            rows = ref.shape[0]
+            out_ref[at : at + rows, :] = ref[...].astype(F32)
+            at += rows
+
+
+def forecast_kernel(north_ref, east_ref, mix_ref, in_ref, q_ref, t1_ref, t2_ref):
     def load(s, _):
         for r in range(ROWS):
             q_ref[pl.ds(pl.multiple_of(s * PITCH + r * LEVELS, 8), LEVELS), :] = in_ref[
-                pl.ds(s * PACK + r, LEVELS, stride=ROWS), :
+                pl.ds(s * CELL_ROWS + r, LEVELS, stride=ROWS), :
             ]
         return 0
 
-    lax.fori_loop(0, STRIPS, load, 0)
+    lax.fori_loop(0, STRIPS, load, 0, unroll=4)
 
     def level_group(g, _):
         sub = lax.broadcasted_iota(jnp.int32, (8, COLS), 0)
@@ -118,10 +109,12 @@
 
     lax.fori_loop(0, LEVELS // 8, level_group, 0)
 
+
+def select_kernel(where_ref, aux_ref, q_ref, out_ref, meta_ref, hx_ref):
     for g in range(2):
         lanes, rows = [], []
         for j in range(OBS_CHUNKS):
-            cell = in_ref[pl.ds(g * 8 * PACK + CELL_ROWS + j, 8, stride=PACK), :].astype(jnp.int32)
+            cell = aux_ref[pl.ds(g * 8 * AUX + LISTS + j, 8, stride=AUX), :].astype(jnp.int32)
             lanes.append(cell & (COLS - 1))
             line = cell >> 7
             rows.append((line & (ROWS - 1)) * LEVELS + (line >> 2))
@@ -138,28 +131,11 @@
         for j in range(OBS_CHUNKS):
             hx_ref[pl.ds(g * 64 + j, 8, stride=OBS_CHUNKS), :] = acc[j]
 
-    def store(s, _):
-        base = pl.multiple_of(s * PITCH, 8)
-        to = pl.multiple_of(s * CELL_ROWS, 8)
-        out_ref[pl.ds(to, CELL_ROWS), :] = q_ref[pl.ds(base, CELL_ROWS), :].T
-        return 0
-
-    lax.fori_loop(0, STRIPS, store, 0)
-
-    meta_ref[...] = jnp.zeros_like(meta_ref)
-    for t in range(3):
-        strip = lax.rem(where_ref[0] + STRIPS - 1 + t, STRIPS)
-        for which in range(3):
-            meta_ref[pl.ds(t * 64 + which, 8, stride=8), :] = in_ref[
-                pl.ds(pl.multiple_of(strip * PACK + CELL_ROWS + which * 8, 8), 8), :
-            ]
-
-
-def select_kernel(where_ref, list_ref, hx_ref, in_ref, out_ref):
     def strip(a, _):
+        columns = q_ref[pl.ds(pl.multiple_of(a * PITCH, 8), CELL_ROWS), :].T
         for kb in range(PER_MEM):
-            out_ref[pl.ds((kb * STRIPS + a) * SEND, COLS_HERE), :] = in_ref[
-                pl.ds(pl.multiple_of(a * CELL_ROWS + kb * COLS_HERE, 8), COLS_HERE), :
+            out_ref[pl.ds((kb * STRIPS + a) * SEND, COLS_HERE), :] = columns[
+                kb * COLS_HERE : (kb + 1) * COLS_HERE
             ]
         sources = []
         for t in range(3):
@@ -167,7 +143,7 @@
             for j in range(OBS_CHUNKS):
                 sources.append(jnp.broadcast_to(hx_ref[pl.ds(near + j, 1), :], (8, COLS)))
         for g in range(PER_MEM // 2):
-            slot = list_ref[pl.ds(pl.multiple_of(a * PER_MEM * SLOT_ROWS + g * 8, 8), 8), :]
+            slot = aux_ref[pl.ds(pl.multiple_of(a * AUX + g * 8, 8), 8), :].astype(jnp.int32)
             lanes = slot & (COLS - 1)
             chunk = slot >> 7
             found = lane_gather(sources[0], lanes)
@@ -181,6 +157,14 @@
         return 0
 
     lax.fori_loop(0, STRIPS, strip, 0)
+
+    meta_ref[...] = jnp.zeros_like(meta_ref)
+    for t in range(3):
+        strip = lax.rem(where_ref[0] + STRIPS - 1 + t, STRIPS)
+        for which in range(3):
+            meta_ref[pl.ds(t * 64 + which, 8, stride=8), :] = aux_ref[
+                pl.ds(pl.multiple_of(strip * AUX + LISTS + which * 8, 8), 8), :
+            ]
 
 
 def parts(x):
@@ -285,7 +269,7 @@
             out_ref[pl.ds(m * CELL_ROWS + r, LEVELS, stride=ROWS), :] = block[r * LEVELS : (r + 1) * LEVELS]
         return 0
 
-    lax.fori_loop(0, PER_MEM, member, 0)
+    lax.fori_loop(0, PER_MEM, member, 0, unroll=4)
 
 
 PARAMS = pltpu.CompilerParams(vmem_limit_bytes=20 * 1024 * 1024)
@@ -297,54 +281,51 @@
     dom, mem = lax.axis_index("dom"), lax.axis_index("mem")
     where = jnp.stack([dom, mem]).astype(jnp.int32)
     own = tile_list.reshape(SLOT_ROWS, COLS)
-    lists = own
+    pieces = [own]
     for bit in range(4):
-        other = lax.ppermute(lists, "mem", [(i, i ^ (1 << bit)) for i in range(PER_MEM)])
-        lists = jnp.concatenate([lists, other], axis=0)
-
-    packed = pl.pallas_call(
-        pack_kernel,
-        compiler_params=PARAMS,
-        name="pack",
-        out_shape=jax.ShapeDtypeStruct((PER_MEM * PACK, COLS), F32),
-        in_specs=[pl.BlockSpec(memory_space=pl.ANY), VMEM, VMEM, VMEM],
+        pairs = [(i, i ^ (1 << bit)) for i in range(PER_MEM)]
+        pieces.append(lax.ppermute(jnp.concatenate(pieces, axis=0), "mem", pairs))
+    whole = lax.all_to_all(
+        prior.reshape(PER_MEM, CELL_ROWS, COLS), "dom", split_axis=0, concat_axis=0, tiled=True
+    )
+    aux = pl.pallas_call(
+        aux_kernel,
+        compiler_params=PARAMS,
+        name="aux",
+        out_shape=jax.ShapeDtypeStruct((STRIPS * AUX, COLS), F32),
+        in_specs=[VMEM] * 8,
         out_specs=VMEM,
-        scratch_shapes=[pltpu.SemaphoreType.DMA((PER_MEM,))],
     )(
-        prior.reshape(PER_MEM * CELL_ROWS, COLS),
+        *pieces,
         obs_cell.reshape(OBS_CHUNKS, COLS),
         obs_value.reshape(OBS_CHUNKS, COLS),
         obs_var.reshape(OBS_CHUNKS, COLS),
     )
-    whole = lax.all_to_all(
-        packed.reshape(PER_MEM, PACK, COLS), "dom", split_axis=0, concat_axis=0, tiled=True
-    )
     every = lax.all_to_all(
-        jnp.broadcast_to(lists[None], (STRIPS, PER_MEM * SLOT_ROWS, COLS)),
-        "dom", split_axis=0, concat_axis=0, tiled=True,
-    )
-    field, hx, near = pl.pallas_call(
+        aux.reshape(STRIPS, AUX, COLS), "dom", split_axis=0, concat_axis=0, tiled=True
+    )
+    levels = pl.pallas_call(
         forecast_kernel,
         compiler_params=PARAMS,
         cost_estimate=pl.CostEstimate(flops=30_000_000, bytes_accessed=60_000_000, transcendentals=0),
         name="forecast",
+        out_shape=jax.ShapeDtypeStruct((STRIPS * PITCH, COLS), F32),
+        in_specs=[SMEM, SMEM, SMEM, VMEM],
+        out_specs=VMEM,
+        scratch_shapes=[pltpu.VMEM((STRIPS * PITCH, COLS), F32)] * 2,
+    )(north, east, mix, whole.reshape(STRIPS * CELL_ROWS, COLS))
+    sent, near = pl.pallas_call(
+        select_kernel,
+        compiler_params=PARAMS,
+        name="select",
         out_shape=(
-            jax.ShapeDtypeStruct((STRIPS * CELL_ROWS, COLS), F32),
-            jax.ShapeDtypeStruct((STRIPS * OBS_CHUNKS, COLS), F32),
+            jax.ShapeDtypeStruct((PER_MEM * STRIPS * SEND, COLS), F32),
             jax.ShapeDtypeStruct((META * 8, COLS), F32),
         ),
-        in_specs=[SMEM, SMEM, SMEM, SMEM, VMEM],
-        out_specs=(VMEM, VMEM, VMEM),
-        scratch_shapes=[pltpu.VMEM((STRIPS * PITCH, COLS), F32)] * 3,
-    )(where, north, east, mix, whole.reshape(STRIPS * PACK, COLS))
-    sent = pl.pallas_call(
-        select_kernel,
-        compiler_params=PARAMS,
-        name="select",
-        out_shape=jax.ShapeDtypeStruct((PER_MEM * STRIPS * SEND, COLS), F32),
-        in_specs=[SMEM, VMEM, VMEM, VMEM],
-        out_specs=VMEM,
-    )(where, every.reshape(STRIPS * PER_MEM * SLOT_ROWS, COLS), hx, field)
+        in_specs=[SMEM, VMEM, VMEM],
+        out_specs=(VMEM, VMEM),
+        scratch_shapes=[pltpu.VMEM((STRIPS * OBS_CHUNKS, COLS), F32)],
+    )(where, every.reshape(STRIPS * AUX, COLS), levels)
     tiles = lax.all_to_all(
         sent.reshape(PER_MEM * STRIPS, SEND // 4, 4, COLS),
         ("mem", "dom"), split_axis=0, concat_axis=0, tiled=True,

time: 159 us -> 152 us (0.956)
  local copies, waits for them, and re-layouts: 4.19 us -> 0.05 us
  Pallas kernels: 33.4 us -> 29.5 us
  blocking collectives: 90.2 us -> 86.8 us
  waiting for transfers between devices: 5.78 us -> 9.03 us
    pallas_call x1, Pallas kernels: 14.9 us -> 6.44 us  [shards(): pl.pallas_call(forecast_kernel, compiler_params=PARAMS, cost_estimate=pl....]
    pallas_call x1, Pallas kernels: 5.28 us -> 12.6 us  [shards(): pl.pallas_call(select_kernel, compiler_params=PARAMS, name='select', out_...]
    all_to_all x1, blocking collectives: 57.2 us -> 53.8 us  [shards(): lax.all_to_all(sent.reshape(PER_MEM * STRIPS, SEND // 4, 4, COLS), ('mem'...]
    unnamed x18 -> x16, local copies, waits for them, and re-layouts: 3.31 us -> 0.04 us
    all_to_all x2, waiting for transfers between devices: 0.92 us -> 4.17 us  [the longest x1 4.16 us: shards(): lax.all_to_all(aux.reshape(STRIPS, AUX, COLS), 'dom', split_axis=0, conca...]
    pallas_call x1, Pallas kernels: 2.57 us -> 0.91 us  [shards(): pl.pallas_call(aux_kernel, compiler_params=PARAMS, name='aux', out_shape=...]
  transfers between devices with their start and end apart: 6 -> 6, of which waited for: 5 -> 5; matrix products, arithmetic and copies ran while one was open for 0% -> 0% of each run, Pallas kernels for 9% -> 5%
where the time goes in v3:
time: 152 us
  blocking collectives  86.8 us (57%)
  Pallas kernels  29.5 us (19%)
  starting transfers between devices  26.1 us (17%)
  waiting for transfers between devices  9.03 us (6%)
    all_to_all x1, blocking collectives, shards(): lax.all_to_all(sent.reshape(PER_MEM * STRIPS, SEND // 4, 4, COLS), ('mem'...  53.8 us
    all_to_all x1, blocking collectives, shards(): lax.all_to_all(updated.reshape(PER_MEM, COLS_HERE * PER_MEM, COLS), 'mem'...  33 us
    pallas_call x1, Pallas kernels, shards(): pl.pallas_call(select_kernel, compiler_params=PARAMS, name='select', out_...  12.6 us
    ppermute x4, starting transfers between devices, shards(): pieces.append(lax.ppermute(jnp.concatenate(pieces, axis=0), 'mem', pairs))  11.8 us
    pallas_call x1, Pallas kernels, shards(): pl.pallas_call(update_kernel, compiler_params=PARAMS, name='update', out_...  8.01 us
    all_to_all x1, starting transfers between devices, shards(): lax.all_to_all(prior.reshape(PER_MEM, CELL_ROWS, COLS), 'dom', split_axis...  7.72 us
    all_to_all x1, starting transfers between devices, shards(): lax.all_to_all(aux.reshape(STRIPS, AUX, COLS), 'dom', split_axis=0, conca...  6.64 us
    pallas_call x1, Pallas kernels, shards(): pl.pallas_call(forecast_kernel, compiler_params=PARAMS, cost_estimate=pl....  6.44 us
  transfers between devices with their start and end apart: 6, of which 5 were waited for; matrix products, arithmetic and copies ran while one was open for 0% of the time, Pallas kernels for 5%

profile of v3, /device:TPU:1, one launch (start us, length us, event | category | flops | bytes accessed | tf_op | source)
XLA Modules:
  0.0 151.7 jit_solution(15855674623401591624)
XLA Ops:
  0.0 0.0 copy-start.7
  0.0 0.0 copy-start.2
  0.0 0.0 copy-start.1
  0.0 0.0 copy-start
  0.0 7.7 %all-to-all-start.1 = ((f32[16,128,128]{2,1,0:T(8,128)}), f32[16,128,128]{2,1,0:T(8,128)S(1)}, u32[]{:S(2)}, u32[]{:S(2)}) async-start(f32[16,128,128]{2,1,0:T(8,128)} %bitcast.23), calls=%async_computation.1 | async-start | bytes 2097152 | tf_op jit(solution)/shard_map/all_to_all | solution.py:288
  7.7 0.0 copy-done.7
  7.8 0.0 copy-start.3
  7.8 0.0 copy-start.4
  7.8 0.0 copy-start.5
  7.8 1.0 collective-permute-start
  8.8 0.8 collective-permute-done.l1_ref
  9.7 1.6 %collective-permute-start.1 = (s32[8,128]{1,0:T(8,128)S(1)}, s32[8,128]{1,0:T(8,128)S(1)}, u32[]{:S(2)}, u32[]{:S(2)}) collective-permute-start(s32[8,128]{1,0:T(8,128)S(1)} %pad_add_fusion.2), channel_id=1, source_target_pairs={{0,32},{16,48},{32,0},{48,16},{64,96},{80,112},{96,64},{112,80},{1... | collective-permute-start | bytes 12296 | tf_op jit(solution)/shard_map/ppermute | solution.py:287
  11.3 1.3 collective-permute-done.1.l2_ref
  12.6 3.0 %collective-permute-start.2 = (s32[16,128]{1,0:T(8,128)S(1)}, s32[16,128]{1,0:T(8,128)S(1)}, u32[]{:S(2)}, u32[]{:S(2)}) collective-permute-start(s32[16,128]{1,0:T(8,128)S(1)} %pad_add_fusion.1), channel_id=1, source_target_pairs={{0,64},{16,80},{32,96},{48,112},{64,0},{80,16},{96,32},{112,48},{1... | collective-permute-start | bytes 24584 | tf_op jit(solution)/shard_map/ppermute | solution.py:287
  15.6 1.3 collective-permute-done.2.l3_ref
  16.9 6.1 %collective-permute-start.3 = (s32[32,128]{1,0:T(8,128)S(1)}, s32[32,128]{1,0:T(8,128)S(1)}, u32[]{:S(2)}, u32[]{:S(2)}) collective-permute-start(s32[32,128]{1,0:T(8,128)S(1)} %pad_add_fusion), channel_id=1, source_target_pairs={{0,128},{16,144},{32,160},{48,176},{64,192},{80,208},{96,224},{112... | collective-permute-start | bytes 49160 | tf_op jit(solution)/shard_map/ppermute | solution.py:287
  23.1 1.4 collective-permute-done.3.l4_ref
  24.5 0.0 copy-done.2
  24.5 0.0 copy-done.1
  24.5 0.0 copy-done
  24.5 0.9 aux.1
  25.4 0.0 all-to-all-done.1
  25.4 6.6 %all-to-all-start = ((f32[16,88,128]{2,1,0:T(8,128)}), f32[16,88,128]{2,1,0:T(8,128)S(1)}, u32[]{:S(2)}, u32[]{:S(2)}) async-start(f32[16,88,128]{2,1,0:T(8,128)} %bitcast.5), calls=%async_computation | async-start | bytes 1441792 | tf_op jit(solution)/shard_map/all_to_all | solution.py:304
  32.1 0.1 pad_add_fusion.3.where_ref
  32.1 0.0 copy-done.3
  32.1 0.0 copy-done.4
  32.1 0.0 copy-done.5
  32.1 6.4 %forecast.1.q_ref = f32[2176,128]{1,0:T(8,128)S(1)} custom-call(f32[32]{0:T(128)S(1)} %copy-done.3, f32[32]{0:T(128)S(1)} %copy-done.4, f32[32]{0:T(128)S(1)} %copy-done.5, f32[2048,128]{1,0:T(8,128)S(1)} %bitcast.15), custom_call_target="tpu_custom_call" | custom-call | flops 30000000 | bytes 60000000 | tf_op jit(solution)/shard_map/forecast/pallas_call | solution.py:307
  38.6 4.2 %all-to-all-done = f32[16,88,128]{2,1,0:T(8,128)S(1)} async-done(((f32[16,88,128]{2,1,0:T(8,128)}), f32[16,88,128]{2,1,0:T(8,128)S(1)}, u32[]{:S(2)}, u32[]{:S(2)}) %all-to-all-start) | async-done | bytes 720928 | tf_op jit(solution)/shard_map/all_to_all | solution.py:304
  42.8 12.6 %select.1 = (f32[3072,128]{1,0:T(8,128)S(1)}, f32[192,128]{1,0:T(8,128)S(1)}) custom-call(s32[2]{0:T(128)S(1)} %pad_add_fusion.3.where_ref, f32[1408,128]{1,0:T(8,128)S(1)} %bitcast.18, f32[2176,128]{1,0:T(8,128)S(1)} %forecast.1.q_ref), custom_call_target="tpu_custom_call" | custom-call | tf_op jit(solution)/shard_map/select/pallas_call | solution.py:317
  55.3 0.0 copy-start.6
  55.3 53.8 %all_to_all.20 = f32[256,3,4,128]{3,2,1,0:T(4,128)S(1)} all-to-all(f32[256,3,4,128]{3,2,1,0:T(4,128)S(1)} %bitcast.19), channel_id=1, replica_groups=mesh['mem'=16,'dom'=16] {'mem','dom'}, dimensions={0} | all-to-all | bytes 3145728 | tf_op jit(solution)/shard_map/all_to_all | solution.py:329
  109.2 0.0 copy-done.6
  109.2 8.0 %update.1 = f32[16,8,16,128]{3,2,1,0:T(8,128)S(1)} custom-call(s32[2]{0:T(128)S(1)} %pad_add_fusion.3.where_ref, s32[1,2]{1,0:T(1,128)S(1)} %copy-done.6, s32[4,128]{1,0:T(4,128)S(1)} %reshape.39.own_ref.list_ref, f32[192,128]{1,0:T(8,128)S(1)} %get-tuple-element.7.meta_ref, f32[3072,128]{1,0:T(8,128)S(1)} %bitcast.14), custom_call_target="tpu_custom_call" | custom-call | tf_op jit(solution)/shard_map/update/pallas_call | solution.py:333
  117.2 33.0 %all_to_all.21 = f32[16,128,128]{2,1,0:T(8,128)S(1)} all-to-all(f32[16,128,128]{2,1,0:T(8,128)S(1)} %bitcast.16), channel_id=1, replica_groups=mesh['mem'=16,'dom'=16] {'mem'}, dimensions={0} | all-to-all | bytes 2097152 | tf_op jit(solution)/shard_map/all_to_all | solution.py:342
  150.2 1.5 %finish.1 = f32[2048,128]{1,0:T(8,128)} custom-call(f32[2048,128]{1,0:T(8,128)S(1)} %bitcast.17), custom_call_target="tpu_custom_call" | custom-call | tf_op jit(solution)/shard_map/finish/pallas_call | solution.py:345
  (4 shorter events, 0.0 us)
Async XLA Ops:
  0.0 7.7 %copy-start.7 = (s32[1,2,256]{2,1,0:T(2,128)S(1)}, s32[1,2,256]{2,1,0:T(2,128)}, u32[]{:S(2)}) copy-start(s32[1,2,256]{2,1,0:T(2,128)} %param.16) | copy-start | bytes 6148
  0.0 24.5 %copy-start.2 = (f32[1024]{0:T(1024)S(1)}, f32[1024]{0:T(1024)}, u32[]{:S(2)}) copy-start(f32[1024]{0:T(1024)} %param.15) | copy-start | bytes 12292
  0.0 24.5 %copy-start.1 = (f32[1024]{0:T(1024)S(1)}, f32[1024]{0:T(1024)}, u32[]{:S(2)}) copy-start(f32[1024]{0:T(1024)} %param.14) | copy-start | bytes 12292
  0.0 24.5 %copy-start = (s32[1024]{0:T(1024)S(1)}, s32[1024]{0:T(1024)}, u32[]{:S(2)}) copy-start(s32[1024]{0:T(1024)} %param.13) | copy-start | bytes 12292
  0.0 25.4 %all-to-all-start.1 = ((f32[16,128,128]{2,1,0:T(8,128)}), f32[16,128,128]{2,1,0:T(8,128)S(1)}, u32[]{:S(2)}, u32[]{:S(2)}) async-start(f32[16,128,128]{2,1,0:T(8,128)} %bitcast.23), calls=%async_computation.1 | async-start | bytes 2097152 | tf_op jit(solution)/shard_map/all_to_all | solution.py:288
  7.8 24.4 %copy-start.3 = (f32[32]{0:T(128)S(1)}, f32[32]{0:T(128)}, u32[]{:S(2)}) copy-start(f32[32]{0:T(128)} %north_ref.1) | copy-start | bytes 388
  7.8 24.4 %copy-start.4 = (f32[32]{0:T(128)S(1)}, f32[32]{0:T(128)}, u32[]{:S(2)}) copy-start(f32[32]{0:T(128)} %east_ref.1) | copy-start | bytes 388
  7.8 24.4 %copy-start.5 = (f32[32]{0:T(128)S(1)}, f32[32]{0:T(128)}, u32[]{:S(2)}) copy-start(f32[32]{0:T(128)} %mix_ref.1) | copy-start | bytes 388
  7.8 1.9 %collective-permute-start = (s32[4,128]{1,0:T(4,128)S(1)}, s32[4,128]{1,0:T(4,128)S(1)}, u32[]{:S(2)}, u32[]{:S(2)}) collective-permute-start(s32[4,128]{1,0:T(4,128)S(1)} %reshape.39.own_ref.list_ref), channel_id=1, source_target_pairs={{0,16},{16,0},{32,48},{48,32},{64,80},{80,64},{96,112},{112,96},{1... | collective-permute-start | bytes 6152 | tf_op jit(solution)/shard_map/ppermute | solution.py:287
  9.7 2.9 %collective-permute-start.1 = (s32[8,128]{1,0:T(8,128)S(1)}, s32[8,128]{1,0:T(8,128)S(1)}, u32[]{:S(2)}, u32[]{:S(2)}) collective-permute-start(s32[8,128]{1,0:T(8,128)S(1)} %pad_add_fusion.2), channel_id=1, source_target_pairs={{0,32},{16,48},{32,0},{48,16},{64,96},{80,112},{96,64},{112,80},{1... | collective-permute-start | bytes 12296 | tf_op jit(solution)/shard_map/ppermute | solution.py:287
  12.6 4.3 %collective-permute-start.2 = (s32[16,128]{1,0:T(8,128)S(1)}, s32[16,128]{1,0:T(8,128)S(1)}, u32[]{:S(2)}, u32[]{:S(2)}) collective-permute-start(s32[16,128]{1,0:T(8,128)S(1)} %pad_add_fusion.1), channel_id=1, source_target_pairs={{0,64},{16,80},{32,96},{48,112},{64,0},{80,16},{96,32},{112,48},{1... | collective-permute-start | bytes 24584 | tf_op jit(solution)/shard_map/ppermute | solution.py:287
  16.9 7.5 %collective-permute-start.3 = (s32[32,128]{1,0:T(8,128)S(1)}, s32[32,128]{1,0:T(8,128)S(1)}, u32[]{:S(2)}, u32[]{:S(2)}) collective-permute-start(s32[32,128]{1,0:T(8,128)S(1)} %pad_add_fusion), channel_id=1, source_target_pairs={{0,128},{16,144},{32,160},{48,176},{64,192},{80,208},{96,224},{112... | collective-permute-start | bytes 49160 | tf_op jit(solution)/shard_map/ppermute | solution.py:287
  25.4 17.4 %all-to-all-start = ((f32[16,88,128]{2,1,0:T(8,128)}), f32[16,88,128]{2,1,0:T(8,128)S(1)}, u32[]{:S(2)}, u32[]{:S(2)}) async-start(f32[16,88,128]{2,1,0:T(8,128)} %bitcast.5), calls=%async_computation | async-start | bytes 1441792 | tf_op jit(solution)/shard_map/all_to_all | solution.py:304
  55.3 53.9 %copy-start.6 = (s32[1,2]{1,0:T(1,128)S(1)}, s32[1,2]{1,0:T(1,128)}, u32[]{:S(2)}) copy-start(s32[1,2]{1,0:T(1,128)} %count_ref.1) | copy-start | bytes 28

commit v4 on v3

--- a/solution.py
+++ b/solution.py
@@ -25,6 +25,7 @@
 STRIPS = 16
 HEIGHT = STRIPS * ROWS
 PITCH = CELL_ROWS + 8
+FIELD = STRIPS * PITCH
 LISTS = PER_MEM * SLOT_ROWS
 AUX = LISTS + META
 
@@ -42,6 +43,9 @@
     return lax.gather(
         values, lanes[..., None], LANES, (1, 1), mode=lax.GatherScatterMode.PROMISE_IN_BOUNDS
     )
+
+
+ARRIVAL = (0, 1, 7, 3, 4, 2, 5, 6)
 
 
 def aux_kernel(own_ref, l1_ref, l2_ref, l3_ref, l4_ref, cell_ref, value_ref, var_ref, out_ref):
@@ -109,33 +113,35 @@
 
     lax.fori_loop(0, LEVELS // 8, level_group, 0)
 
+    def turn(s, _):
+        q_ref[pl.ds(pl.multiple_of(FIELD + s * CELL_ROWS, 8), CELL_ROWS), :] = q_ref[
+            pl.ds(pl.multiple_of(s * PITCH, 8), CELL_ROWS), :
+        ].T
+        return 0
+
+    lax.fori_loop(0, STRIPS, turn, 0, unroll=4)
+
 
 def select_kernel(where_ref, aux_ref, q_ref, out_ref, meta_ref, hx_ref):
-    for g in range(2):
-        lanes, rows = [], []
-        for j in range(OBS_CHUNKS):
-            cell = aux_ref[pl.ds(g * 8 * AUX + LISTS + j, 8, stride=AUX), :].astype(jnp.int32)
-            lanes.append(cell & (COLS - 1))
-            line = cell >> 7
-            rows.append((line & (ROWS - 1)) * LEVELS + (line >> 2))
-
-        def pick(p, acc):
+    def extract(i, _):
+        g, j = i // OBS_CHUNKS, i % OBS_CHUNKS
+        cell = aux_ref[pl.ds(g * 8 * AUX + LISTS + j, 8, stride=AUX), :].astype(jnp.int32)
+        lanes = cell & (COLS - 1)
+        line = cell >> 7
+        rows = (line & (ROWS - 1)) * LEVELS + (line >> 2)
+        sums = [jnp.zeros((8, COLS), F32) for _ in range(4)]
+        for p in range(CELL_ROWS):
             src = q_ref[pl.ds(p + g * 8 * PITCH, 8, stride=PITCH), :]
-            return tuple(
-                jnp.where(rows[j] == p, lane_gather(src, lanes[j]), acc[j]) for j in range(OBS_CHUNKS)
-            )
-
-        acc = lax.fori_loop(
-            0, CELL_ROWS, pick, tuple(jnp.zeros((8, COLS), F32) for _ in range(OBS_CHUNKS)), unroll=16
-        )
-        for j in range(OBS_CHUNKS):
-            hx_ref[pl.ds(g * 64 + j, 8, stride=OBS_CHUNKS), :] = acc[j]
+            sums[p % 4] = jnp.where(rows == p, lane_gather(src, lanes), sums[p % 4])
+        hx_ref[pl.ds(g * 64 + j, 8, stride=OBS_CHUNKS), :] = (sums[0] + sums[1]) + (sums[2] + sums[3])
+        return 0
+
+    lax.fori_loop(0, 2 * OBS_CHUNKS, extract, 0)
 
     def strip(a, _):
-        columns = q_ref[pl.ds(pl.multiple_of(a * PITCH, 8), CELL_ROWS), :].T
         for kb in range(PER_MEM):
-            out_ref[pl.ds((kb * STRIPS + a) * SEND, COLS_HERE), :] = columns[
-                kb * COLS_HERE : (kb + 1) * COLS_HERE
+            out_ref[pl.ds((kb * STRIPS + a) * SEND, COLS_HERE), :] = q_ref[
+                pl.ds(pl.multiple_of(FIELD + a * CELL_ROWS + kb * COLS_HERE, 8), COLS_HERE), :
             ]
         sources = []
         for t in range(3):
@@ -150,7 +156,7 @@
             for j in range(1, META):
                 found = jnp.where(chunk == j, lane_gather(sources[j], lanes), found)
             for i in range(2):
-                kb = lax.bitwise_xor(where_ref[1], 2 * g + i)
+                kb = ((where_ref[1] >> 1) + ARRIVAL[g] & 7) * 2 + ((where_ref[1] & 1) ^ i)
                 out_ref[pl.ds((kb * STRIPS + a) * SEND + COLS_HERE, SLOT_ROWS), :] = found[
                     i * SLOT_ROWS : (i + 1) * SLOT_ROWS
                 ]
@@ -236,19 +242,24 @@
         it_ref[t] = product(parts(it), parts(factor))
 
     def iteration(_, c):
+        roots = [parts(root_ref[t]) for t in range(2)]
+        its = [parts(it_ref[t]) for t in range(2)]
+        factors = [parts(plus_identity(-0.5 * product(roots[t], its[t]), 1.5)) for t in range(2)]
         for t in range(2):
-            root, it = parts(root_ref[t]), parts(it_ref[t])
-            factor = parts(plus_identity(-0.5 * product(root, it), 1.5))
-            it_ref[t] = product(it, factor)
-            root_ref[t] = product(factor, root)
+            both = [jnp.concatenate([its[t][i], roots[t][i]], axis=0) for i in range(2)]
+            both = product(both, factors[t])
+            it_ref[t] = both[:members]
+            root_ref[t] = both[members:]
         return c
 
     lax.fori_loop(0, NS_ITERS - 2, iteration, 0)
 
+    roots = [parts(root_ref[t]) for t in range(2)]
+    its = [parts(it_ref[t]) for t in range(2)]
+    factors = [parts(plus_identity(-0.5 * product(roots[t], its[t]), 1.5)) for t in range(2)]
+    fulls = [product(factors[t], roots[t]) for t in range(2)]
     for t in range(2):
-        root, it = parts(root_ref[t]), parts(it_ref[t])
-        factor = parts(plus_identity(-0.5 * product(root, it), 1.5))
-        full = product(factor, root)
+        full = fulls[t]
         inner = jnp.sum(full * drives[t], axis=0, keepdims=True)
         shift = jnp.sum(full * inner, axis=1, keepdims=True) / norms[t]
         scale = jnp.sqrt((members - 1) / norms[t])
@@ -281,10 +292,18 @@
     dom, mem = lax.axis_index("dom"), lax.axis_index("mem")
     where = jnp.stack([dom, mem]).astype(jnp.int32)
     own = tile_list.reshape(SLOT_ROWS, COLS)
-    pieces = [own]
-    for bit in range(4):
-        pairs = [(i, i ^ (1 << bit)) for i in range(PER_MEM)]
-        pieces.append(lax.ppermute(jnp.concatenate(pieces, axis=0), "mem", pairs))
+    def shifted(x, by):
+        return lax.ppermute(x, "mem", [((i + by) % PER_MEM, i) for i in range(PER_MEM)])
+
+    chip = jnp.concatenate(
+        [own, lax.ppermute(own, "mem", [(i, i ^ 1) for i in range(PER_MEM)])], axis=0
+    )
+    ahead, behind = shifted(chip, 2), shifted(chip, -2)
+    pieces = [
+        chip, ahead, behind,
+        shifted(jnp.concatenate([chip, ahead, behind], axis=0), 6),
+        shifted(jnp.concatenate([chip, ahead], axis=0), -6),
+    ]
     whole = lax.all_to_all(
         prior.reshape(PER_MEM, CELL_ROWS, COLS), "dom", split_axis=0, concat_axis=0, tiled=True
     )
@@ -309,7 +328,7 @@
         compiler_params=PARAMS,
         cost_estimate=pl.CostEstimate(flops=30_000_000, bytes_accessed=60_000_000, transcendentals=0),
         name="forecast",
-        out_shape=jax.ShapeDtypeStruct((STRIPS * PITCH, COLS), F32),
+        out_shape=jax.ShapeDtypeStruct((FIELD + STRIPS * CELL_ROWS, COLS), F32),
         in_specs=[SMEM, SMEM, SMEM, VMEM],
         out_specs=VMEM,
         scratch_shapes=[pltpu.VMEM((STRIPS * PITCH, COLS), F32)] * 2,

time: 152 us -> 147 us (0.967)
  Pallas kernels: 29.5 us -> 26.6 us
    pallas_call x1, Pallas kernels: 12.6 us -> 9.27 us  [shards(): pl.pallas_call(select_kernel, compiler_params=PARAMS, name='select', out_...]
    ppermute x4 -> x5, waiting for transfers between devices: 4.86 us -> 6.51 us  [the longest x4 5.68 us: shifted(): lax.ppermute(x, 'mem', [((i + by) % PER_MEM, i) for i in range(PER_MEM)])]
    pallas_call x1, Pallas kernels: 6.44 us -> 8.03 us  [shards(): pl.pallas_call(forecast_kernel, compiler_params=PARAMS, cost_estimate=pl....]
    all_to_all x1, waiting for transfers between devices: 4.16 us -> 2.64 us  [shards(): lax.all_to_all(aux.reshape(STRIPS, AUX, COLS), 'dom', split_axis=0, conca...]
    ppermute x4 -> x5, starting transfers between devices: 11.8 us -> 11.1 us  [the longest x4 10 us: shifted(): lax.ppermute(x, 'mem', [((i + by) % PER_MEM, i) for i in range(PER_MEM)])]
  transfers between devices with their start and end apart: 6 -> 7, of which waited for: 5 -> 4; matrix products, arithmetic and copies ran while one was open for 0% -> 0% of each run, Pallas kernels for 5% -> 6%
where the time goes in v4:
time: 147 us
  blocking collectives  85.4 us (58%)
  Pallas kernels  26.6 us (18%)
  starting transfers between devices  25.5 us (17%)
  waiting for transfers between devices  9.14 us (6%)
    all_to_all x1, blocking collectives, shards(): lax.all_to_all(sent.reshape(PER_MEM * STRIPS, SEND // 4, 4, COLS), ('mem'...  52.4 us
    all_to_all x1, blocking collectives, shards(): lax.all_to_all(updated.reshape(PER_MEM, COLS_HERE * PER_MEM, COLS), 'mem'...  33 us
    ppermute x4, starting transfers between devices, shifted(): lax.ppermute(x, 'mem', [((i + by) % PER_MEM, i) for i in range(PER_MEM)])  10 us
    pallas_call x1, Pallas kernels, shards(): pl.pallas_call(select_kernel, compiler_params=PARAMS, name='select', out_...  9.27 us
    pallas_call x1, Pallas kernels, shards(): pl.pallas_call(forecast_kernel, compiler_params=PARAMS, cost_estimate=pl....  8.03 us
    all_to_all x1, starting transfers between devices, shards(): lax.all_to_all(prior.reshape(PER_MEM, CELL_ROWS, COLS), 'dom', split_axis...  7.72 us
    pallas_call x1, Pallas kernels, shards(): pl.pallas_call(update_kernel, compiler_params=PARAMS, name='update', out_...  6.85 us
    all_to_all x1, starting transfers between devices, shards(): lax.all_to_all(aux.reshape(STRIPS, AUX, COLS), 'dom', split_axis=0, conca...  6.73 us
  transfers between devices with their start and end apart: 7, of which 4 were waited for; matrix products, arithmetic and copies ran while one was open for 0% of the time, Pallas kernels for 6%

profile of v4, /device:TPU:1, one launch (start us, length us, event | category | flops | bytes accessed | tf_op | source)
XLA Modules:
  0.0 146.9 jit_solution(6888002999745923798)
XLA Ops:
  0.0 0.0 copy-start.7
  0.0 0.0 copy-start.2
  0.0 0.0 copy-start.1
  0.0 0.0 copy-start
  0.0 7.7 %all-to-all-start.1 = ((f32[16,128,128]{2,1,0:T(8,128)}), f32[16,128,128]{2,1,0:T(8,128)S(1)}, u32[]{:S(2)}, u32[]{:S(2)}) async-start(f32[16,128,128]{2,1,0:T(8,128)} %bitcast.22), calls=%async_computation.1 | async-start | bytes 2097152 | tf_op jit(solution)/shard_map/all_to_all | solution.py:307
  7.7 0.0 copy-done.7
  7.8 0.0 copy-start.3
  7.8 0.0 copy-start.4
  7.8 0.0 copy-start.5
  7.8 1.0 collective-permute-start
  8.8 0.8 collective-permute-done
  9.7 1.6 %collective-permute-start.2 = (s32[8,128]{1,0:T(8,128)S(1)}, s32[8,128]{1,0:T(8,128)S(1)}, u32[]{:S(2)}, u32[]{:S(2)}) collective-permute-start(s32[8,128]{1,0:T(8,128)S(1)} %pad_add_fusion.2.own_ref), channel_id=1, source_target_pairs={{224,0},{240,16},{0,32},{16,48},{32,64},{48,80},{64,96},{80,112},{... | collective-permute-start | bytes 12296 | tf_op jit(solution)/shard_map/ppermute | solution.py:296
  11.3 4.0 %collective-permute-start.1 = (s32[8,128]{1,0:T(8,128)S(1)}, s32[8,128]{1,0:T(8,128)S(1)}, u32[]{:S(2)}, u32[]{:S(2)}) collective-permute-start(s32[8,128]{1,0:T(8,128)S(1)} %pad_add_fusion.2.own_ref), channel_id=1, source_target_pairs={{32,0},{48,16},{64,32},{80,48},{96,64},{112,80},{128,96},{144,112}... | collective-permute-start | bytes 12296 | tf_op jit(solution)/shard_map/ppermute | solution.py:296
  15.3 1.2 collective-permute-done.2.l2_ref
  16.5 0.0 collective-permute-done.1.l1_ref
  16.6 3.1 %collective-permute-start.3 = (s32[24,128]{1,0:T(8,128)S(1)}, s32[24,128]{1,0:T(8,128)S(1)}, u32[]{:S(2)}, u32[]{:S(2)}) collective-permute-start(s32[24,128]{1,0:T(8,128)S(1)} %pad_add_fusion), channel_id=1, source_target_pairs={{96,0},{112,16},{128,32},{144,48},{160,64},{176,80},{192,96},{208,... | collective-permute-start | bytes 36872 | tf_op jit(solution)/shard_map/ppermute | solution.py:296
  19.6 1.3 collective-permute-start.4
  20.9 4.5 %collective-permute-done.4.l4_ref = s32[16,128]{1,0:T(8,128)S(1)} collective-permute-done((s32[16,128]{1,0:T(8,128)S(1)}, s32[16,128]{1,0:T(8,128)S(1)}, u32[]{:S(2)}, u32[]{:S(2)}) %collective-permute-start.4) | collective-permute-done | bytes 8224 | tf_op jit(solution)/shard_map/ppermute | solution.py:296
  25.4 0.0 collective-permute-done.3.l3_ref
  25.4 0.0 copy-done.2
  25.4 0.0 copy-done.1
  25.4 0.0 copy-done
  25.4 0.9 aux.1
  26.3 0.0 all-to-all-done.1
  26.3 6.7 %all-to-all-start = ((f32[16,88,128]{2,1,0:T(8,128)}), f32[16,88,128]{2,1,0:T(8,128)}, u32[]{:S(2)}, u32[]{:S(2)}) async-start(f32[16,88,128]{2,1,0:T(8,128)} %bitcast.5), calls=%async_computation | async-start | bytes 1441792 | tf_op jit(solution)/shard_map/all_to_all | solution.py:323
  33.1 0.1 pad_add_fusion.3.where_ref
  33.2 0.0 copy-done.3
  33.2 0.0 copy-done.4
  33.2 0.0 copy-done.5
  33.2 8.0 %forecast.1.q_ref = f32[4224,128]{1,0:T(8,128)S(1)} custom-call(f32[32]{0:T(128)S(1)} %copy-done.3, f32[32]{0:T(128)S(1)} %copy-done.4, f32[32]{0:T(128)S(1)} %copy-done.5, f32[2048,128]{1,0:T(8,128)S(1)} %bitcast.15), custom_call_target="tpu_custom_call" | custom-call | flops 30000000 | bytes 60000000 | tf_op jit(solution)/shard_map/forecast/pallas_call | solution.py:326
  41.2 2.6 %all-to-all-done = f32[16,88,128]{2,1,0:T(8,128)} async-done(((f32[16,88,128]{2,1,0:T(8,128)}), f32[16,88,128]{2,1,0:T(8,128)}, u32[]{:S(2)}, u32[]{:S(2)}) %all-to-all-start) | async-done | bytes 720928 | tf_op jit(solution)/shard_map/all_to_all | solution.py:323
  43.8 9.3 %select.1 = (f32[3072,128]{1,0:T(8,128)S(1)}, f32[192,128]{1,0:T(8,128)S(1)}) custom-call(s32[2]{0:T(128)S(1)} %pad_add_fusion.3.where_ref, f32[1408,128]{1,0:T(8,128)} %bitcast.6.aux_ref, f32[4224,128]{1,0:T(8,128)S(1)} %forecast.1.q_ref), custom_call_target="tpu_custom_call" | custom-call | tf_op jit(solution)/shard_map/select/pallas_call | solution.py:336
  53.1 0.0 copy-start.6
  53.1 52.4 %all_to_all.20 = f32[256,3,4,128]{3,2,1,0:T(4,128)S(1)} all-to-all(f32[256,3,4,128]{3,2,1,0:T(4,128)S(1)} %bitcast.18), channel_id=1, replica_groups=mesh['mem'=16,'dom'=16] {'mem','dom'}, dimensions={0} | all-to-all | bytes 3145728 | tf_op jit(solution)/shard_map/all_to_all | solution.py:348
  105.6 0.0 copy-done.6
  105.6 6.9 %update.1 = f32[16,8,16,128]{3,2,1,0:T(8,128)S(1)} custom-call(s32[2]{0:T(128)S(1)} %pad_add_fusion.3.where_ref, s32[1,2]{1,0:T(1,128)S(1)} %copy-done.6, s32[4,128]{1,0:T(4,128)S(1)} %reshape.39.list_ref, f32[192,128]{1,0:T(8,128)S(1)} %get-tuple-element.7.meta_ref, f32[3072,128]{1,0:T(8,128)S(1)} %bitcast.14), custom_call_target="tpu_custom_call" | custom-call | tf_op jit(solution)/shard_map/update/pallas_call | solution.py:352
  112.4 33.0 %all_to_all.21 = f32[16,128,128]{2,1,0:T(8,128)S(1)} all-to-all(f32[16,128,128]{2,1,0:T(8,128)S(1)} %bitcast.16), channel_id=1, replica_groups=mesh['mem'=16,'dom'=16] {'mem'}, dimensions={0} | all-to-all | bytes 2097152 | tf_op jit(solution)/shard_map/all_to_all | solution.py:361
  145.4 1.5 %finish.1 = f32[2048,128]{1,0:T(8,128)} custom-call(f32[2048,128]{1,0:T(8,128)S(1)} %bitcast.17), custom_call_target="tpu_custom_call" | custom-call | tf_op jit(solution)/shard_map/finish/pallas_call | solution.py:364
  (4 shorter events, 0.0 us)
Async XLA Ops:
  0.0 7.7 %copy-start.7 = (s32[1,2,256]{2,1,0:T(2,128)S(1)}, s32[1,2,256]{2,1,0:T(2,128)}, u32[]{:S(2)}) copy-start(s32[1,2,256]{2,1,0:T(2,128)} %param.16) | copy-start | bytes 6148
  0.0 25.4 %copy-start.2 = (f32[1024]{0:T(1024)S(1)}, f32[1024]{0:T(1024)}, u32[]{:S(2)}) copy-start(f32[1024]{0:T(1024)} %param.15) | copy-start | bytes 12292
  0.0 25.4 %copy-start.1 = (f32[1024]{0:T(1024)S(1)}, f32[1024]{0:T(1024)}, u32[]{:S(2)}) copy-start(f32[1024]{0:T(1024)} %param.14) | copy-start | bytes 12292
  0.0 25.4 %copy-start = (s32[1024]{0:T(1024)S(1)}, s32[1024]{0:T(1024)}, u32[]{:S(2)}) copy-start(s32[1024]{0:T(1024)} %param.13) | copy-start | bytes 12292
  0.0 26.3 %all-to-all-start.1 = ((f32[16,128,128]{2,1,0:T(8,128)}), f32[16,128,128]{2,1,0:T(8,128)S(1)}, u32[]{:S(2)}, u32[]{:S(2)}) async-start(f32[16,128,128]{2,1,0:T(8,128)} %bitcast.22), calls=%async_computation.1 | async-start | bytes 2097152 | tf_op jit(solution)/shard_map/all_to_all | solution.py:307
  7.8 25.4 %copy-start.3 = (f32[32]{0:T(128)S(1)}, f32[32]{0:T(128)}, u32[]{:S(2)}) copy-start(f32[32]{0:T(128)} %north_ref.1) | copy-start | bytes 388
  7.8 25.4 %copy-start.4 = (f32[32]{0:T(128)S(1)}, f32[32]{0:T(128)}, u32[]{:S(2)}) copy-start(f32[32]{0:T(128)} %east_ref.1) | copy-start | bytes 388
  7.8 25.4 %copy-start.5 = (f32[32]{0:T(128)S(1)}, f32[32]{0:T(128)}, u32[]{:S(2)}) copy-start(f32[32]{0:T(128)} %mix_ref.1) | copy-start | bytes 388
  7.8 1.9 %collective-permute-start = (s32[4,128]{1,0:T(4,128)S(1)}, s32[4,128]{1,0:T(4,128)S(1)}, u32[]{:S(2)}, u32[]{:S(2)}) collective-permute-start(s32[4,128]{1,0:T(4,128)S(1)} %reshape.39.list_ref), channel_id=1, source_target_pairs={{0,16},{16,0},{32,48},{48,32},{64,80},{80,64},{96,112},{112,96},{1... | collective-permute-start | bytes 6152 | tf_op jit(solution)/shard_map/ppermute | solution.py:299
  9.7 6.9 %collective-permute-start.2 = (s32[8,128]{1,0:T(8,128)S(1)}, s32[8,128]{1,0:T(8,128)S(1)}, u32[]{:S(2)}, u32[]{:S(2)}) collective-permute-start(s32[8,128]{1,0:T(8,128)S(1)} %pad_add_fusion.2.own_ref), channel_id=1, source_target_pairs={{224,0},{240,16},{0,32},{16,48},{32,64},{48,80},{64,96},{80,112},{... | collective-permute-start | bytes 12296 | tf_op jit(solution)/shard_map/ppermute | solution.py:296
  11.3 5.2 %collective-permute-start.1 = (s32[8,128]{1,0:T(8,128)S(1)}, s32[8,128]{1,0:T(8,128)S(1)}, u32[]{:S(2)}, u32[]{:S(2)}) collective-permute-start(s32[8,128]{1,0:T(8,128)S(1)} %pad_add_fusion.2.own_ref), channel_id=1, source_target_pairs={{32,0},{48,16},{64,32},{80,48},{96,64},{112,80},{128,96},{144,112}... | collective-permute-start | bytes 12296 | tf_op jit(solution)/shard_map/ppermute | solution.py:296
  16.6 8.9 %collective-permute-start.3 = (s32[24,128]{1,0:T(8,128)S(1)}, s32[24,128]{1,0:T(8,128)S(1)}, u32[]{:S(2)}, u32[]{:S(2)}) collective-permute-start(s32[24,128]{1,0:T(8,128)S(1)} %pad_add_fusion), channel_id=1, source_target_pairs={{96,0},{112,16},{128,32},{144,48},{160,64},{176,80},{192,96},{208,... | collective-permute-start | bytes 36872 | tf_op jit(solution)/shard_map/ppermute | solution.py:296
  19.6 5.8 %collective-permute-start.4 = (s32[16,128]{1,0:T(8,128)S(1)}, s32[16,128]{1,0:T(8,128)S(1)}, u32[]{:S(2)}, u32[]{:S(2)}) collective-permute-start(s32[16,128]{1,0:T(8,128)S(1)} %pad_add_fusion.1), channel_id=1, source_target_pairs={{160,0},{176,16},{192,32},{208,48},{224,64},{240,80},{0,96},{16,11... | collective-permute-start | bytes 24584 | tf_op jit(solution)/shard_map/ppermute | solution.py:296
  26.3 17.5 %all-to-all-start = ((f32[16,88,128]{2,1,0:T(8,128)}), f32[16,88,128]{2,1,0:T(8,128)}, u32[]{:S(2)}, u32[]{:S(2)}) async-start(f32[16,88,128]{2,1,0:T(8,128)} %bitcast.5), calls=%async_computation | async-start | bytes 1441792 | tf_op jit(solution)/shard_map/all_to_all | solution.py:323
  53.1 52.4 %copy-start.6 = (s32[1,2]{1,0:T(1,128)S(1)}, s32[1,2]{1,0:T(1,128)}, u32[]{:S(2)}) copy-start(s32[1,2]{1,0:T(1,128)} %count_ref.1) | copy-start | bytes 28

commit v5 on v4

--- a/solution.py
+++ b/solution.py
@@ -123,20 +123,38 @@
 
 
 def select_kernel(where_ref, aux_ref, q_ref, out_ref, meta_ref, hx_ref):
-    def extract(i, _):
-        g, j = i // OBS_CHUNKS, i % OBS_CHUNKS
-        cell = aux_ref[pl.ds(g * 8 * AUX + LISTS + j, 8, stride=AUX), :].astype(jnp.int32)
+    sub = lax.broadcasted_iota(jnp.int32, (COLS, 2 * COLS), 0)
+
+    def extract(s):
+        s = lax.rem(s, STRIPS)
+        cell = aux_ref[pl.ds(pl.multiple_of(s * AUX + LISTS, 8), 8), :].astype(jnp.int32)
         lanes = cell & (COLS - 1)
         line = cell >> 7
         rows = (line & (ROWS - 1)) * LEVELS + (line >> 2)
-        sums = [jnp.zeros((8, COLS), F32) for _ in range(4)]
-        for p in range(CELL_ROWS):
-            src = q_ref[pl.ds(p + g * 8 * PITCH, 8, stride=PITCH), :]
-            sums[p % 4] = jnp.where(rows == p, lane_gather(src, lanes), sums[p % 4])
-        hx_ref[pl.ds(g * 64 + j, 8, stride=OBS_CHUNKS), :] = (sums[0] + sums[1]) + (sums[2] + sums[3])
-        return 0
-
-    lax.fori_loop(0, 2 * OBS_CHUNKS, extract, 0)
+        block = q_ref[pl.ds(pl.multiple_of(FIELD + s * CELL_ROWS, 8), CELL_ROWS), :]
+        high = block.astype(BF16)
+        rest = block - high.astype(F32)
+        middle = rest.astype(BF16)
+        low = (rest - middle.astype(F32)).astype(BF16)
+        block = jnp.concatenate([high, middle, low], axis=1)
+        found = []
+        for j in range(0, OBS_CHUNKS, 2):
+            row = jnp.concatenate([rows[j : j + 1], rows[j + 1 : j + 2]], axis=1)
+            lane = jnp.concatenate([lanes[j : j + 1], lanes[j + 1 : j + 2]], axis=1)
+            pick = jnp.where(sub == row, 1.0, 0.0).astype(BF16)
+            picked = jnp.dot(
+                block, jnp.concatenate([pick, pick, pick], axis=0), preferred_element_type=F32
+            )
+            picked = jnp.sum(jnp.where(sub == lane, picked, 0.0), axis=0, keepdims=True)
+            found += [picked[:, :COLS], picked[:, COLS:]]
+        for j in range(OBS_CHUNKS):
+            hx_ref[pl.ds(s * OBS_CHUNKS + j, 1), :] = found[j]
+
+    def first(i, _):
+        extract(i + STRIPS - 1)
+        return 0
+
+    lax.fori_loop(0, 3, first, 0)
 
     def strip(a, _):
         for kb in range(PER_MEM):
@@ -160,6 +178,7 @@
                 out_ref[pl.ds((kb * STRIPS + a) * SEND + COLS_HERE, SLOT_ROWS), :] = found[
                     i * SLOT_ROWS : (i + 1) * SLOT_ROWS
                 ]
+        extract(a + 2)
         return 0
 
     lax.fori_loop(0, STRIPS, strip, 0)
@@ -264,13 +283,16 @@
         shift = jnp.sum(full * inner, axis=1, keepdims=True) / norms[t]
         scale = jnp.sqrt((members - 1) / norms[t])
         root = parts(full * scale)
-        for c in range(4 * t, 4 * t + 4):
-            x = in_ref[pl.ds(c, members, stride=SEND), :]
+        for c in range(4 * t, 4 * t + 4, 2):
+            x = jnp.concatenate(
+                [in_ref[pl.ds(c + i, members, stride=SEND), :] for i in range(2)], axis=1
+            )
             mean = jnp.sum(x, axis=0, keepdims=True) * (1.0 / members)
             x = x - mean
             moved = mean + jnp.sum(x * shift, axis=0, keepdims=True)
             out = product(root, parts(x)) + moved
-            out_ref[:, c] = out.reshape(PER_MEM, PER_MEM, COLS)
+            for i in range(2):
+                out_ref[:, c + i] = out[:, i * COLS : (i + 1) * COLS].reshape(PER_MEM, PER_MEM, COLS)
 
 
 def finish_kernel(in_ref, out_ref):

time: 147 us -> 145 us (0.986)
  Pallas kernels: 26.6 us -> 24.6 us
    pallas_call x1, Pallas kernels: 9.27 us -> 7.73 us  [shards(): pl.pallas_call(select_kernel, compiler_params=PARAMS, name='select', out_...]
where the time goes in v5:
time: 145 us
  blocking collectives  85.4 us (59%)
  starting transfers between devices  25.5 us (18%)
  Pallas kernels  24.6 us (17%)
  waiting for transfers between devices  9.14 us (6%)
    all_to_all x1, blocking collectives, shards(): lax.all_to_all(sent.reshape(PER_MEM * STRIPS, SEND // 4, 4, COLS), ('mem'...  52.4 us
    all_to_all x1, blocking collectives, shards(): lax.all_to_all(updated.reshape(PER_MEM, COLS_HERE * PER_MEM, COLS), 'mem'...  33 us
    ppermute x4, starting transfers between devices, shifted(): lax.ppermute(x, 'mem', [((i + by) % PER_MEM, i) for i in range(PER_MEM)])  10 us
    pallas_call x1, Pallas kernels, shards(): pl.pallas_call(forecast_kernel, compiler_params=PARAMS, cost_estimate=pl....  8.03 us
    pallas_call x1, Pallas kernels, shards(): pl.pallas_call(select_kernel, compiler_params=PARAMS, name='select', out_...  7.73 us
    all_to_all x1, starting transfers between devices, shards(): lax.all_to_all(prior.reshape(PER_MEM, CELL_ROWS, COLS), 'dom', split_axis...  7.72 us
    all_to_all x1, starting transfers between devices, shards(): lax.all_to_all(aux.reshape(STRIPS, AUX, COLS), 'dom', split_axis=0, conca...  6.73 us
    pallas_call x1, Pallas kernels, shards(): pl.pallas_call(update_kernel, compiler_params=PARAMS, name='update', out_...  6.46 us
  transfers between devices with their start and end apart: 7, of which 4 were waited for; matrix products, arithmetic and copies ran while one was open for 0% of the time, Pallas kernels for 6%

profile of v5, /device:TPU:1, one launch (start us, length us, event | category | flops | bytes accessed | tf_op | source)
XLA Modules:
  0.0 145.0 jit_solution(3936902441400463615)
XLA Ops:
  0.0 0.0 copy-start.7
  0.0 0.0 copy-start.2
  0.0 0.0 copy-start.1
  0.0 0.0 copy-start
  0.0 7.7 %all-to-all-start.1 = ((f32[16,128,128]{2,1,0:T(8,128)}), f32[16,128,128]{2,1,0:T(8,128)S(1)}, u32[]{:S(2)}, u32[]{:S(2)}) async-start(f32[16,128,128]{2,1,0:T(8,128)} %bitcast.22), calls=%async_computation.1 | async-start | bytes 2097152 | tf_op jit(solution)/shard_map/all_to_all | solution.py:329
  7.7 0.0 copy-done.7
  7.8 0.0 copy-start.3
  7.8 0.0 copy-start.4
  7.8 0.0 copy-start.5
  7.8 1.0 collective-permute-start
  8.8 0.8 collective-permute-done
  9.7 1.6 %collective-permute-start.2 = (s32[8,128]{1,0:T(8,128)S(1)}, s32[8,128]{1,0:T(8,128)S(1)}, u32[]{:S(2)}, u32[]{:S(2)}) collective-permute-start(s32[8,128]{1,0:T(8,128)S(1)} %pad_add_fusion.2.own_ref), channel_id=1, source_target_pairs={{224,0},{240,16},{0,32},{16,48},{32,64},{48,80},{64,96},{80,112},{... | collective-permute-start | bytes 12296 | tf_op jit(solution)/shard_map/ppermute | solution.py:318
  11.3 4.0 %collective-permute-start.1 = (s32[8,128]{1,0:T(8,128)S(1)}, s32[8,128]{1,0:T(8,128)S(1)}, u32[]{:S(2)}, u32[]{:S(2)}) collective-permute-start(s32[8,128]{1,0:T(8,128)S(1)} %pad_add_fusion.2.own_ref), channel_id=1, source_target_pairs={{32,0},{48,16},{64,32},{80,48},{96,64},{112,80},{128,96},{144,112}... | collective-permute-start | bytes 12296 | tf_op jit(solution)/shard_map/ppermute | solution.py:318
  15.3 1.2 collective-permute-done.2.l2_ref
  16.5 0.0 collective-permute-done.1.l1_ref
  16.6 3.1 %collective-permute-start.3 = (s32[24,128]{1,0:T(8,128)S(1)}, s32[24,128]{1,0:T(8,128)S(1)}, u32[]{:S(2)}, u32[]{:S(2)}) collective-permute-start(s32[24,128]{1,0:T(8,128)S(1)} %pad_add_fusion), channel_id=1, source_target_pairs={{96,0},{112,16},{128,32},{144,48},{160,64},{176,80},{192,96},{208,... | collective-permute-start | bytes 36872 | tf_op jit(solution)/shard_map/ppermute | solution.py:318
  19.6 1.3 collective-permute-start.4
  20.9 4.5 %collective-permute-done.4.l4_ref = s32[16,128]{1,0:T(8,128)S(1)} collective-permute-done((s32[16,128]{1,0:T(8,128)S(1)}, s32[16,128]{1,0:T(8,128)S(1)}, u32[]{:S(2)}, u32[]{:S(2)}) %collective-permute-start.4) | collective-permute-done | bytes 8224 | tf_op jit(solution)/shard_map/ppermute | solution.py:318
  25.4 0.0 collective-permute-done.3.l3_ref
  25.4 0.0 copy-done.2
  25.4 0.0 copy-done.1
  25.4 0.0 copy-done
  25.4 0.9 aux.1
  26.3 0.0 all-to-all-done.1
  26.3 6.7 %all-to-all-start = ((f32[16,88,128]{2,1,0:T(8,128)}), f32[16,88,128]{2,1,0:T(8,128)}, u32[]{:S(2)}, u32[]{:S(2)}) async-start(f32[16,88,128]{2,1,0:T(8,128)} %bitcast.5), calls=%async_computation | async-start | bytes 1441792 | tf_op jit(solution)/shard_map/all_to_all | solution.py:345
  33.1 0.1 pad_add_fusion.3.where_ref
  33.2 0.0 copy-done.3
  33.2 0.0 copy-done.4
  33.2 0.0 copy-done.5
  33.2 8.0 %forecast.1.q_ref = f32[4224,128]{1,0:T(8,128)S(1)} custom-call(f32[32]{0:T(128)S(1)} %copy-done.3, f32[32]{0:T(128)S(1)} %copy-done.4, f32[32]{0:T(128)S(1)} %copy-done.5, f32[2048,128]{1,0:T(8,128)S(1)} %bitcast.15), custom_call_target="tpu_custom_call" | custom-call | flops 30000000 | bytes 60000000 | tf_op jit(solution)/shard_map/forecast/pallas_call | solution.py:348
  41.2 2.6 %all-to-all-done = f32[16,88,128]{2,1,0:T(8,128)} async-done(((f32[16,88,128]{2,1,0:T(8,128)}), f32[16,88,128]{2,1,0:T(8,128)}, u32[]{:S(2)}, u32[]{:S(2)}) %all-to-all-start) | async-done | bytes 720928 | tf_op jit(solution)/shard_map/all_to_all | solution.py:345
  43.8 7.7 %select.1 = (f32[3072,128]{1,0:T(8,128)S(1)}, f32[192,128]{1,0:T(8,128)S(1)}) custom-call(s32[2]{0:T(128)S(1)} %pad_add_fusion.3.where_ref, f32[1408,128]{1,0:T(8,128)} %bitcast.6.aux_ref, f32[4224,128]{1,0:T(8,128)S(1)} %forecast.1.q_ref), custom_call_target="tpu_custom_call" | custom-call | tf_op jit(solution)/shard_map/select/pallas_call | solution.py:358
  51.6 0.0 copy-start.6
  51.6 52.4 %all_to_all.20 = f32[256,3,4,128]{3,2,1,0:T(4,128)S(1)} all-to-all(f32[256,3,4,128]{3,2,1,0:T(4,128)S(1)} %bitcast.18), channel_id=1, replica_groups=mesh['mem'=16,'dom'=16] {'mem','dom'}, dimensions={0} | all-to-all | bytes 3145728 | tf_op jit(solution)/shard_map/all_to_all | solution.py:370
  104.0 0.0 copy-done.6
  104.0 6.5 %update.1 = f32[16,8,16,128]{3,2,1,0:T(8,128)S(1)} custom-call(s32[2]{0:T(128)S(1)} %pad_add_fusion.3.where_ref, s32[1,2]{1,0:T(1,128)S(1)} %copy-done.6, s32[4,128]{1,0:T(4,128)S(1)} %reshape.39.list_ref, f32[192,128]{1,0:T(8,128)S(1)} %get-tuple-element.7.meta_ref, f32[3072,128]{1,0:T(8,128)S(1)} %bitcast.14), custom_call_target="tpu_custom_call" | custom-call | tf_op jit(solution)/shard_map/update/pallas_call | solution.py:374
  110.5 33.0 %all_to_all.21 = f32[16,128,128]{2,1,0:T(8,128)S(1)} all-to-all(f32[16,128,128]{2,1,0:T(8,128)S(1)} %bitcast.16), channel_id=1, replica_groups=mesh['mem'=16,'dom'=16] {'mem'}, dimensions={0} | all-to-all | bytes 2097152 | tf_op jit(solution)/shard_map/all_to_all | solution.py:383
  143.5 1.5 %finish.1 = f32[2048,128]{1,0:T(8,128)} custom-call(f32[2048,128]{1,0:T(8,128)S(1)} %bitcast.17), custom_call_target="tpu_custom_call" | custom-call | tf_op jit(solution)/shard_map/finish/pallas_call | solution.py:386
  (4 shorter events, 0.0 us)
Async XLA Ops:
  0.0 7.7 %copy-start.7 = (s32[1,2,256]{2,1,0:T(2,128)S(1)}, s32[1,2,256]{2,1,0:T(2,128)}, u32[]{:S(2)}) copy-start(s32[1,2,256]{2,1,0:T(2,128)} %param.16) | copy-start | bytes 6148
  0.0 25.4 %copy-start.2 = (f32[1024]{0:T(1024)S(1)}, f32[1024]{0:T(1024)}, u32[]{:S(2)}) copy-start(f32[1024]{0:T(1024)} %param.15) | copy-start | bytes 12292
  0.0 25.4 %copy-start.1 = (f32[1024]{0:T(1024)S(1)}, f32[1024]{0:T(1024)}, u32[]{:S(2)}) copy-start(f32[1024]{0:T(1024)} %param.14) | copy-start | bytes 12292
  0.0 25.4 %copy-start = (s32[1024]{0:T(1024)S(1)}, s32[1024]{0:T(1024)}, u32[]{:S(2)}) copy-start(s32[1024]{0:T(1024)} %param.13) | copy-start | bytes 12292
  0.0 26.3 %all-to-all-start.1 = ((f32[16,128,128]{2,1,0:T(8,128)}), f32[16,128,128]{2,1,0:T(8,128)S(1)}, u32[]{:S(2)}, u32[]{:S(2)}) async-start(f32[16,128,128]{2,1,0:T(8,128)} %bitcast.22), calls=%async_computation.1 | async-start | bytes 2097152 | tf_op jit(solution)/shard_map/all_to_all | solution.py:329
  7.8 25.4 %copy-start.3 = (f32[32]{0:T(128)S(1)}, f32[32]{0:T(128)}, u32[]{:S(2)}) copy-start(f32[32]{0:T(128)} %north_ref.1) | copy-start | bytes 388
  7.8 25.4 %copy-start.4 = (f32[32]{0:T(128)S(1)}, f32[32]{0:T(128)}, u32[]{:S(2)}) copy-start(f32[32]{0:T(128)} %east_ref.1) | copy-start | bytes 388
  7.8 25.4 %copy-start.5 = (f32[32]{0:T(128)S(1)}, f32[32]{0:T(128)}, u32[]{:S(2)}) copy-start(f32[32]{0:T(128)} %mix_ref.1) | copy-start | bytes 388
  7.8 1.9 %collective-permute-start = (s32[4,128]{1,0:T(4,128)S(1)}, s32[4,128]{1,0:T(4,128)S(1)}, u32[]{:S(2)}, u32[]{:S(2)}) collective-permute-start(s32[4,128]{1,0:T(4,128)S(1)} %reshape.39.list_ref), channel_id=1, source_target_pairs={{0,16},{16,0},{32,48},{48,32},{64,80},{80,64},{96,112},{112,96},{1... | collective-permute-start | bytes 6152 | tf_op jit(solution)/shard_map/ppermute | solution.py:321
  9.7 6.9 %collective-permute-start.2 = (s32[8,128]{1,0:T(8,128)S(1)}, s32[8,128]{1,0:T(8,128)S(1)}, u32[]{:S(2)}, u32[]{:S(2)}) collective-permute-start(s32[8,128]{1,0:T(8,128)S(1)} %pad_add_fusion.2.own_ref), channel_id=1, source_target_pairs={{224,0},{240,16},{0,32},{16,48},{32,64},{48,80},{64,96},{80,112},{... | collective-permute-start | bytes 12296 | tf_op jit(solution)/shard_map/ppermute | solution.py:318
  11.3 5.2 %collective-permute-start.1 = (s32[8,128]{1,0:T(8,128)S(1)}, s32[8,128]{1,0:T(8,128)S(1)}, u32[]{:S(2)}, u32[]{:S(2)}) collective-permute-start(s32[8,128]{1,0:T(8,128)S(1)} %pad_add_fusion.2.own_ref), channel_id=1, source_target_pairs={{32,0},{48,16},{64,32},{80,48},{96,64},{112,80},{128,96},{144,112}... | collective-permute-start | bytes 12296 | tf_op jit(solution)/shard_map/ppermute | solution.py:318
  16.6 8.9 %collective-permute-start.3 = (s32[24,128]{1,0:T(8,128)S(1)}, s32[24,128]{1,0:T(8,128)S(1)}, u32[]{:S(2)}, u32[]{:S(2)}) collective-permute-start(s32[24,128]{1,0:T(8,128)S(1)} %pad_add_fusion), channel_id=1, source_target_pairs={{96,0},{112,16},{128,32},{144,48},{160,64},{176,80},{192,96},{208,... | collective-permute-start | bytes 36872 | tf_op jit(solution)/shard_map/ppermute | solution.py:318
  19.6 5.8 %collective-permute-start.4 = (s32[16,128]{1,0:T(8,128)S(1)}, s32[16,128]{1,0:T(8,128)S(1)}, u32[]{:S(2)}, u32[]{:S(2)}) collective-permute-start(s32[16,128]{1,0:T(8,128)S(1)} %pad_add_fusion.1), channel_id=1, source_target_pairs={{160,0},{176,16},{192,32},{208,48},{224,64},{240,80},{0,96},{16,11... | collective-permute-start | bytes 24584 | tf_op jit(solution)/shard_map/ppermute | solution.py:318
  26.3 17.5 %all-to-all-start = ((f32[16,88,128]{2,1,0:T(8,128)}), f32[16,88,128]{2,1,0:T(8,128)}, u32[]{:S(2)}, u32[]{:S(2)}) async-start(f32[16,88,128]{2,1,0:T(8,128)} %bitcast.5), calls=%async_computation | async-start | bytes 1441792 | tf_op jit(solution)/shard_map/all_to_all | solution.py:345
  51.6 52.4 %copy-start.6 = (s32[1,2]{1,0:T(1,128)S(1)}, s32[1,2]{1,0:T(1,128)}, u32[]{:S(2)}) copy-start(s32[1,2]{1,0:T(1,128)} %count_ref.1) | copy-start | bytes 28

commit v6 on v5

--- a/solution.py
+++ b/solution.py
@@ -154,7 +154,7 @@
         extract(i + STRIPS - 1)
         return 0
 
-    lax.fori_loop(0, 3, first, 0)
+    lax.fori_loop(0, 3, first, 0, unroll=3)
 
     def strip(a, _):
         for kb in range(PER_MEM):
@@ -214,7 +214,7 @@
     def plus_identity(x, scale):
         return jnp.where(diagonal, x + scale, x)
 
-    norms, drives = [], []
+    drives, scales = [], []
     for t in range(2):
         values, rhos, anomalies = [], [], []
         for h in range(2):
@@ -250,15 +250,18 @@
         rho = jnp.concatenate(rhos, axis=1)
         innovation = jnp.concatenate(values, axis=1)
         drives.append(jnp.sum(anomaly * (rho * innovation), axis=1, keepdims=True))
-        scaled = parts(anomaly * jnp.sqrt(rho))
-        gram = product(scaled, scaled, (((1,), (1,)), ((), ())))
-        gram = plus_identity(gram, (members - 1) / INFLATION)
-        norm = jnp.sqrt(jnp.sum(jnp.sum(gram * gram, axis=1, keepdims=True), axis=0, keepdims=True))
-        norms.append(norm)
-        it = gram / norm
-        factor = plus_identity(-0.5 * it, 1.5)
-        root_ref[t] = factor
-        it_ref[t] = product(parts(it), parts(factor))
+        scales.append(parts(anomaly * jnp.sqrt(rho)))
+    grams = [
+        plus_identity(product(x, x, (((1,), (1,)), ((), ()))), (members - 1) / INFLATION) for x in scales
+    ]
+    norms = [
+        jnp.sqrt(jnp.sum(jnp.sum(x * x, axis=0, keepdims=True), axis=1, keepdims=True)) for x in grams
+    ]
+    its = [gram / norm for gram, norm in zip(grams, norms)]
+    factors = [plus_identity(-0.5 * it, 1.5) for it in its]
+    for t in range(2):
+        root_ref[t] = factors[t]
+        it_ref[t] = product(parts(its[t]), parts(factors[t]))
 
     def iteration(_, c):
         roots = [parts(root_ref[t]) for t in range(2)]
@@ -295,14 +298,23 @@
                 out_ref[:, c + i] = out[:, i * COLS : (i + 1) * COLS].reshape(PER_MEM, PER_MEM, COLS)
 
 
-def finish_kernel(in_ref, out_ref):
-    def member(m, _):
-        block = in_ref[pl.ds(m, COLS, stride=PER_MEM), :].T
-        for r in range(ROWS):
-            out_ref[pl.ds(m * CELL_ROWS + r, LEVELS, stride=ROWS), :] = block[r * LEVELS : (r + 1) * LEVELS]
-        return 0
-
-    lax.fori_loop(0, PER_MEM, member, 0, unroll=4)
+def finish_kernel(in_ref, out_ref, turned_ref, sems):
+    group = 4
+
+    def copy(g):
+        rows = pl.ds(g * group * CELL_ROWS, group * CELL_ROWS)
+        return pltpu.make_async_copy(turned_ref.at[rows, :], out_ref.at[rows, :], sems.at[g])
+
+    for g in range(PER_MEM // group):
+        for m in range(g * group, (g + 1) * group):
+            block = in_ref[pl.ds(m, COLS, stride=PER_MEM), :].T
+            for r in range(ROWS):
+                turned_ref[pl.ds(m * CELL_ROWS + r, LEVELS, stride=ROWS), :] = block[
+                    r * LEVELS : (r + 1) * LEVELS
+                ]
+        copy(g).start()
+    for g in range(PER_MEM // group):
+        copy(g).wait()
 
 
 PARAMS = pltpu.CompilerParams(vmem_limit_bytes=20 * 1024 * 1024)
@@ -389,7 +401,11 @@
         name="finish",
         out_shape=jax.ShapeDtypeStruct((PER_MEM * CELL_ROWS, COLS), F32),
         in_specs=[VMEM],
-        out_specs=VMEM,
+        out_specs=pl.BlockSpec(memory_space=pl.ANY),
+        scratch_shapes=[
+            pltpu.VMEM((PER_MEM * CELL_ROWS, COLS), F32),
+            pltpu.SemaphoreType.DMA((4,)),
+        ],
     )(back.reshape(PER_MEM * COLS_HERE * PER_MEM, COLS))
     return result.reshape(PER_MEM, LEVELS, ROWS, COLS)
 

time: 145 us -> 144 us (level)
  no operation moved by 1% of the time
where the time goes in v6:
time: 144 us
  blocking collectives  85.4 us (59%)
  starting transfers between devices  25.5 us (18%)
  Pallas kernels  23.7 us (16%)
  waiting for transfers between devices  9.14 us (6%)
    all_to_all x1, blocking collectives, shards(): lax.all_to_all(sent.reshape(PER_MEM * STRIPS, SEND // 4, 4, COLS), ('mem'...  52.4 us
    all_to_all x1, blocking collectives, shards(): lax.all_to_all(updated.reshape(PER_MEM, COLS_HERE * PER_MEM, COLS), 'mem'...  33 us
    ppermute x4, starting transfers between devices, shifted(): lax.ppermute(x, 'mem', [((i + by) % PER_MEM, i) for i in range(PER_MEM)])  10 us
    pallas_call x1, Pallas kernels, shards(): pl.pallas_call(forecast_kernel, compiler_params=PARAMS, cost_estimate=pl....  8.03 us
    all_to_all x1, starting transfers between devices, shards(): lax.all_to_all(prior.reshape(PER_MEM, CELL_ROWS, COLS), 'dom', split_axis...  7.72 us
    pallas_call x1, Pallas kernels, shards(): pl.pallas_call(select_kernel, compiler_params=PARAMS, name='select', out_...  7.52 us
    all_to_all x1, starting transfers between devices, shards(): lax.all_to_all(aux.reshape(STRIPS, AUX, COLS), 'dom', split_axis=0, conca...  6.73 us
    pallas_call x1, Pallas kernels, shards(): pl.pallas_call(update_kernel, compiler_params=PARAMS, name='update', out_...  6.05 us
  transfers between devices with their start and end apart: 7, of which 4 were waited for; matrix products, arithmetic and copies ran while one was open for 0% of the time, Pallas kernels for 6%

profile of v6, /device:TPU:1, one launch (start us, length us, event | category | flops | bytes accessed | tf_op | source)
XLA Modules:
  0.0 144.0 jit_solution(12843284315456538730)
XLA Ops:
  0.0 0.0 copy-start.7
  0.0 0.0 copy-start.2
  0.0 0.0 copy-start.1
  0.0 0.0 copy-start
  0.0 7.7 %all-to-all-start.1 = ((f32[16,128,128]{2,1,0:T(8,128)}), f32[16,128,128]{2,1,0:T(8,128)S(1)}, u32[]{:S(2)}, u32[]{:S(2)}) async-start(f32[16,128,128]{2,1,0:T(8,128)} %bitcast.22), calls=%async_computation.1 | async-start | bytes 2097152 | tf_op jit(solution)/shard_map/all_to_all | solution.py:341
  7.7 0.0 copy-done.7
  7.8 0.0 copy-start.3
  7.8 0.0 copy-start.4
  7.8 0.0 copy-start.5
  7.8 1.0 collective-permute-start
  8.8 0.8 collective-permute-done
  9.7 1.6 %collective-permute-start.2 = (s32[8,128]{1,0:T(8,128)S(1)}, s32[8,128]{1,0:T(8,128)S(1)}, u32[]{:S(2)}, u32[]{:S(2)}) collective-permute-start(s32[8,128]{1,0:T(8,128)S(1)} %pad_add_fusion.2.own_ref), channel_id=1, source_target_pairs={{224,0},{240,16},{0,32},{16,48},{32,64},{48,80},{64,96},{80,112},{... | collective-permute-start | bytes 12296 | tf_op jit(solution)/shard_map/ppermute | solution.py:330
  11.3 4.0 %collective-permute-start.1 = (s32[8,128]{1,0:T(8,128)S(1)}, s32[8,128]{1,0:T(8,128)S(1)}, u32[]{:S(2)}, u32[]{:S(2)}) collective-permute-start(s32[8,128]{1,0:T(8,128)S(1)} %pad_add_fusion.2.own_ref), channel_id=1, source_target_pairs={{32,0},{48,16},{64,32},{80,48},{96,64},{112,80},{128,96},{144,112}... | collective-permute-start | bytes 12296 | tf_op jit(solution)/shard_map/ppermute | solution.py:330
  15.3 1.2 collective-permute-done.2.l2_ref
  16.5 0.0 collective-permute-done.1.l1_ref
  16.6 3.1 %collective-permute-start.3 = (s32[24,128]{1,0:T(8,128)S(1)}, s32[24,128]{1,0:T(8,128)S(1)}, u32[]{:S(2)}, u32[]{:S(2)}) collective-permute-start(s32[24,128]{1,0:T(8,128)S(1)} %pad_add_fusion), channel_id=1, source_target_pairs={{96,0},{112,16},{128,32},{144,48},{160,64},{176,80},{192,96},{208,... | collective-permute-start | bytes 36872 | tf_op jit(solution)/shard_map/ppermute | solution.py:330
  19.6 1.3 collective-permute-start.4
  20.9 4.5 %collective-permute-done.4.l4_ref = s32[16,128]{1,0:T(8,128)S(1)} collective-permute-done((s32[16,128]{1,0:T(8,128)S(1)}, s32[16,128]{1,0:T(8,128)S(1)}, u32[]{:S(2)}, u32[]{:S(2)}) %collective-permute-start.4) | collective-permute-done | bytes 8224 | tf_op jit(solution)/shard_map/ppermute | solution.py:330
  25.4 0.0 collective-permute-done.3.l3_ref
  25.4 0.0 copy-done.2
  25.4 0.0 copy-done.1
  25.4 0.0 copy-done
  25.4 0.9 aux.1
  26.3 0.0 all-to-all-done.1
  26.3 6.7 %all-to-all-start = ((f32[16,88,128]{2,1,0:T(8,128)}), f32[16,88,128]{2,1,0:T(8,128)}, u32[]{:S(2)}, u32[]{:S(2)}) async-start(f32[16,88,128]{2,1,0:T(8,128)} %bitcast.5), calls=%async_computation | async-start | bytes 1441792 | tf_op jit(solution)/shard_map/all_to_all | solution.py:357
  33.1 0.1 pad_add_fusion.3.where_ref
  33.2 0.0 copy-done.3
  33.2 0.0 copy-done.4
  33.2 0.0 copy-done.5
  33.2 8.0 %forecast.1.q_ref = f32[4224,128]{1,0:T(8,128)S(1)} custom-call(f32[32]{0:T(128)S(1)} %copy-done.3, f32[32]{0:T(128)S(1)} %copy-done.4, f32[32]{0:T(128)S(1)} %copy-done.5, f32[2048,128]{1,0:T(8,128)S(1)} %bitcast.15), custom_call_target="tpu_custom_call" | custom-call | flops 30000000 | bytes 60000000 | tf_op jit(solution)/shard_map/forecast/pallas_call | solution.py:360
  41.2 2.6 %all-to-all-done = f32[16,88,128]{2,1,0:T(8,128)} async-done(((f32[16,88,128]{2,1,0:T(8,128)}), f32[16,88,128]{2,1,0:T(8,128)}, u32[]{:S(2)}, u32[]{:S(2)}) %all-to-all-start) | async-done | bytes 720928 | tf_op jit(solution)/shard_map/all_to_all | solution.py:357
  43.8 7.5 %select.1 = (f32[3072,128]{1,0:T(8,128)S(1)}, f32[192,128]{1,0:T(8,128)S(1)}) custom-call(s32[2]{0:T(128)S(1)} %pad_add_fusion.3.where_ref, f32[1408,128]{1,0:T(8,128)} %bitcast.6.aux_ref, f32[4224,128]{1,0:T(8,128)S(1)} %forecast.1.q_ref), custom_call_target="tpu_custom_call" | custom-call | tf_op jit(solution)/shard_map/select/pallas_call | solution.py:370
  51.4 0.0 copy-start.6
  51.4 52.4 %all_to_all.20 = f32[256,3,4,128]{3,2,1,0:T(4,128)S(1)} all-to-all(f32[256,3,4,128]{3,2,1,0:T(4,128)S(1)} %bitcast.18), channel_id=1, replica_groups=mesh['mem'=16,'dom'=16] {'mem','dom'}, dimensions={0} | all-to-all | bytes 3145728 | tf_op jit(solution)/shard_map/all_to_all | solution.py:382
  103.8 0.0 copy-done.6
  103.8 6.0 %update.1 = f32[16,8,16,128]{3,2,1,0:T(8,128)S(1)} custom-call(s32[2]{0:T(128)S(1)} %pad_add_fusion.3.where_ref, s32[1,2]{1,0:T(1,128)S(1)} %copy-done.6, s32[4,128]{1,0:T(4,128)S(1)} %reshape.39.list_ref, f32[192,128]{1,0:T(8,128)S(1)} %get-tuple-element.7.meta_ref, f32[3072,128]{1,0:T(8,128)S(1)} %bitcast.14), custom_call_target="tpu_custom_call" | custom-call | tf_op jit(solution)/shard_map/update/pallas_call | solution.py:386
  109.9 33.0 %all_to_all.21 = f32[16,128,128]{2,1,0:T(8,128)S(1)} all-to-all(f32[16,128,128]{2,1,0:T(8,128)S(1)} %bitcast.16), channel_id=1, replica_groups=mesh['mem'=16,'dom'=16] {'mem'}, dimensions={0} | all-to-all | bytes 2097152 | tf_op jit(solution)/shard_map/all_to_all | solution.py:395
  142.9 1.1 finish.1
  (4 shorter events, 0.0 us)
Async XLA Ops:
  0.0 7.7 %copy-start.7 = (s32[1,2,256]{2,1,0:T(2,128)S(1)}, s32[1,2,256]{2,1,0:T(2,128)}, u32[]{:S(2)}) copy-start(s32[1,2,256]{2,1,0:T(2,128)} %param.16) | copy-start | bytes 6148
  0.0 25.4 %copy-start.2 = (f32[1024]{0:T(1024)S(1)}, f32[1024]{0:T(1024)}, u32[]{:S(2)}) copy-start(f32[1024]{0:T(1024)} %param.15) | copy-start | bytes 12292
  0.0 25.4 %copy-start.1 = (f32[1024]{0:T(1024)S(1)}, f32[1024]{0:T(1024)}, u32[]{:S(2)}) copy-start(f32[1024]{0:T(1024)} %param.14) | copy-start | bytes 12292
  0.0 25.4 %copy-start = (s32[1024]{0:T(1024)S(1)}, s32[1024]{0:T(1024)}, u32[]{:S(2)}) copy-start(s32[1024]{0:T(1024)} %param.13) | copy-start | bytes 12292
  0.0 26.3 %all-to-all-start.1 = ((f32[16,128,128]{2,1,0:T(8,128)}), f32[16,128,128]{2,1,0:T(8,128)S(1)}, u32[]{:S(2)}, u32[]{:S(2)}) async-start(f32[16,128,128]{2,1,0:T(8,128)} %bitcast.22), calls=%async_computation.1 | async-start | bytes 2097152 | tf_op jit(solution)/shard_map/all_to_all | solution.py:341
  7.8 25.4 %copy-start.3 = (f32[32]{0:T(128)S(1)}, f32[32]{0:T(128)}, u32[]{:S(2)}) copy-start(f32[32]{0:T(128)} %north_ref.1) | copy-start | bytes 388
  7.8 25.4 %copy-start.4 = (f32[32]{0:T(128)S(1)}, f32[32]{0:T(128)}, u32[]{:S(2)}) copy-start(f32[32]{0:T(128)} %east_ref.1) | copy-start | bytes 388
  7.8 25.4 %copy-start.5 = (f32[32]{0:T(128)S(1)}, f32[32]{0:T(128)}, u32[]{:S(2)}) copy-start(f32[32]{0:T(128)} %mix_ref.1) | copy-start | bytes 388
  7.8 1.9 %collective-permute-start = (s32[4,128]{1,0:T(4,128)S(1)}, s32[4,128]{1,0:T(4,128)S(1)}, u32[]{:S(2)}, u32[]{:S(2)}) collective-permute-start(s32[4,128]{1,0:T(4,128)S(1)} %reshape.39.list_ref), channel_id=1, source_target_pairs={{0,16},{16,0},{32,48},{48,32},{64,80},{80,64},{96,112},{112,96},{1... | collective-permute-start | bytes 6152 | tf_op jit(solution)/shard_map/ppermute | solution.py:333
  9.7 6.9 %collective-permute-start.2 = (s32[8,128]{1,0:T(8,128)S(1)}, s32[8,128]{1,0:T(8,128)S(1)}, u32[]{:S(2)}, u32[]{:S(2)}) collective-permute-start(s32[8,128]{1,0:T(8,128)S(1)} %pad_add_fusion.2.own_ref), channel_id=1, source_target_pairs={{224,0},{240,16},{0,32},{16,48},{32,64},{48,80},{64,96},{80,112},{... | collective-permute-start | bytes 12296 | tf_op jit(solution)/shard_map/ppermute | solution.py:330
  11.3 5.2 %collective-permute-start.1 = (s32[8,128]{1,0:T(8,128)S(1)}, s32[8,128]{1,0:T(8,128)S(1)}, u32[]{:S(2)}, u32[]{:S(2)}) collective-permute-start(s32[8,128]{1,0:T(8,128)S(1)} %pad_add_fusion.2.own_ref), channel_id=1, source_target_pairs={{32,0},{48,16},{64,32},{80,48},{96,64},{112,80},{128,96},{144,112}... | collective-permute-start | bytes 12296 | tf_op jit(solution)/shard_map/ppermute | solution.py:330
  16.6 8.9 %collective-permute-start.3 = (s32[24,128]{1,0:T(8,128)S(1)}, s32[24,128]{1,0:T(8,128)S(1)}, u32[]{:S(2)}, u32[]{:S(2)}) collective-permute-start(s32[24,128]{1,0:T(8,128)S(1)} %pad_add_fusion), channel_id=1, source_target_pairs={{96,0},{112,16},{128,32},{144,48},{160,64},{176,80},{192,96},{208,... | collective-permute-start | bytes 36872 | tf_op jit(solution)/shard_map/ppermute | solution.py:330
  19.6 5.8 %collective-permute-start.4 = (s32[16,128]{1,0:T(8,128)S(1)}, s32[16,128]{1,0:T(8,128)S(1)}, u32[]{:S(2)}, u32[]{:S(2)}) collective-permute-start(s32[16,128]{1,0:T(8,128)S(1)} %pad_add_fusion.1), channel_id=1, source_target_pairs={{160,0},{176,16},{192,32},{208,48},{224,64},{240,80},{0,96},{16,11... | collective-permute-start | bytes 24584 | tf_op jit(solution)/shard_map/ppermute | solution.py:330
  26.3 17.5 %all-to-all-start = ((f32[16,88,128]{2,1,0:T(8,128)}), f32[16,88,128]{2,1,0:T(8,128)}, u32[]{:S(2)}, u32[]{:S(2)}) async-start(f32[16,88,128]{2,1,0:T(8,128)} %bitcast.5), calls=%async_computation | async-start | bytes 1441792 | tf_op jit(solution)/shard_map/all_to_all | solution.py:357
  51.4 52.4 %copy-start.6 = (s32[1,2]{1,0:T(1,128)S(1)}, s32[1,2]{1,0:T(1,128)}, u32[]{:S(2)}) copy-start(s32[1,2]{1,0:T(1,128)} %count_ref.1) | copy-start | bytes 28

commit v7 on v6

--- a/solution.py
+++ b/solution.py
@@ -27,7 +27,7 @@
 PITCH = CELL_ROWS + 8
 FIELD = STRIPS * PITCH
 LISTS = PER_MEM * SLOT_ROWS
-AUX = LISTS + META
+AUX = LISTS + OBS_CHUNKS
 
 
 LANES = lax.GatherDimensionNumbers(
@@ -48,8 +48,8 @@
 ARRIVAL = (0, 1, 7, 3, 4, 2, 5, 6)
 
 
-def aux_kernel(own_ref, l1_ref, l2_ref, l3_ref, l4_ref, cell_ref, value_ref, var_ref, out_ref):
-    parts_in = [own_ref, l1_ref, l2_ref, l3_ref, l4_ref, cell_ref, value_ref, var_ref]
+def aux_kernel(own_ref, l1_ref, l2_ref, l3_ref, l4_ref, cell_ref, out_ref):
+    parts_in = [own_ref, l1_ref, l2_ref, l3_ref, l4_ref, cell_ref]
     for s in range(STRIPS):
         at = s * AUX
         for ref in parts_in:
@@ -183,13 +183,9 @@
 
     lax.fori_loop(0, STRIPS, strip, 0)
 
-    meta_ref[...] = jnp.zeros_like(meta_ref)
     for t in range(3):
-        strip = lax.rem(where_ref[0] + STRIPS - 1 + t, STRIPS)
-        for which in range(3):
-            meta_ref[pl.ds(t * 64 + which, 8, stride=8), :] = aux_ref[
-                pl.ds(pl.multiple_of(strip * AUX + LISTS + which * 8, 8), 8), :
-            ]
+        near = lax.rem(where_ref[0] + STRIPS - 1 + t, STRIPS)
+        meta_ref[t * 8 : (t + 1) * 8, :] = aux_ref[pl.ds(pl.multiple_of(near * AUX + LISTS, 8), 8), :]
 
 
 def parts(x):
@@ -204,7 +200,7 @@
     return dot(a[0], b[0]) + (dot(a[0], b[1]) + dot(a[1], b[0]))
 
 
-def update_kernel(where_ref, count_ref, list_ref, meta_ref, in_ref, out_ref, it_ref, root_ref):
+def update_kernel(where_ref, count_ref, list_ref, cells_ref, behind_ref, here_ref, ahead_ref, in_ref, out_ref, it_ref, root_ref, meta_ref):
     members = 256
     row_id = lax.broadcasted_iota(jnp.int32, (members, members), 0)
     col_id = lax.broadcasted_iota(jnp.int32, (members, members), 1)
@@ -213,6 +209,12 @@
 
     def plus_identity(x, scale):
         return jnp.where(diagonal, x + scale, x)
+
+    meta_ref[...] = jnp.zeros_like(meta_ref)
+    for t, ref in enumerate((behind_ref, here_ref, ahead_ref)):
+        meta_ref[pl.ds(t * 64, 8, stride=8), :] = cells_ref[t * 8 : (t + 1) * 8, :]
+        for which in range(2):
+            meta_ref[pl.ds(t * 64 + 1 + which, 8, stride=8), :] = ref[which * 8 : (which + 1) * 8, :]
 
     drives, scales = [], []
     for t in range(2):
@@ -341,18 +343,21 @@
     whole = lax.all_to_all(
         prior.reshape(PER_MEM, CELL_ROWS, COLS), "dom", split_axis=0, concat_axis=0, tiled=True
     )
+    observed = jnp.concatenate([obs_value, obs_var]).reshape(2 * OBS_CHUNKS, COLS)
+    observed, whole = lax.optimization_barrier((observed, whole))
+    ring = [(i, (i + 1) % STRIPS) for i in range(STRIPS)]
+    behind_obs = lax.ppermute(observed, "dom", ring)
+    ahead_obs = lax.ppermute(observed, "dom", [(b, a) for a, b in ring])
     aux = pl.pallas_call(
         aux_kernel,
         compiler_params=PARAMS,
         name="aux",
         out_shape=jax.ShapeDtypeStruct((STRIPS * AUX, COLS), F32),
-        in_specs=[VMEM] * 8,
+        in_specs=[VMEM] * 6,
         out_specs=VMEM,
     )(
         *pieces,
         obs_cell.reshape(OBS_CHUNKS, COLS),
-        obs_value.reshape(OBS_CHUNKS, COLS),
-        obs_var.reshape(OBS_CHUNKS, COLS),
     )
     every = lax.all_to_all(
         aux.reshape(STRIPS, AUX, COLS), "dom", split_axis=0, concat_axis=0, tiled=True
@@ -373,7 +378,7 @@
         name="select",
         out_shape=(
             jax.ShapeDtypeStruct((PER_MEM * STRIPS * SEND, COLS), F32),
-            jax.ShapeDtypeStruct((META * 8, COLS), F32),
+            jax.ShapeDtypeStruct((META, COLS), F32),
         ),
         in_specs=[SMEM, VMEM, VMEM],
         out_specs=(VMEM, VMEM),
@@ -388,10 +393,14 @@
         compiler_params=PARAMS,
         name="update",
         out_shape=jax.ShapeDtypeStruct((PER_MEM, COLS_HERE, PER_MEM, COLS), F32),
-        in_specs=[SMEM, SMEM, VMEM, VMEM, VMEM],
+        in_specs=[SMEM, SMEM] + [VMEM] * 6,
         out_specs=VMEM,
-        scratch_shapes=[pltpu.VMEM((2, 256, 256), F32), pltpu.VMEM((2, 256, 256), F32)],
-    )(where, tile_count, own, near, tiles.reshape(PER_MEM * STRIPS * SEND, COLS))
+        scratch_shapes=[
+            pltpu.VMEM((2, 256, 256), F32),
+            pltpu.VMEM((2, 256, 256), F32),
+            pltpu.VMEM((META * 8, COLS), F32),
+        ],
+    )(where, tile_count, own, near, behind_obs, observed, ahead_obs, tiles.reshape(PER_MEM * STRIPS * SEND, COLS))
     back = lax.all_to_all(
         updated.reshape(PER_MEM, COLS_HERE * PER_MEM, COLS), "mem", split_axis=0, concat_axis=0, tiled=True
     )

time: 144 us -> 144 us (level)
  blocking collectives: 85.4 us -> 33 us
  waiting for transfers between devices: 9.14 us -> 44.9 us
  starting transfers between devices: 25.5 us -> 41.1 us
    all_to_all x1 -> x0, blocking collectives: 52.4 us -> none  [shards(): lax.all_to_all(sent.reshape(PER_MEM * STRIPS, SEND // 4, 4, COLS), ('mem'...]
    all_to_all x0 -> x1, waiting for transfers between devices: none -> 34.2 us  [shards(): lax.all_to_all(sent.reshape(PER_MEM * STRIPS, SEND // 4, 4, COLS), ('mem'...]
    all_to_all x0 -> x1, starting transfers between devices: none -> 11.6 us  [shards(): lax.all_to_all(sent.reshape(PER_MEM * STRIPS, SEND // 4, 4, COLS), ('mem'...]
    ppermute x0 -> x2, starting transfers between devices: none -> 4.95 us  [the longest x1 3.52 us: shards(): ahead_obs = lax.ppermute(observed, 'dom', [(b, a) for a, b in ring])]
    ppermute x0 -> x2, waiting for transfers between devices: none -> 1.91 us  [the longest x1 1.9 us: shards(): behind_obs = lax.ppermute(observed, 'dom', ring)]
  transfers between devices with their start and end apart: 7 -> 10, of which waited for: 4 -> 7; matrix products, arithmetic and copies ran while one was open for 0% -> 0% of each run, Pallas kernels for 6% -> 6%
where the time goes in v7:
time: 144 us
  waiting for transfers between devices  44.9 us (31%)
  starting transfers between devices  41.1 us (29%)
  blocking collectives  33 us (23%)
  Pallas kernels  23.6 us (16%)
    all_to_all x1, waiting for transfers between devices, shards(): lax.all_to_all(sent.reshape(PER_MEM * STRIPS, SEND // 4, 4, COLS), ('mem'...  34.2 us
    all_to_all x1, blocking collectives, shards(): lax.all_to_all(updated.reshape(PER_MEM, COLS_HERE * PER_MEM, COLS), 'mem'...  33 us
    all_to_all x1, starting transfers between devices, shards(): lax.all_to_all(sent.reshape(PER_MEM * STRIPS, SEND // 4, 4, COLS), ('mem'...  11.6 us
    ppermute x4, starting transfers between devices, shifted(): lax.ppermute(x, 'mem', [((i + by) % PER_MEM, i) for i in range(PER_MEM)])  8.84 us
    pallas_call x1, Pallas kernels, shards(): pl.pallas_call(forecast_kernel, compiler_params=PARAMS, cost_estimate=pl....  8.03 us
    all_to_all x1, starting transfers between devices, shards(): lax.all_to_all(prior.reshape(PER_MEM, CELL_ROWS, COLS), 'dom', split_axis...  7.72 us
    pallas_call x1, Pallas kernels, shards(): pl.pallas_call(select_kernel, compiler_params=PARAMS, name='select', out_...  7.48 us
    all_to_all x1, starting transfers between devices, shards(): lax.all_to_all(aux.reshape(STRIPS, AUX, COLS), 'dom', split_axis=0, conca...  6.94 us
  transfers between devices with their start and end apart: 10, of which 7 were waited for; matrix products, arithmetic and copies ran while one was open for 0% of the time, Pallas kernels for 6%

profile of v7, /device:TPU:1, one launch (start us, length us, event | category | flops | bytes accessed | tf_op | source)
XLA Modules:
  0.0 144.0 jit_solution(14698288550712551430)
XLA Ops:
  0.0 0.0 copy-start.8
  0.0 0.0 copy-start.1
  0.0 0.0 copy-start.6
  0.0 0.0 copy-start.7
  0.0 0.0 copy-start.2
  0.0 0.0 copy-start.3
  0.0 0.0 copy-start.4
  0.0 7.7 %all-to-all-start.1 = ((f32[16,128,128]{2,1,0:T(8,128)}), f32[16,128,128]{2,1,0:T(8,128)S(1)}, u32[]{:S(2)}, u32[]{:S(2)}) async-start(f32[16,128,128]{2,1,0:T(8,128)} %bitcast.20), calls=%async_computation.1 | async-start | bytes 2097152 | tf_op jit(solution)/shard_map/all_to_all | solution.py:343
  7.8 0.0 copy-done.8
  7.8 1.0 collective-permute-start
  8.8 0.8 collective-permute-done
  9.7 5.6 %collective-permute-start.1 = (s32[8,128]{1,0:T(8,128)S(1)}, s32[8,128]{1,0:T(8,128)S(1)}, u32[]{:S(2)}, u32[]{:S(2)}) collective-permute-start(s32[8,128]{1,0:T(8,128)S(1)} %pad_add_fusion.2.own_ref), channel_id=1, source_target_pairs={{32,0},{48,16},{64,32},{80,48},{96,64},{112,80},{128,96},{144,112}... | collective-permute-start | bytes 12296 | tf_op jit(solution)/shard_map/ppermute | solution.py:332
  15.2 0.0 collective-permute-start.2
  15.2 0.8 collective-permute-done.1.l1_ref
  16.0 3.2 %collective-permute-done.2.l2_ref = s32[8,128]{1,0:T(8,128)S(1)} collective-permute-done((s32[8,128]{1,0:T(8,128)S(1)}, s32[8,128]{1,0:T(8,128)S(1)}, u32[]{:S(2)}, u32[]{:S(2)}) %collective-permute-start.2) | collective-permute-done | bytes 4128 | tf_op jit(solution)/shard_map/ppermute | solution.py:332
  19.2 0.1 collective-permute-start.3
  19.3 3.2 %collective-permute-start.4 = (s32[16,128]{1,0:T(8,128)S(1)}, s32[16,128]{1,0:T(8,128)S(1)}, u32[]{:S(2)}, u32[]{:S(2)}) collective-permute-start(s32[16,128]{1,0:T(8,128)S(1)} %pad_add_fusion.1), channel_id=1, source_target_pairs={{160,0},{176,16},{192,32},{208,48},{224,64},{240,80},{0,96},{16,11... | collective-permute-start | bytes 24584 | tf_op jit(solution)/shard_map/ppermute | solution.py:332
  22.5 2.7 %collective-permute-done.4.l4_ref = s32[16,128]{1,0:T(8,128)S(1)} collective-permute-done((s32[16,128]{1,0:T(8,128)S(1)}, s32[16,128]{1,0:T(8,128)S(1)}, u32[]{:S(2)}, u32[]{:S(2)}) %collective-permute-start.4) | collective-permute-done | bytes 8224 | tf_op jit(solution)/shard_map/ppermute | solution.py:332
  25.2 0.0 collective-permute-done.3.l3_ref
  25.2 0.0 copy-done.1
  25.2 0.9 aux.1
  26.0 0.0 all-to-all-done.1
  26.0 6.9 %all-to-all-start = ((f32[16,72,128]{2,1,0:T(8,128)}), f32[16,72,128]{2,1,0:T(8,128)}, u32[]{:S(2)}, u32[]{:S(2)}) async-start(f32[16,72,128]{2,1,0:T(8,128)} %bitcast.3), calls=%async_computation | async-start | bytes 1179648 | tf_op jit(solution)/shard_map/all_to_all | solution.py:362
  33.0 0.1 pad_add_fusion.3.where_ref
  33.1 0.0 copy-done.6
  33.1 0.0 copy-done.7
  33.1 0.0 copy-done.2
  33.1 0.0 copy-done.3
  33.1 0.0 copy-done.4
  33.1 8.0 %forecast.1.q_ref = f32[4224,128]{1,0:T(8,128)S(1)} custom-call(f32[32]{0:T(128)S(1)} %copy-done.2, f32[32]{0:T(128)S(1)} %copy-done.3, f32[32]{0:T(128)S(1)} %copy-done.4, f32[2048,128]{1,0:T(8,128)S(1)} %bitcast.15), custom_call_target="tpu_custom_call" | custom-call | flops 30000000 | bytes 60000000 | tf_op jit(solution)/shard_map/forecast/pallas_call | solution.py:365
  41.1 1.3 all-to-all-done
  42.4 7.5 %select.1 = (f32[3072,128]{1,0:T(8,128)S(1)}, f32[24,128]{1,0:T(8,128)S(1)}) custom-call(s32[2]{0:T(128)S(1)} %pad_add_fusion.3.where_ref, f32[1152,128]{1,0:T(8,128)} %bitcast.4.aux_ref, f32[4224,128]{1,0:T(8,128)S(1)} %forecast.1.q_ref), custom_call_target="tpu_custom_call" | custom-call | tf_op jit(solution)/shard_map/select/pallas_call | solution.py:375
  49.9 0.0 copy-start
  49.9 1.2 copy-done
  51.1 0.0 copy-start.5
  51.1 11.6 %all-to-all-start.2 = ((f32[256,3,4,128]{3,2,1,0:T(4,128)}), f32[256,3,4,128]{3,2,1,0:T(4,128)S(1)}, u32[]{:S(2)}, u32[]{:S(2)}) async-start(f32[256,3,4,128]{3,2,1,0:T(4,128)} %bitcast.18), calls=%async_computation.2 | async-start | bytes 3145728 | tf_op jit(solution)/shard_map/all_to_all | solution.py:387
  62.7 1.4 collective-permute-start.5
  64.1 3.5 %collective-permute-start.6 = (f32[16,128]{1,0:T(8,128)S(1)}, f32[16,128]{1,0:T(8,128)S(1)}, u32[]{:S(2)}, u32[]{:S(2)}) collective-permute-start(f32[16,128]{1,0:T(8,128)S(1)} %pad_maximum_fusion.here_ref), channel_id=1, source_target_pairs={{1,0},{2,1},{3,2},{4,3},{5,4},{6,5},{7,6},{8,7},{9,8},{10,9},{11,1... | collective-permute-start | bytes 24584 | tf_op jit(solution)/shard_map/ppermute | solution.py:350
  67.6 1.9 %collective-permute-done.5.behind_ref = f32[16,128]{1,0:T(8,128)S(1)} collective-permute-done((f32[16,128]{1,0:T(8,128)S(1)}, f32[16,128]{1,0:T(8,128)S(1)}, u32[]{:S(2)}, u32[]{:S(2)}) %collective-permute-start.5) | collective-permute-done | bytes 8224 | tf_op jit(solution)/shard_map/ppermute | solution.py:349
  69.5 0.0 collective-permute-done.6.ahead_ref
  69.5 34.2 %all-to-all-done.2 = f32[256,3,4,128]{3,2,1,0:T(4,128)S(1)} async-done(((f32[256,3,4,128]{3,2,1,0:T(4,128)}), f32[256,3,4,128]{3,2,1,0:T(4,128)S(1)}, u32[]{:S(2)}, u32[]{:S(2)}) %all-to-all-start.2) | async-done | bytes 1572896 | tf_op jit(solution)/shard_map/all_to_all | solution.py:387
  103.8 0.0 copy-done.5
  103.8 6.1 %update.1 = f32[16,8,16,128]{3,2,1,0:T(8,128)S(1)} custom-call(s32[2]{0:T(128)S(1)} %pad_add_fusion.3.where_ref, s32[1,2]{1,0:T(1,128)S(1)} %copy-done.5, s32[4,128]{1,0:T(4,128)S(1)} %reshape.36.list_ref, f32[24,128]{1,0:T(8,128)S(1)} %get-tuple-element.10.cells_ref, f32[16,128]{1,0:T(8,128)S(1)} %collective-permute-done.5.behind_ref, ...), custom_call_target="tpu_custom_call" | custom-call | tf_op jit(solution)/shard_map/update/pallas_call | solution.py:391
  109.8 33.0 %all_to_all.20 = f32[16,128,128]{2,1,0:T(8,128)S(1)} all-to-all(f32[16,128,128]{2,1,0:T(8,128)S(1)} %bitcast.16), channel_id=1, replica_groups=mesh['mem'=16,'dom'=16] {'mem'}, dimensions={0} | all-to-all | bytes 2097152 | tf_op jit(solution)/shard_map/all_to_all | solution.py:404
  142.8 1.1 finish.1
  (5 shorter events, 0.0 us)
Async XLA Ops:
  0.0 7.8 %copy-start.8 = (s32[1,2,256]{2,1,0:T(2,128)S(1)}, s32[1,2,256]{2,1,0:T(2,128)}, u32[]{:S(2)}) copy-start(s32[1,2,256]{2,1,0:T(2,128)} %param.16) | copy-start | bytes 6148
  0.0 25.2 %copy-start.1 = (s32[1024]{0:T(1024)S(1)}, s32[1024]{0:T(1024)}, u32[]{:S(2)}) copy-start(s32[1024]{0:T(1024)} %param.13) | copy-start | bytes 12292
  0.0 33.1 %copy-start.6 = (f32[1024]{0:T(1024)S(1)}, f32[1024]{0:T(1024)}, u32[]{:S(2)}) copy-start(f32[1024]{0:T(1024)} %param.15) | copy-start | bytes 12292
  0.0 33.1 %copy-start.7 = (f32[1024]{0:T(1024)S(1)}, f32[1024]{0:T(1024)}, u32[]{:S(2)}) copy-start(f32[1024]{0:T(1024)} %param.14) | copy-start | bytes 12292
  0.0 33.1 %copy-start.2 = (f32[32]{0:T(128)S(1)}, f32[32]{0:T(128)}, u32[]{:S(2)}) copy-start(f32[32]{0:T(128)} %north_ref.1) | copy-start | bytes 388
  0.0 33.1 %copy-start.3 = (f32[32]{0:T(128)S(1)}, f32[32]{0:T(128)}, u32[]{:S(2)}) copy-start(f32[32]{0:T(128)} %east_ref.1) | copy-start | bytes 388
  0.0 33.1 %copy-start.4 = (f32[32]{0:T(128)S(1)}, f32[32]{0:T(128)}, u32[]{:S(2)}) copy-start(f32[32]{0:T(128)} %mix_ref.1) | copy-start | bytes 388
  0.0 26.0 %all-to-all-start.1 = ((f32[16,128,128]{2,1,0:T(8,128)}), f32[16,128,128]{2,1,0:T(8,128)S(1)}, u32[]{:S(2)}, u32[]{:S(2)}) async-start(f32[16,128,128]{2,1,0:T(8,128)} %bitcast.20), calls=%async_computation.1 | async-start | bytes 2097152 | tf_op jit(solution)/shard_map/all_to_all | solution.py:343
  7.8 1.9 %collective-permute-start = (s32[4,128]{1,0:T(4,128)S(1)}, s32[4,128]{1,0:T(4,128)S(1)}, u32[]{:S(2)}, u32[]{:S(2)}) collective-permute-start(s32[4,128]{1,0:T(4,128)S(1)} %reshape.36.list_ref), channel_id=1, source_target_pairs={{0,16},{16,0},{32,48},{48,32},{64,80},{80,64},{96,112},{112,96},{1... | collective-permute-start | bytes 6152 | tf_op jit(solution)/shard_map/ppermute | solution.py:335
  9.7 6.3 %collective-permute-start.1 = (s32[8,128]{1,0:T(8,128)S(1)}, s32[8,128]{1,0:T(8,128)S(1)}, u32[]{:S(2)}, u32[]{:S(2)}) collective-permute-start(s32[8,128]{1,0:T(8,128)S(1)} %pad_add_fusion.2.own_ref), channel_id=1, source_target_pairs={{32,0},{48,16},{64,32},{80,48},{96,64},{112,80},{128,96},{144,112}... | collective-permute-start | bytes 12296 | tf_op jit(solution)/shard_map/ppermute | solution.py:332
  15.2 4.0 %collective-permute-start.2 = (s32[8,128]{1,0:T(8,128)S(1)}, s32[8,128]{1,0:T(8,128)S(1)}, u32[]{:S(2)}, u32[]{:S(2)}) collective-permute-start(s32[8,128]{1,0:T(8,128)S(1)} %pad_add_fusion.2.own_ref), channel_id=1, source_target_pairs={{224,0},{240,16},{0,32},{16,48},{32,64},{48,80},{64,96},{80,112},{... | collective-permute-start | bytes 12296 | tf_op jit(solution)/shard_map/ppermute | solution.py:332
  19.2 6.0 %collective-permute-start.3 = (s32[24,128]{1,0:T(8,128)S(1)}, s32[24,128]{1,0:T(8,128)S(1)}, u32[]{:S(2)}, u32[]{:S(2)}) collective-permute-start(s32[24,128]{1,0:T(8,128)S(1)} %pad_add_fusion), channel_id=1, source_target_pairs={{96,0},{112,16},{128,32},{144,48},{160,64},{176,80},{192,96},{208,... | collective-permute-start | bytes 36872 | tf_op jit(solution)/shard_map/ppermute | solution.py:332
  19.3 5.8 %collective-permute-start.4 = (s32[16,128]{1,0:T(8,128)S(1)}, s32[16,128]{1,0:T(8,128)S(1)}, u32[]{:S(2)}, u32[]{:S(2)}) collective-permute-start(s32[16,128]{1,0:T(8,128)S(1)} %pad_add_fusion.1), channel_id=1, source_target_pairs={{160,0},{176,16},{192,32},{208,48},{224,64},{240,80},{0,96},{16,11... | collective-permute-start | bytes 24584 | tf_op jit(solution)/shard_map/ppermute | solution.py:332
  26.0 16.4 %all-to-all-start = ((f32[16,72,128]{2,1,0:T(8,128)}), f32[16,72,128]{2,1,0:T(8,128)}, u32[]{:S(2)}, u32[]{:S(2)}) async-start(f32[16,72,128]{2,1,0:T(8,128)} %bitcast.3), calls=%async_computation | async-start | bytes 1179648 | tf_op jit(solution)/shard_map/all_to_all | solution.py:362
  49.9 1.2 copy-start
  51.1 52.7 %copy-start.5 = (s32[1,2]{1,0:T(1,128)S(1)}, s32[1,2]{1,0:T(1,128)}, u32[]{:S(2)}) copy-start(s32[1,2]{1,0:T(1,128)} %count_ref.1) | copy-start | bytes 28
  51.1 52.7 %all-to-all-start.2 = ((f32[256,3,4,128]{3,2,1,0:T(4,128)}), f32[256,3,4,128]{3,2,1,0:T(4,128)S(1)}, u32[]{:S(2)}, u32[]{:S(2)}) async-start(f32[256,3,4,128]{3,2,1,0:T(4,128)} %bitcast.18), calls=%async_computation.2 | async-start | bytes 3145728 | tf_op jit(solution)/shard_map/all_to_all | solution.py:387
  62.7 6.9 %collective-permute-start.5 = (f32[16,128]{1,0:T(8,128)S(1)}, f32[16,128]{1,0:T(8,128)S(1)}, u32[]{:S(2)}, u32[]{:S(2)}) collective-permute-start(f32[16,128]{1,0:T(8,128)S(1)} %pad_maximum_fusion.here_ref), channel_id=1, source_target_pairs={{0,1},{1,2},{2,3},{3,4},{4,5},{5,6},{6,7},{7,8},{8,9},{9,10},{10,1... | collective-permute-start | bytes 24584 | tf_op jit(solution)/shard_map/ppermute | solution.py:349
  64.1 5.4 %collective-permute-start.6 = (f32[16,128]{1,0:T(8,128)S(1)}, f32[16,128]{1,0:T(8,128)S(1)}, u32[]{:S(2)}, u32[]{:S(2)}) collective-permute-start(f32[16,128]{1,0:T(8,128)S(1)} %pad_maximum_fusion.here_ref), channel_id=1, source_target_pairs={{1,0},{2,1},{3,2},{4,3},{5,4},{6,5},{7,6},{8,7},{9,8},{10,9},{11,1... | collective-permute-start | bytes 24584 | tf_op jit(solution)/shard_map/ppermute | solution.py:350

commit v8 on v7

--- a/solution.py
+++ b/solution.py
@@ -122,7 +122,7 @@
     lax.fori_loop(0, STRIPS, turn, 0, unroll=4)
 
 
-def select_kernel(where_ref, aux_ref, q_ref, out_ref, meta_ref, hx_ref):
+def select_kernel(where_ref, aux_ref, q_ref, behind_ref, ahead_ref, out_ref, meta_ref, hx_ref):
     sub = lax.broadcasted_iota(jnp.int32, (COLS, 2 * COLS), 0)
 
     def extract(s):
@@ -380,10 +380,10 @@
             jax.ShapeDtypeStruct((PER_MEM * STRIPS * SEND, COLS), F32),
             jax.ShapeDtypeStruct((META, COLS), F32),
         ),
-        in_specs=[SMEM, VMEM, VMEM],
+        in_specs=[SMEM, VMEM, VMEM] + [pl.BlockSpec(memory_space=pl.ANY)] * 2,
         out_specs=(VMEM, VMEM),
         scratch_shapes=[pltpu.VMEM((STRIPS * OBS_CHUNKS, COLS), F32)],
-    )(where, every.reshape(STRIPS * AUX, COLS), levels)
+    )(where, every.reshape(STRIPS * AUX, COLS), levels, behind_obs, ahead_obs)
     tiles = lax.all_to_all(
         sent.reshape(PER_MEM * STRIPS, SEND // 4, 4, COLS),
         ("mem", "dom"), split_axis=0, concat_axis=0, tiled=True,

time: 144 us -> 149 us (1.035)
  blocking collectives: 33 us -> 88.2 us
  waiting for transfers between devices: 44.9 us -> 6.55 us
  starting transfers between devices: 41.1 us -> 30.2 us
    all_to_all x0 -> x1, blocking collectives: none -> 55.2 us  [shards(): lax.all_to_all(sent.reshape(PER_MEM * STRIPS, SEND // 4, 4, COLS), ('mem'...]
    all_to_all x1 -> x0, waiting for transfers between devices: 34.2 us -> none  [shards(): lax.all_to_all(sent.reshape(PER_MEM * STRIPS, SEND // 4, 4, COLS), ('mem'...]
    all_to_all x1 -> x0, starting transfers between devices: 11.6 us -> none  [shards(): lax.all_to_all(sent.reshape(PER_MEM * STRIPS, SEND // 4, 4, COLS), ('mem'...]
    ppermute x1, waiting for transfers between devices: 1.9 us -> 0.01 us  [shards(): behind_obs = lax.ppermute(observed, 'dom', ring)]
  transfers between devices with their start and end apart: 10 -> 9, of which waited for: 7 -> 3; matrix products, arithmetic and copies ran while one was open for 0% -> 0% of each run, Pallas kernels for 6% -> 6%
where the time goes in v8:
time: 149 us
  blocking collectives  88.2 us (59%)
  starting transfers between devices  30.2 us (20%)
  Pallas kernels  23.6 us (16%)
  waiting for transfers between devices  6.55 us (4%)
    all_to_all x1, blocking collectives, shards(): lax.all_to_all(sent.reshape(PER_MEM * STRIPS, SEND // 4, 4, COLS), ('mem'...  55.2 us
    all_to_all x1, blocking collectives, shards(): lax.all_to_all(updated.reshape(PER_MEM, COLS_HERE * PER_MEM, COLS), 'mem'...  33 us
    ppermute x4, starting transfers between devices, shifted(): lax.ppermute(x, 'mem', [((i + by) % PER_MEM, i) for i in range(PER_MEM)])  10 us
    pallas_call x1, Pallas kernels, shards(): pl.pallas_call(forecast_kernel, compiler_params=PARAMS, cost_estimate=pl....  8.03 us
    all_to_all x1, starting transfers between devices, shards(): lax.all_to_all(prior.reshape(PER_MEM, CELL_ROWS, COLS), 'dom', split_axis...  7.72 us
    pallas_call x1, Pallas kernels, shards(): pl.pallas_call(select_kernel, compiler_params=PARAMS, name='select', out_...  7.48 us
    all_to_all x1, starting transfers between devices, shards(): lax.all_to_all(aux.reshape(STRIPS, AUX, COLS), 'dom', split_axis=0, conca...  6.69 us
    pallas_call x1, Pallas kernels, shards(): pl.pallas_call(update_kernel, compiler_params=PARAMS, name='update', out_...  6.06 us
  transfers between devices with their start and end apart: 9, of which 3 were waited for; matrix products, arithmetic and copies ran while one was open for 0% of the time, Pallas kernels for 6%

profile of v8, /device:TPU:1, one launch (start us, length us, event | category | flops | bytes accessed | tf_op | source)
XLA Modules:
  0.0 148.8 jit_solution(6358138817834968748)
XLA Ops:
  0.0 0.0 copy-start.7
  0.0 0.0 copy-start
  0.0 0.0 copy-start.5
  0.0 0.0 copy-start.6
  0.0 0.0 copy-start.1
  0.0 0.0 copy-start.2
  0.0 0.0 copy-start.3
  0.0 7.7 %all-to-all-start.1 = ((f32[16,128,128]{2,1,0:T(8,128)}), f32[16,128,128]{2,1,0:T(8,128)S(1)}, u32[]{:S(2)}, u32[]{:S(2)}) async-start(f32[16,128,128]{2,1,0:T(8,128)} %bitcast.20), calls=%async_computation.1 | async-start | bytes 2097152 | tf_op jit(solution)/shard_map/all_to_all | solution.py:343
  7.8 0.0 copy-done.7
  7.8 1.0 collective-permute-start
  8.8 0.8 collective-permute-done
  9.7 1.6 %collective-permute-start.2 = (s32[8,128]{1,0:T(8,128)S(1)}, s32[8,128]{1,0:T(8,128)S(1)}, u32[]{:S(2)}, u32[]{:S(2)}) collective-permute-start(s32[8,128]{1,0:T(8,128)S(1)} %pad_add_fusion.2.own_ref), channel_id=1, source_target_pairs={{224,0},{240,16},{0,32},{16,48},{32,64},{48,80},{64,96},{80,112},{... | collective-permute-start | bytes 12296 | tf_op jit(solution)/shard_map/ppermute | solution.py:332
  11.3 4.0 %collective-permute-start.1 = (s32[8,128]{1,0:T(8,128)S(1)}, s32[8,128]{1,0:T(8,128)S(1)}, u32[]{:S(2)}, u32[]{:S(2)}) collective-permute-start(s32[8,128]{1,0:T(8,128)S(1)} %pad_add_fusion.2.own_ref), channel_id=1, source_target_pairs={{32,0},{48,16},{64,32},{80,48},{96,64},{112,80},{128,96},{144,112}... | collective-permute-start | bytes 12296 | tf_op jit(solution)/shard_map/ppermute | solution.py:332
  15.3 1.2 collective-permute-done.2.l2_ref
  16.5 0.0 collective-permute-done.1.l1_ref
  16.5 3.1 %collective-permute-start.3 = (s32[24,128]{1,0:T(8,128)S(1)}, s32[24,128]{1,0:T(8,128)S(1)}, u32[]{:S(2)}, u32[]{:S(2)}) collective-permute-start(s32[24,128]{1,0:T(8,128)S(1)} %pad_add_fusion), channel_id=1, source_target_pairs={{96,0},{112,16},{128,32},{144,48},{160,64},{176,80},{192,96},{208,... | collective-permute-start | bytes 36872 | tf_op jit(solution)/shard_map/ppermute | solution.py:332
  19.6 1.3 collective-permute-start.4
  20.9 4.5 %collective-permute-done.4.l4_ref = s32[16,128]{1,0:T(8,128)S(1)} collective-permute-done((s32[16,128]{1,0:T(8,128)S(1)}, s32[16,128]{1,0:T(8,128)S(1)}, u32[]{:S(2)}, u32[]{:S(2)}) %collective-permute-start.4) | collective-permute-done | bytes 8224 | tf_op jit(solution)/shard_map/ppermute | solution.py:332
  25.4 0.0 collective-permute-done.3.l3_ref
  25.4 0.0 copy-done
  25.4 0.9 aux.1
  26.3 0.0 all-to-all-done.1
  26.3 6.7 %all-to-all-start = ((f32[16,72,128]{2,1,0:T(8,128)}), f32[16,72,128]{2,1,0:T(8,128)}, u32[]{:S(2)}, u32[]{:S(2)}) async-start(f32[16,72,128]{2,1,0:T(8,128)} %bitcast.3), calls=%async_computation | async-start | bytes 1179648 | tf_op jit(solution)/shard_map/all_to_all | solution.py:362
  33.0 0.0 copy-done.5
  33.0 0.0 copy-done.6
  33.0 4.7 %collective-permute-start.6 = (f32[16,128]{1,0:T(8,128)S(1)}, f32[16,128]{1,0:T(8,128)S(1)}, u32[]{:S(2)}, u32[]{:S(2)}) collective-permute-start(f32[16,128]{1,0:T(8,128)S(1)} %pad_maximum_fusion.here_ref), channel_id=1, source_target_pairs={{1,0},{2,1},{3,2},{4,3},{5,4},{6,5},{7,6},{8,7},{9,8},{10,9},{11,1... | collective-permute-start | bytes 24584 | tf_op jit(solution)/shard_map/ppermute | solution.py:350
  37.8 0.0 collective-permute-start.5
  37.8 0.1 pad_add_fusion.3.where_ref
  37.8 0.0 copy-done.1
  37.8 0.0 copy-done.2
  37.8 0.0 copy-done.3
  37.8 8.0 %forecast.1.q_ref = f32[4224,128]{1,0:T(8,128)S(1)} custom-call(f32[32]{0:T(128)S(1)} %copy-done.1, f32[32]{0:T(128)S(1)} %copy-done.2, f32[32]{0:T(128)S(1)} %copy-done.3, f32[2048,128]{1,0:T(8,128)S(1)} %bitcast.15), custom_call_target="tpu_custom_call" | custom-call | flops 30000000 | bytes 60000000 | tf_op jit(solution)/shard_map/forecast/pallas_call | solution.py:365
  45.9 0.0 all-to-all-done
  45.9 0.0 collective-permute-done.6.ahead_ref
  45.9 0.0 collective-permute-done.5.behind_ref
  45.9 7.5 %select.1 = (f32[3072,128]{1,0:T(8,128)S(1)}, f32[24,128]{1,0:T(8,128)S(1)}) custom-call(s32[2]{0:T(128)S(1)} %pad_add_fusion.3.where_ref, f32[1152,128]{1,0:T(8,128)} %bitcast.4.aux_ref, f32[4224,128]{1,0:T(8,128)S(1)} %forecast.1.q_ref, f32[16,128]{1,0:T(8,128)S(1)} %collective-permute-done.5.behind_ref, f32[16,128]{1,0:T(8,128)S(1)} %collective-permute-done.6.ahead_ref), custom_call_target="tpu_custom_call" | custom-call | tf_op jit(solution)/shard_map/select/pallas_call | solution.py:375
  53.4 0.0 copy-start.4
  53.4 55.2 %all_to_all.20 = f32[256,3,4,128]{3,2,1,0:T(4,128)S(1)} all-to-all(f32[256,3,4,128]{3,2,1,0:T(4,128)S(1)} %bitcast.18), channel_id=1, replica_groups=mesh['mem'=16,'dom'=16] {'mem','dom'}, dimensions={0} | all-to-all | bytes 3145728 | tf_op jit(solution)/shard_map/all_to_all | solution.py:387
  108.6 0.0 copy-done.4
  108.6 6.1 %update.1 = f32[16,8,16,128]{3,2,1,0:T(8,128)S(1)} custom-call(s32[2]{0:T(128)S(1)} %pad_add_fusion.3.where_ref, s32[1,2]{1,0:T(1,128)S(1)} %copy-done.4, s32[4,128]{1,0:T(4,128)S(1)} %reshape.36.list_ref, f32[24,128]{1,0:T(8,128)S(1)} %get-tuple-element.11.cells_ref, f32[16,128]{1,0:T(8,128)S(1)} %collective-permute-done.5.behind_ref, ...), custom_call_target="tpu_custom_call" | custom-call | tf_op jit(solution)/shard_map/update/pallas_call | solution.py:391
  114.6 33.0 %all_to_all.21 = f32[16,128,128]{2,1,0:T(8,128)S(1)} all-to-all(f32[16,128,128]{2,1,0:T(8,128)S(1)} %bitcast.16), channel_id=1, replica_groups=mesh['mem'=16,'dom'=16] {'mem'}, dimensions={0} | all-to-all | bytes 2097152 | tf_op jit(solution)/shard_map/all_to_all | solution.py:404
  147.7 1.1 finish.1
  (5 shorter events, 0.0 us)
Async XLA Ops:
  0.0 7.8 %copy-start.7 = (s32[1,2,256]{2,1,0:T(2,128)S(1)}, s32[1,2,256]{2,1,0:T(2,128)}, u32[]{:S(2)}) copy-start(s32[1,2,256]{2,1,0:T(2,128)} %param.16) | copy-start | bytes 6148
  0.0 25.4 %copy-start = (s32[1024]{0:T(1024)S(1)}, s32[1024]{0:T(1024)}, u32[]{:S(2)}) copy-start(s32[1024]{0:T(1024)} %param.13) | copy-start | bytes 12292
  0.0 33.0 %copy-start.5 = (f32[1024]{0:T(1024)S(1)}, f32[1024]{0:T(1024)}, u32[]{:S(2)}) copy-start(f32[1024]{0:T(1024)} %param.15) | copy-start | bytes 12292
  0.0 33.0 %copy-start.6 = (f32[1024]{0:T(1024)S(1)}, f32[1024]{0:T(1024)}, u32[]{:S(2)}) copy-start(f32[1024]{0:T(1024)} %param.14) | copy-start | bytes 12292
  0.0 37.8 %copy-start.1 = (f32[32]{0:T(128)S(1)}, f32[32]{0:T(128)}, u32[]{:S(2)}) copy-start(f32[32]{0:T(128)} %north_ref.1) | copy-start | bytes 388
  0.0 37.8 %copy-start.2 = (f32[32]{0:T(128)S(1)}, f32[32]{0:T(128)}, u32[]{:S(2)}) copy-start(f32[32]{0:T(128)} %east_ref.1) | copy-start | bytes 388
  0.0 37.8 %copy-start.3 = (f32[32]{0:T(128)S(1)}, f32[32]{0:T(128)}, u32[]{:S(2)}) copy-start(f32[32]{0:T(128)} %mix_ref.1) | copy-start | bytes 388
  0.0 26.3 %all-to-all-start.1 = ((f32[16,128,128]{2,1,0:T(8,128)}), f32[16,128,128]{2,1,0:T(8,128)S(1)}, u32[]{:S(2)}, u32[]{:S(2)}) async-start(f32[16,128,128]{2,1,0:T(8,128)} %bitcast.20), calls=%async_computation.1 | async-start | bytes 2097152 | tf_op jit(solution)/shard_map/all_to_all | solution.py:343
  7.8 1.9 %collective-permute-start = (s32[4,128]{1,0:T(4,128)S(1)}, s32[4,128]{1,0:T(4,128)S(1)}, u32[]{:S(2)}, u32[]{:S(2)}) collective-permute-start(s32[4,128]{1,0:T(4,128)S(1)} %reshape.36.list_ref), channel_id=1, source_target_pairs={{0,16},{16,0},{32,48},{48,32},{64,80},{80,64},{96,112},{112,96},{1... | collective-permute-start | bytes 6152 | tf_op jit(solution)/shard_map/ppermute | solution.py:335
  9.7 6.9 %collective-permute-start.2 = (s32[8,128]{1,0:T(8,128)S(1)}, s32[8,128]{1,0:T(8,128)S(1)}, u32[]{:S(2)}, u32[]{:S(2)}) collective-permute-start(s32[8,128]{1,0:T(8,128)S(1)} %pad_add_fusion.2.own_ref), channel_id=1, source_target_pairs={{224,0},{240,16},{0,32},{16,48},{32,64},{48,80},{64,96},{80,112},{... | collective-permute-start | bytes 12296 | tf_op jit(solution)/shard_map/ppermute | solution.py:332
  11.3 5.2 %collective-permute-start.1 = (s32[8,128]{1,0:T(8,128)S(1)}, s32[8,128]{1,0:T(8,128)S(1)}, u32[]{:S(2)}, u32[]{:S(2)}) collective-permute-start(s32[8,128]{1,0:T(8,128)S(1)} %pad_add_fusion.2.own_ref), channel_id=1, source_target_pairs={{32,0},{48,16},{64,32},{80,48},{96,64},{112,80},{128,96},{144,112}... | collective-permute-start | bytes 12296 | tf_op jit(solution)/shard_map/ppermute | solution.py:332
  16.5 8.9 %collective-permute-start.3 = (s32[24,128]{1,0:T(8,128)S(1)}, s32[24,128]{1,0:T(8,128)S(1)}, u32[]{:S(2)}, u32[]{:S(2)}) collective-permute-start(s32[24,128]{1,0:T(8,128)S(1)} %pad_add_fusion), channel_id=1, source_target_pairs={{96,0},{112,16},{128,32},{144,48},{160,64},{176,80},{192,96},{208,... | collective-permute-start | bytes 36872 | tf_op jit(solution)/shard_map/ppermute | solution.py:332
  19.6 5.8 %collective-permute-start.4 = (s32[16,128]{1,0:T(8,128)S(1)}, s32[16,128]{1,0:T(8,128)S(1)}, u32[]{:S(2)}, u32[]{:S(2)}) collective-permute-start(s32[16,128]{1,0:T(8,128)S(1)} %pad_add_fusion.1), channel_id=1, source_target_pairs={{160,0},{176,16},{192,32},{208,48},{224,64},{240,80},{0,96},{16,11... | collective-permute-start | bytes 24584 | tf_op jit(solution)/shard_map/ppermute | solution.py:332
  26.3 19.6 %all-to-all-start = ((f32[16,72,128]{2,1,0:T(8,128)}), f32[16,72,128]{2,1,0:T(8,128)}, u32[]{:S(2)}, u32[]{:S(2)}) async-start(f32[16,72,128]{2,1,0:T(8,128)} %bitcast.3), calls=%async_computation | async-start | bytes 1179648 | tf_op jit(solution)/shard_map/all_to_all | solution.py:362
  33.0 12.9 %collective-permute-start.6 = (f32[16,128]{1,0:T(8,128)S(1)}, f32[16,128]{1,0:T(8,128)S(1)}, u32[]{:S(2)}, u32[]{:S(2)}) collective-permute-start(f32[16,128]{1,0:T(8,128)S(1)} %pad_maximum_fusion.here_ref), channel_id=1, source_target_pairs={{1,0},{2,1},{3,2},{4,3},{5,4},{6,5},{7,6},{8,7},{9,8},{10,9},{11,1... | collective-permute-start | bytes 24584 | tf_op jit(solution)/shard_map/ppermute | solution.py:350
  37.8 8.1 %collective-permute-start.5 = (f32[16,128]{1,0:T(8,128)S(1)}, f32[16,128]{1,0:T(8,128)S(1)}, u32[]{:S(2)}, u32[]{:S(2)}) collective-permute-start(f32[16,128]{1,0:T(8,128)S(1)} %pad_maximum_fusion.here_ref), channel_id=1, source_target_pairs={{0,1},{1,2},{2,3},{3,4},{4,5},{5,6},{6,7},{7,8},{8,9},{9,10},{10,1... | collective-permute-start | bytes 24584 | tf_op jit(solution)/shard_map/ppermute | solution.py:349
  53.4 55.2 %copy-start.4 = (s32[1,2]{1,0:T(1,128)S(1)}, s32[1,2]{1,0:T(1,128)}, u32[]{:S(2)}) copy-start(s32[1,2]{1,0:T(1,128)} %count_ref.1) | copy-start | bytes 28
